TPU v7x, 32 devices: a whole 2x2x4 slice. The times are simulated.
32 devices in a mesh: groups: 2 (over y), space: 4 (over x, core), tm: 4 (over z).
Axes of the slice: x: 2, y: 2, z: 4, core: 2. Of those that a mesh axis runs over, the one named last changes fastest.
Arguments:
- start_states: float32 [8, 64, 32, 128], P(('groups', 'tm'), None, 'space'), parts along dimension 0, may hold values from -6 to 6
- velocity: float32 [3, 64, 32, 128], P(None, None, 'space'), may hold values from -0.15 to 0.15
- diffusivity: float32 [64, 32, 128], P(None, 'space'), may hold values from 0.01 to 0.09
Outputs:
- corrected_ends: float32 [8, 64, 32, 128], P(('groups', 'tm'), None, 'space'), parts along dimension 0
- jumps: float32 [8, 64, 32, 128], P(('groups', 'tm'), None, 'space'), parts along dimension 0
There are 2 independent parts, one for each index of `groups`. A program takes and returns all parts, laid end to end along the dimension named above; an argument that names none is the same for every part. Nothing has to cross between parts.
All inputs are finite; a program needn't handle non-finite values.
Results may differ from a plain program's by a relative error of at most 0.0001.
Values sent between devices are 32-bit elements; how exact they have to be, the bound alone decides.
No kernel may reach another device: no remote copies, remote signals or barrier semaphores. Data moves between devices by JAX's collectives and lax.ppermute only.
A program may use at most 128 MiB of HBM per device.

v0:
```python
import jax
import jax.numpy as jnp
from jax import lax
from jax.sharding import PartitionSpec as P

FINE_STEPS = 2


def extended(block, sides, width):
    for axis, dim in sides:
        count = lax.axis_size(axis)
        forward = [(i, i + 1) for i in range(count - 1)]
        backward = [(target, source) for source, target in forward]
        low = lax.ppermute(
            lax.slice_in_dim(block, block.shape[dim] - width, None, axis=dim), axis, forward
        )
        high = lax.ppermute(lax.slice_in_dim(block, 0, width, axis=dim), axis, backward)
        block = jnp.concatenate([low, block, high], axis=dim)
    return block


def from_behind(value, axis, steps):
    count = lax.axis_size(axis)
    initial, last = (max(0, -steps), min(count, count - steps))
    return lax.ppermute(value, axis, [(source, source + steps) for source in range(initial, last)])


def update(tracer, x_padded, coefficients):
    z_padded = jnp.pad(tracer, ((1, 1), (0, 0), (0, 0)))
    y_padded = jnp.pad(tracer, ((0, 0), (0, 0), (1, 1)))
    neighbours = (
        (z_padded[:-2], z_padded[2:]),
        (x_padded[:, :-2], x_padded[:, 2:]),
        (y_padded[:, :, :-2], y_padded[:, :, 2:]),
    )
    diffusion = coefficients[3]
    updated = tracer
    for axis_number in range(3):
        lower_side, upper_side = neighbours[axis_number]
        speed_field = coefficients[axis_number]
        updated = (
            updated
            - (
                jnp.maximum(speed_field, 0.0) * (tracer - lower_side)
                + jnp.minimum(speed_field, 0.0) * (upper_side - tracer)
            )
            + diffusion * (upper_side + lower_side - 2.0 * tracer)
        )
    return updated


def restrict(tracer):
    dims_now = tracer.shape
    reshaped = tracer.reshape(
        dims_now[:-3] + (dims_now[-3] // 4, 4, dims_now[-2] // 4, 4, dims_now[-1] // 4, 4)
    )
    return jnp.mean(reshaped, axis=(-5, -3, -1))


def prolong(coarse):
    depth, rows, cols = coarse.shape
    spread = jnp.broadcast_to(coarse[:, None, :, None, :, None], (depth, 4, rows, 4, cols, 4))
    return spread.reshape(depth * 4, rows * 4, cols * 4)


def local(start_states, velocity, diffusivity):
    initial = start_states[0]
    coefficients = jnp.concatenate([velocity, diffusivity[None]], 0)
    finished = initial
    for repeat in range(FINE_STEPS):
        bordered = extended(finished, (("space", 1),), 1)
        finished = update(finished, bordered, coefficients)
    earlier_end = from_behind(finished, "tm", 1)
    tm_index = lax.axis_index("tm")
    jump_field = jnp.where(tm_index == 0, jnp.zeros_like(initial), initial - earlier_end)
    coarse_scale = jnp.array([0.5, 0.5, 0.5, 0.125], jnp.float32)[:, None, None, None]
    coarse_coefficients = restrict(coefficients) * coarse_scale
    packed = jnp.stack([restrict(finished), restrict(initial)])

    def coarse_step(current):
        x_padded = extended(current, (("space", 1),), 1)
        return update(current, x_padded, coarse_coefficients)

    old_coarse = coarse_step(packed[1])
    defect = packed[0] - old_coarse
    everyone = lax.all_gather(jnp.stack([defect, packed[1]])[None], "tm", axis=0, tiled=True)

    def advance(position, carried):
        current, own_image = carried
        imaged = coarse_step(current)
        own_image = jnp.where(tm_index == position, imaged, own_image)
        return (imaged + everyone[position, 0], own_image)

    ignored, own_image = lax.fori_loop(
        0, lax.axis_size("tm"), advance, (everyone[0, 1], jnp.zeros_like(old_coarse))
    )
    change = own_image - old_coarse
    corrected = finished + prolong(change)
    return (corrected[None], jump_field[None])


def solution(mesh):
    in_specs = (
        P(("groups", "tm"), None, "space", None),
        P(None, None, "space", None),
        P(None, "space", None),
    )
    out_specs = (P(("groups", "tm"), None, "space", None), P(("groups", "tm"), None, "space", None))
    return jax.shard_map(local, mesh=mesh, in_specs=in_specs, out_specs=out_specs, check_vma=False)
```

profile of v0, /device:TPU:0, one launch (start us, length us, event | category | flops | bytes accessed | tf_op | source)
XLA Modules:
  0.0 174.7 jit_solution(6776922208838569203)
XLA Ops:
  0.6 1.7 fusion.57
  2.3 2.3 %collective-permute-start.2 = (f32[64,1,128]{2,1,0:T(1,128)}, f32[64,1,128]{2,1,0:T(1,128)S(1)}, u32[]{:S(2)}, u32[]{:S(2)}) collective-permute-start(f32[64,1,128]{2,1,0:T(1,128)} %get-tuple-element.216), channel_id=1, source_target_pairs={{0,4},{4,8},{8,12},{1,5},{5,9},{9,13},{2,6},{6,10},{10,14},{3,7},{... | collective-permute-start | bytes 98312 | tf_op jit(solution)/shard_map/ppermute | solution.py:14
  4.7 0.0 copy-start
  4.7 1.4 collective-permute-start.3
  6.1 10.8 %reshape_squeeze.3 = f32[16,4,2,4,32,4]{5,4,3,2,1,0:T(8,128)} reshape(f32[1,64,8,128]{3,2,1,0:T(8,128)} %param.6) | data formatting | bytes 524288 | tf_op jit(solution)/shard_map/reshape;squeeze | solution.py:54
  17.0 4.1 %reduce_sum.28 = f32[16,2,32]{2,1,0:T(2,128)S(1)} reduce(f32[16,4,2,4,32,4]{5,4,3,2,1,0:T(8,128)} %reshape_squeeze.3, f32[]{:T(128)} %constant.72.clone.1), dimensions={1,3,5}, to_apply=%region_1.2 | reduce | flops 64512 | bytes 266244 | tf_op jit(solution)/shard_map/reduce_sum | solution.py:57
  21.1 0.6 fusion.58
  21.7 5.1 %collective-permute-start.6 = (f32[16,1,32]{2,1,0:T(1,128)}, f32[16,1,32]{2,1,0:T(1,128)S(1)}, u32[]{:S(2)}, u32[]{:S(2)}) collective-permute-start(f32[16,1,32]{2,1,0:T(1,128)} %get-tuple-element.219), channel_id=1, source_target_pairs={{0,4},{4,8},{8,12},{1,5},{5,9},{9,13},{2,6},{6,10},{10,14},{3,7},{... | collective-permute-start | bytes 6152 | tf_op jit(solution)/shard_map/ppermute | solution.py:14
  26.8 1.3 collective-permute-start.7
  28.1 0.0 copy-done
  28.1 27.3 %concatenate.52 = f32[3,16,4,2,4,32,4]{6,5,4,3,2,1,0:T(8,128)} reshape(f32[3,64,8,128]{3,2,1,0:T(8,128)S(1)} %copy-done) | data formatting | bytes 1572864 | tf_op jit(solution)/shard_map/concatenate | solution.py:68
  55.5 0.0 copy-start.2
  55.5 16.5 %copy.18 = f32[3,16,4,2,4,32,4]{5,1,6,4,3,2,0:T(8,128)S(1)} copy(f32[3,16,4,2,4,32,4]{6,5,4,3,2,1,0:T(8,128)} %concatenate.52) | data formatting | bytes 1572864 | tf_op jit(solution)/shard_map/concatenate | solution.py:68
  72.0 0.0 copy-done.2
  72.0 10.0 %concatenate.53 = f32[1,16,4,2,4,32,4]{6,5,4,3,2,1,0:T(8,128)} reshape(f32[64,8,128]{2,1,0:T(8,128)S(1)} %copy-done.2) | data formatting | bytes 524288 | tf_op jit(solution)/shard_map/concatenate | solution.py:68
  82.0 0.0 copy-start.1
  82.0 6.9 %copy.19 = f32[1,16,4,2,4,32,4]{5,1,6,4,3,2,0:T(8,128)} copy(f32[1,16,4,2,4,32,4]{6,5,4,3,2,1,0:T(8,128)} %concatenate.53) | data formatting | bytes 524288 | tf_op jit(solution)/shard_map/concatenate | solution.py:68
  88.9 1.7 maximum_reduce_fusion
  90.6 0.0 collective-permute-done.2
  90.6 0.0 collective-permute-done.3
  90.6 0.0 copy-done.1
  90.7 1.6 fusion.27
  92.3 4.3 %collective-permute-start.4 = (f32[64,1,128]{2,1,0:T(1,128)S(1)}, f32[64,1,128]{2,1,0:T(1,128)S(1)}, u32[]{:S(2)}, u32[]{:S(2)}) collective-permute-start(f32[64,1,128]{2,1,0:T(1,128)S(1)} %get-tuple-element.214), channel_id=1, source_target_pairs={{0,4},{4,8},{8,12},{1,5},{5,9},{9,13},{2,6},{6,10},{10,14},{3,7},{... | collective-permute-start | bytes 98312 | tf_op jit(solution)/shard_map/ppermute | solution.py:14
  96.6 1.3 collective-permute-start.5
  97.9 0.8 copy_multiply_fusion
  98.7 0.0 collective-permute-done.4
  98.7 2.3 %collective-permute-done.5 = f32[64,1,128]{2,1,0:T(1,128)S(1)} collective-permute-done((f32[64,1,128]{2,1,0:T(1,128)S(1)}, f32[64,1,128]{2,1,0:T(1,128)S(1)}, u32[]{:S(2)}, u32[]{:S(2)}) %collective-permute-start.5) | collective-permute-done | bytes 32800 | tf_op jit(solution)/shard_map/ppermute | solution.py:17
  100.9 1.6 fusion.15
  102.6 10.0 %reshape.61 = f32[16,4,2,4,32,4]{5,4,3,2,1,0:T(8,128)} reshape(f32[64,8,128]{2,1,0:T(8,128)S(1)} %fusion.15) | data formatting | bytes 524288 | tf_op jit(solution)/shard_map/reshape | solution.py:54
  112.6 3.5 %collective-permute-start.8 = (f32[64,8,128]{2,1,0:T(8,128)S(1)}, f32[64,8,128]{2,1,0:T(8,128)S(1)}, u32[]{:S(2)}, u32[]{:S(2)}) collective-permute-start(f32[64,8,128]{2,1,0:T(8,128)S(1)} %fusion.15), channel_id=1, source_target_pairs={{0,1},{1,2},{2,3},{4,5},{5,6},{6,7},{8,9},{9,10},{10,11},{12,13},{... | collective-permute-start | bytes 786440 | tf_op jit(solution)/shard_map/ppermute | solution.py:25
  116.1 4.1 %reduce_sum.27 = f32[16,2,32]{2,1,0:T(2,128)S(1)} reduce(f32[16,4,2,4,32,4]{5,4,3,2,1,0:T(8,128)} %reshape.61, f32[]{:T(128)} %constant.72.clone.1), dimensions={1,3,5}, to_apply=%region_0.1 | reduce | flops 64512 | bytes 266244 | tf_op jit(solution)/shard_map/reduce_sum | solution.py:57
  120.2 0.0 collective-permute-done.6
  120.2 0.0 collective-permute-done.7
  120.2 0.1 subtract_bitcast_fusion
  120.4 13.8 %all-gather = f32[8,16,2,32]{3,1,2,0:T(8,128)S(1)} all-gather(f32[2,16,2,32]{3,1,2,0:T(8,128)S(1)} %copy.21), channel_id=2, replica_groups=mesh['groups'=2,'space'=4,'tm'=4] {'tm'}, dimensions={0}, use_global_device_ids=true | all-gather | bytes 40960 | tf_op jit(solution)/shard_map/all_gather | solution.py:86
  134.1 0.1 copy.22
  134.2 26.5 %while.18 = (s32[]{:T(128)}, f32[16,2,32]{2,1,0:T(2,128)S(1)}, f32[16,2,32]{2,1,0:T(2,128)S(1)}, f32[4,16,2,32]{3,2,1,0:T(2,128)S(1)}, f32[4,2,16,2,32]{4,3,2,1,...) while((s32[]{:T(128)}, f32[16,2,32]{2,1,0:T(2,128)S(1)}, f32[16,2,32]{2,1,0:T(2,128)S(1)}, ...), condition=%wide.region_4.5_spmd.clone, body=%wide.region_3.4_spmd.clone.sunk | while | flops 43012 | bytes 73925 | solution.py:94
  134.3 1.3 collective-permute-start
  135.6 3.0 %collective-permute-start.1 = (f32[16,1,32]{2,1,0:T(1,128)S(1)}, f32[16,1,32]{2,1,0:T(1,128)S(1)}, u32[]{:S(2)}, u32[]{:S(2)}) collective-permute-start(f32[16,1,32]{2,1,0:T(1,128)S(1)} %get-tuple-element.263), channel_id=1, source_target_pairs={{0,4},{4,8},{8,12},{1,5},{5,9},{9,13},{2,6},{6,10},{10,14},{3,7},{... | collective-permute-start | bytes 6152 | tf_op jit(solution)/shard_map/while/body/eval_jaxpr/ppermute | solution.py:14
  138.6 0.0 collective-permute-done
  138.6 0.8 collective-permute-done.1
  139.4 0.1 select_select_fusion.2
  139.6 1.3 collective-permute-start
  140.9 4.6 %collective-permute-start.1 = (f32[16,1,32]{2,1,0:T(1,128)S(1)}, f32[16,1,32]{2,1,0:T(1,128)S(1)}, u32[]{:S(2)}, u32[]{:S(2)}) collective-permute-start(f32[16,1,32]{2,1,0:T(1,128)S(1)} %get-tuple-element.263), channel_id=1, source_target_pairs={{0,4},{4,8},{8,12},{1,5},{5,9},{9,13},{2,6},{6,10},{10,14},{3,7},{... | collective-permute-start | bytes 6152 | tf_op jit(solution)/shard_map/while/body/eval_jaxpr/ppermute | solution.py:14
  145.5 0.0 collective-permute-done
  145.5 0.8 collective-permute-done.1
  146.3 0.1 select_select_fusion.2
  146.5 1.3 collective-permute-start
  147.8 4.8 %collective-permute-start.1 = (f32[16,1,32]{2,1,0:T(1,128)S(1)}, f32[16,1,32]{2,1,0:T(1,128)S(1)}, u32[]{:S(2)}, u32[]{:S(2)}) collective-permute-start(f32[16,1,32]{2,1,0:T(1,128)S(1)} %get-tuple-element.263), channel_id=1, source_target_pairs={{0,4},{4,8},{8,12},{1,5},{5,9},{9,13},{2,6},{6,10},{10,14},{3,7},{... | collective-permute-start | bytes 6152 | tf_op jit(solution)/shard_map/while/body/eval_jaxpr/ppermute | solution.py:14
  152.6 0.0 collective-permute-done
  152.6 0.8 collective-permute-done.1
  153.4 0.1 select_select_fusion.2
  153.6 1.3 collective-permute-start
  154.9 4.8 %collective-permute-start.1 = (f32[16,1,32]{2,1,0:T(1,128)S(1)}, f32[16,1,32]{2,1,0:T(1,128)S(1)}, u32[]{:S(2)}, u32[]{:S(2)}) collective-permute-start(f32[16,1,32]{2,1,0:T(1,128)S(1)} %get-tuple-element.263), channel_id=1, source_target_pairs={{0,4},{4,8},{8,12},{1,5},{5,9},{9,13},{2,6},{6,10},{10,14},{3,7},{... | collective-permute-start | bytes 6152 | tf_op jit(solution)/shard_map/while/body/eval_jaxpr/ppermute | solution.py:14
  159.7 0.0 collective-permute-done
  159.7 0.8 collective-permute-done.1
  160.5 0.1 select_select_fusion.2
  160.7 4.4 %broadcast_in_dim.18 = f32[16,4,2,4,32,4]{5,4,3,2,1,0:T(8,128)} broadcast(f32[16,2,32]{2,1,0:T(2,128)S(1)} %sub.274), dimensions={0,2,4} | broadcast | bytes 266240 | tf_op jit(solution)/shard_map/broadcast_in_dim | solution.py:62
  165.1 8.2 %reshape.62 = f32[64,8,128]{2,1,0:T(8,128)S(1)} reshape(f32[16,4,2,4,32,4]{5,4,3,2,1,0:T(8,128)} %broadcast_in_dim.18) | data formatting | bytes 524288 | tf_op jit(solution)/shard_map/reshape | solution.py:63
  173.2 0.7 add_bitcast_fusion
  174.0 0.0 collective-permute-done.8
  174.0 0.7 select_bitcast_fusion
  (15 shorter events, 0.2 us)
Async XLA Ops:
  2.3 88.3 %collective-permute-start.2 = (f32[64,1,128]{2,1,0:T(1,128)}, f32[64,1,128]{2,1,0:T(1,128)S(1)}, u32[]{:S(2)}, u32[]{:S(2)}) collective-permute-start(f32[64,1,128]{2,1,0:T(1,128)} %get-tuple-element.216), channel_id=1, source_target_pairs={{0,4},{4,8},{8,12},{1,5},{5,9},{9,13},{2,6},{6,10},{10,14},{3,7},{... | collective-permute-start | bytes 98312 | tf_op jit(solution)/shard_map/ppermute | solution.py:14
  4.7 23.4 %copy-start = (f32[3,64,8,128]{3,2,1,0:T(8,128)S(1)}, f32[3,64,8,128]{3,2,1,0:T(8,128)}, u32[]{:S(2)}) copy-start(f32[3,64,8,128]{3,2,1,0:T(8,128)} %param.7) | copy-start | bytes 2359300
  4.7 86.0 %collective-permute-start.3 = (f32[64,1,128]{2,1,0:T(1,128)S(1)}, f32[64,1,128]{2,1,0:T(1,128)S(1)}, u32[]{:S(2)}, u32[]{:S(2)}) collective-permute-start(f32[64,1,128]{2,1,0:T(1,128)S(1)} %get-tuple-element.217), channel_id=1, source_target_pairs={{4,0},{8,4},{12,8},{5,1},{9,5},{13,9},{6,2},{10,6},{14,10},{7,3},{... | collective-permute-start | bytes 98312 | tf_op jit(solution)/shard_map/ppermute | solution.py:17
  21.7 98.5 %collective-permute-start.6 = (f32[16,1,32]{2,1,0:T(1,128)}, f32[16,1,32]{2,1,0:T(1,128)S(1)}, u32[]{:S(2)}, u32[]{:S(2)}) collective-permute-start(f32[16,1,32]{2,1,0:T(1,128)} %get-tuple-element.219), channel_id=1, source_target_pairs={{0,4},{4,8},{8,12},{1,5},{5,9},{9,13},{2,6},{6,10},{10,14},{3,7},{... | collective-permute-start | bytes 6152 | tf_op jit(solution)/shard_map/ppermute | solution.py:14
  26.8 93.4 %collective-permute-start.7 = (f32[16,1,32]{2,1,0:T(1,128)}, f32[16,1,32]{2,1,0:T(1,128)S(1)}, u32[]{:S(2)}, u32[]{:S(2)}) collective-permute-start(f32[16,1,32]{2,1,0:T(1,128)} %get-tuple-element.220), channel_id=1, source_target_pairs={{4,0},{8,4},{12,8},{5,1},{9,5},{13,9},{6,2},{10,6},{14,10},{7,3},{... | collective-permute-start | bytes 6152 | tf_op jit(solution)/shard_map/ppermute | solution.py:17
  55.5 16.5 %copy-start.2 = (f32[64,8,128]{2,1,0:T(8,128)S(1)}, f32[64,8,128]{2,1,0:T(8,128)}, u32[]{:S(2)}) copy-start(f32[64,8,128]{2,1,0:T(8,128)} %param.8) | copy-start | bytes 786436
  82.0 8.6 %copy-start.1 = (f32[1,64,8,128]{3,2,1,0:T(8,128)S(1)}, f32[1,64,8,128]{3,2,1,0:T(8,128)}, u32[]{:S(2)}) copy-start(f32[1,64,8,128]{3,2,1,0:T(8,128)} %param.6) | copy-start | bytes 786436
  92.3 6.4 %collective-permute-start.4 = (f32[64,1,128]{2,1,0:T(1,128)S(1)}, f32[64,1,128]{2,1,0:T(1,128)S(1)}, u32[]{:S(2)}, u32[]{:S(2)}) collective-permute-start(f32[64,1,128]{2,1,0:T(1,128)S(1)} %get-tuple-element.214), channel_id=1, source_target_pairs={{0,4},{4,8},{8,12},{1,5},{5,9},{9,13},{2,6},{6,10},{10,14},{3,7},{... | collective-permute-start | bytes 98312 | tf_op jit(solution)/shard_map/ppermute | solution.py:14
  96.6 4.3 %collective-permute-start.5 = (f32[64,1,128]{2,1,0:T(1,128)S(1)}, f32[64,1,128]{2,1,0:T(1,128)S(1)}, u32[]{:S(2)}, u32[]{:S(2)}) collective-permute-start(f32[64,1,128]{2,1,0:T(1,128)S(1)} %get-tuple-element.215), channel_id=1, source_target_pairs={{4,0},{8,4},{12,8},{5,1},{9,5},{13,9},{6,2},{10,6},{14,10},{7,3},{... | collective-permute-start | bytes 98312 | tf_op jit(solution)/shard_map/ppermute | solution.py:17
  112.6 61.4 %collective-permute-start.8 = (f32[64,8,128]{2,1,0:T(8,128)S(1)}, f32[64,8,128]{2,1,0:T(8,128)S(1)}, u32[]{:S(2)}, u32[]{:S(2)}) collective-permute-start(f32[64,8,128]{2,1,0:T(8,128)S(1)} %fusion.15), channel_id=1, source_target_pairs={{0,1},{1,2},{2,3},{4,5},{5,6},{6,7},{8,9},{9,10},{10,11},{12,13},{... | collective-permute-start | bytes 786440 | tf_op jit(solution)/shard_map/ppermute | solution.py:25
  134.3 4.4 %collective-permute-start = (f32[16,1,32]{2,1,0:T(1,128)S(1)}, f32[16,1,32]{2,1,0:T(1,128)S(1)}, u32[]{:S(2)}, u32[]{:S(2)}) collective-permute-start(f32[16,1,32]{2,1,0:T(1,128)S(1)} %get-tuple-element.262), channel_id=1, source_target_pairs={{4,0},{8,4},{12,8},{5,1},{9,5},{13,9},{6,2},{10,6},{14,10},{7,3},{... | collective-permute-start | bytes 6152 | tf_op jit(solution)/shard_map/while/body/eval_jaxpr/ppermute | solution.py:17
  135.6 3.8 %collective-permute-start.1 = (f32[16,1,32]{2,1,0:T(1,128)S(1)}, f32[16,1,32]{2,1,0:T(1,128)S(1)}, u32[]{:S(2)}, u32[]{:S(2)}) collective-permute-start(f32[16,1,32]{2,1,0:T(1,128)S(1)} %get-tuple-element.263), channel_id=1, source_target_pairs={{0,4},{4,8},{8,12},{1,5},{5,9},{9,13},{2,6},{6,10},{10,14},{3,7},{... | collective-permute-start | bytes 6152 | tf_op jit(solution)/shard_map/while/body/eval_jaxpr/ppermute | solution.py:14
  139.6 5.9 %collective-permute-start = (f32[16,1,32]{2,1,0:T(1,128)S(1)}, f32[16,1,32]{2,1,0:T(1,128)S(1)}, u32[]{:S(2)}, u32[]{:S(2)}) collective-permute-start(f32[16,1,32]{2,1,0:T(1,128)S(1)} %get-tuple-element.262), channel_id=1, source_target_pairs={{4,0},{8,4},{12,8},{5,1},{9,5},{13,9},{6,2},{10,6},{14,10},{7,3},{... | collective-permute-start | bytes 6152 | tf_op jit(solution)/shard_map/while/body/eval_jaxpr/ppermute | solution.py:17
  140.9 5.4 %collective-permute-start.1 = (f32[16,1,32]{2,1,0:T(1,128)S(1)}, f32[16,1,32]{2,1,0:T(1,128)S(1)}, u32[]{:S(2)}, u32[]{:S(2)}) collective-permute-start(f32[16,1,32]{2,1,0:T(1,128)S(1)} %get-tuple-element.263), channel_id=1, source_target_pairs={{0,4},{4,8},{8,12},{1,5},{5,9},{9,13},{2,6},{6,10},{10,14},{3,7},{... | collective-permute-start | bytes 6152 | tf_op jit(solution)/shard_map/while/body/eval_jaxpr/ppermute | solution.py:14
  146.5 6.1 %collective-permute-start = (f32[16,1,32]{2,1,0:T(1,128)S(1)}, f32[16,1,32]{2,1,0:T(1,128)S(1)}, u32[]{:S(2)}, u32[]{:S(2)}) collective-permute-start(f32[16,1,32]{2,1,0:T(1,128)S(1)} %get-tuple-element.262), channel_id=1, source_target_pairs={{4,0},{8,4},{12,8},{5,1},{9,5},{13,9},{6,2},{10,6},{14,10},{7,3},{... | collective-permute-start | bytes 6152 | tf_op jit(solution)/shard_map/while/body/eval_jaxpr/ppermute | solution.py:17
  147.8 5.6 %collective-permute-start.1 = (f32[16,1,32]{2,1,0:T(1,128)S(1)}, f32[16,1,32]{2,1,0:T(1,128)S(1)}, u32[]{:S(2)}, u32[]{:S(2)}) collective-permute-start(f32[16,1,32]{2,1,0:T(1,128)S(1)} %get-tuple-element.263), channel_id=1, source_target_pairs={{0,4},{4,8},{8,12},{1,5},{5,9},{9,13},{2,6},{6,10},{10,14},{3,7},{... | collective-permute-start | bytes 6152 | tf_op jit(solution)/shard_map/while/body/eval_jaxpr/ppermute | solution.py:14
  153.6 6.1 %collective-permute-start = (f32[16,1,32]{2,1,0:T(1,128)S(1)}, f32[16,1,32]{2,1,0:T(1,128)S(1)}, u32[]{:S(2)}, u32[]{:S(2)}) collective-permute-start(f32[16,1,32]{2,1,0:T(1,128)S(1)} %get-tuple-element.262), channel_id=1, source_target_pairs={{4,0},{8,4},{12,8},{5,1},{9,5},{13,9},{6,2},{10,6},{14,10},{7,3},{... | collective-permute-start | bytes 6152 | tf_op jit(solution)/shard_map/while/body/eval_jaxpr/ppermute | solution.py:17
  154.9 5.6 %collective-permute-start.1 = (f32[16,1,32]{2,1,0:T(1,128)S(1)}, f32[16,1,32]{2,1,0:T(1,128)S(1)}, u32[]{:S(2)}, u32[]{:S(2)}) collective-permute-start(f32[16,1,32]{2,1,0:T(1,128)S(1)} %get-tuple-element.263), channel_id=1, source_target_pairs={{0,4},{4,8},{8,12},{1,5},{5,9},{9,13},{2,6},{6,10},{10,14},{3,7},{... | collective-permute-start | bytes 6152 | tf_op jit(solution)/shard_map/while/body/eval_jaxpr/ppermute | solution.py:14
where the time goes:
time: 177 us; the launch traced here: 175 us
  local copies, waits for them, and re-layouts  96.6 us (55%)
  starting transfers between devices  41.6 us (24%)
  other arithmetic  16.1 us (9%)
  blocking collectives  13.8 us (8%)
  waiting for transfers between devices  5.44 us (3%)
    concatenate x4, local copies, waits for them, and re-layouts, local(): coefficients = jnp.concatenate([velocity, diffusivity[None]], 0)  60.8 us
    ppermute x7, starting transfers between devices, extended(): lax.ppermute(lax.slice_in_dim(block, block.shape[dim] - width, None, axis...  28.9 us
    all_gather x1, blocking collectives, local(): lax.all_gather(jnp.stack([defect, packed[1]])[None], 'tm', axis=0, tiled=...  13.8 us
    another operation x1, local copies, waits for them, and re-layouts, restrict(): tracer.reshape(dims_now[:-3] + (dims_now[-3] // 4, 4, dims_now[-2] // 4,...  10.8 us
    reshape x1, local copies, waits for them, and re-layouts, restrict(): tracer.reshape(dims_now[:-3] + (dims_now[-3] // 4, 4, dims_now[-2] // 4,...  10 us
    reduce_sum x3, other arithmetic, restrict(): return jnp.mean(reshaped, axis=(-5, -3, -1))  9.89 us
    ppermute x7, starting transfers between devices, extended(): lax.ppermute(lax.slice_in_dim(block, 0, width, axis=dim), axis, backward)  9.18 us
    reshape x1, local copies, waits for them, and re-layouts, prolong(): return spread.reshape(depth * 4, rows * 4, cols * 4)  8.16 us
  transfers between devices with their start and end apart: 15, of which 5 were waited for; matrix products, arithmetic and copies ran while one was open for 63% of the time, Pallas kernels for 0%

commit v1 on v0

v1 whole, which is shorter than its diff:
```python
import jax
import jax.numpy as jnp
from jax import lax
from jax.experimental import pallas as pl
from jax.experimental.pallas import tpu as pltpu
from jax.sharding import PartitionSpec as P

NZ, ROWS, LANES = 64, 8, 128
FLAT = NZ * ROWS
CHUNK = 8
BITS = ((1, 1), (1, 2), (0, 1), (0, 2))

f32 = jnp.float32


def shifted(x, by, axis):
    return pltpu.roll(x, (-by) % x.shape[axis], axis)


def iotas(shape):
    n = len(shape)
    return (
        lax.broadcasted_iota(jnp.int32, shape, n - 2),
        lax.broadcasted_iota(jnp.int32, shape, n - 1),
    )


def restrict_tile(planes):
    sub, lane = iotas((ROWS, LANES))
    for axis, dist in BITS:
        low = ((lane if axis else sub) // dist) % 2 == 0
        planes = [
            jnp.where(low, a + shifted(a, dist, axis), b + shifted(b, -dist, axis))
            for a, b in zip(planes[0::2], planes[1::2])
        ]
    return planes[0]


def prolong_tile(tile):
    sub, lane = iotas((ROWS, LANES))
    planes = [tile]
    for axis, dist in reversed(BITS):
        low = ((lane if axis else sub) // dist) % 2 == 0
        grown = []
        for a in planes:
            grown.append(jnp.where(low, a, shifted(a, -dist, axis)))
            grown.append(jnp.where(low, shifted(a, dist, axis), a))
        planes = grown
    return planes


def plane_sums(ref):
    def one(c):
        at = c * 4 * ROWS
        return (ref[at : at + ROWS] + ref[at + ROWS : at + 2 * ROWS]) + (
            ref[at + 2 * ROWS : at + 3 * ROWS] + ref[at + 3 * ROWS : at + 4 * ROWS]
        )

    return [one(c) for c in range(NZ // 4)]


def weights(cz, cx, cy, diff):
    out = []
    for c in (cz, cx, cy):
        out.append(diff + jnp.maximum(c, 0.0))
        out.append(diff - jnp.minimum(c, 0.0))
    centre = 1.0 - ((out[0] + out[1]) + (out[2] + out[3]) + (out[4] + out[5]))
    return out + [centre]


def row(ref, at):
    return ref[pl.ds(at, NZ, stride=ROWS), :]


def local_kernel(v_ref, vel_ref, d_ref, q_ref, lo_ref, hi_ref, coarse_ref, keep_ref, rstart_ref, p_ref, pv_ref):
    zero = jnp.zeros((ROWS, LANES), f32)
    for ref in (p_ref, pv_ref):
        ref[0:ROWS] = zero
        ref[FLAT + ROWS : FLAT + 2 * ROWS] = zero
    pv_ref[ROWS : FLAT + ROWS] = v_ref[...]
    shape = (CHUNK, ROWS, LANES)
    sub, lane = iotas(shape)
    size = CHUNK * ROWS

    def step(src, dst, dst_off):
        def body(c, carry):
            at = pl.multiple_of(c * size, size)
            load = lambda ref, off: ref[pl.ds(at + off, size), :].reshape(shape)
            w = weights(
                load(vel_ref, 0), load(vel_ref, FLAT), load(vel_ref, 2 * FLAT), load(d_ref, 0)
            )
            v = load(src, ROWS)
            total = w[6] * v + w[0] * load(src, 0) + w[1] * load(src, 2 * ROWS)
            total += jnp.where(sub == 0, 0.0, w[2]) * shifted(v, -1, 1)
            total += jnp.where(sub == ROWS - 1, 0.0, w[3]) * shifted(v, 1, 1)
            total += jnp.where(lane == 0, 0.0, w[4]) * shifted(v, -1, 2)
            total += jnp.where(lane == LANES - 1, 0.0, w[5]) * shifted(v, 1, 2)
            dst[pl.ds(at + dst_off, size), :] = total.reshape(size, LANES)
            return carry

        lax.fori_loop(0, NZ // CHUNK, body, 0)

    step(pv_ref, p_ref, ROWS)
    diff0, diff7 = row(d_ref, 0), row(d_ref, ROWS - 1)
    cx0, cx7 = row(vel_ref, FLAT), row(vel_ref, FLAT + ROWS - 1)
    k0 = diff0 + jnp.maximum(cx0, 0.0)
    k7 = diff7 - jnp.minimum(cx7, 0.0)
    lo_ref[0:NZ] = row(v_ref, 0)
    lo_ref[NZ : 2 * NZ] = row(p_ref, ROWS)
    lo_ref[2 * NZ : 3 * NZ] = k0
    hi_ref[0:NZ] = row(v_ref, ROWS - 1)
    hi_ref[NZ : 2 * NZ] = row(p_ref, 2 * ROWS - 1)
    hi_ref[2 * NZ : 3 * NZ] = k7
    for side, at in enumerate((0, ROWS - 1)):
        w = weights(*(row(vel_ref, d * FLAT + at) for d in range(3)), row(d_ref, at))
        for j, value in enumerate((w[0], w[1], w[4], w[5], w[6])):
            keep_ref[(side * 6 + j) * NZ : (side * 6 + j + 1) * NZ] = value
    keep_ref[5 * NZ : 6 * NZ] = row(d_ref, 1) + jnp.maximum(row(vel_ref, FLAT + 1), 0.0)
    keep_ref[11 * NZ : 12 * NZ] = row(d_ref, ROWS - 2) - jnp.minimum(row(vel_ref, FLAT + ROWS - 2), 0.0)
    step(p_ref, q_ref, 0)
    for d in range(3):
        sums = restrict_tile(plane_sums(vel_ref.at[d * FLAT : (d + 1) * FLAT]))
        coarse_ref[d] = sums * (0.5 / 64)
    coarse_ref[3] = restrict_tile(plane_sums(d_ref)) * (0.125 / 64)
    rstart_ref[...] = restrict_tile(plane_sums(v_ref)) * (1.0 / 64)


def finish_kernel(parts, place_ref, q_ref, lo_ref, hi_ref, fromlow_ref, fromhigh_ref, keep_ref, nextstart_ref, fine_ref, tiles_ref):
    has_low = place_ref[0] > 0
    has_high = place_ref[1] > 0
    part = lambda ref, j: ref[j * NZ : (j + 1) * NZ]
    sub, lane = iotas((NZ, LANES))
    fine_ref[...] = q_ref[...]
    for side in range(2):
        far, own, there = (
            (fromlow_ref, lo_ref, has_low) if side == 0 else (fromhigh_ref, hi_ref, has_high)
        )
        wbz, waz, wby, way, centre, inner = (part(keep_ref, side * 6 + j) for j in range(6))
        k = jnp.where(there, part(own, 2), 0.0)
        delta = k * part(far, 0)
        beyond = part(far, 1) + part(far, 2) * part(own, 0)
        edge = centre * delta + k * beyond
        edge += jnp.where(sub == 0, 0.0, wbz) * shifted(delta, -1, 0)
        edge += jnp.where(sub == NZ - 1, 0.0, waz) * shifted(delta, 1, 0)
        edge += jnp.where(lane == 0, 0.0, wby) * shifted(delta, -1, 1)
        edge += jnp.where(lane == LANES - 1, 0.0, way) * shifted(delta, 1, 1)
        e_at, i_at = (0, 1) if side == 0 else (ROWS - 1, ROWS - 2)
        fine_ref[pl.ds(e_at, NZ, stride=ROWS), :] = row(q_ref, e_at) + edge
        fine_ref[pl.ds(i_at, NZ, stride=ROWS), :] = row(q_ref, i_at) + inner * delta
    tile = restrict_tile(plane_sums(fine_ref)) * (1.0 / 64) - nextstart_ref[...]
    for j in range(parts):
        tiles_ref[j] = tile


def sweep_kernel(bricks, slices, place_ref, jumps_ref, *refs):
    coarse_refs = refs[:bricks]
    fine_ref, earlier_ref, start_ref, corrected_ref, jump_ref, change_ref = refs[bricks:]
    own, n = place_ref[0], place_ref[1]
    sub, lane = iotas((ROWS, LANES))
    zl, zh, y = lane % 4, sub % 4, lane // 4
    w = []
    for b in range(bricks):
        c = coarse_refs[b]
        wb = weights(c[0], c[1], c[2], c[3])
        wb[0] = jnp.where((zl == 0) & (zh == 0), 0.0, wb[0])
        wb[1] = jnp.where((zl == 3) & (zh == 3), 0.0, wb[1])
        wb[4] = jnp.where(y == 0, 0.0, wb[4])
        wb[5] = jnp.where(y == LANES // 4 - 1, 0.0, wb[5])
        if b == 0:
            wb[2] = jnp.where(sub < 4, 0.0, wb[2])
        if b == bricks - 1:
            wb[3] = jnp.where(sub < 4, wb[3], 0.0)
        w.append(wb)

    def coarse_step(m, change):
        e = [change[b] + jumps_ref[b * slices + m] for b in range(bricks)]
        half = [shifted(v, 4, 0) for v in e]
        out = []
        for b in range(bricks):
            v = e[b]
            lower = half[max(b - 1, 0)]
            upper = half[min(b + 1, bricks - 1)]
            zb = jnp.where(zl == 0, shifted(shifted(v, 3, 1), -1, 0), shifted(v, -1, 1))
            za = jnp.where(zl == 3, shifted(shifted(v, -3, 1), 1, 0), shifted(v, 1, 1))
            xb = jnp.where(sub < 4, lower, half[b])
            xa = jnp.where(sub < 4, half[b], upper)
            out.append(
                (w[b][6] * v + w[b][0] * zb + w[b][1] * za)
                + (w[b][2] * xb + w[b][3] * xa)
                + (w[b][4] * shifted(v, -4, 1) + w[b][5] * shifted(v, 4, 1))
            )
        return tuple(out)

    zero = tuple(jnp.zeros((ROWS, LANES), f32) for _ in range(bricks))
    change = lax.fori_loop(0, n, coarse_step, zero)
    for b in range(bricks):
        change_ref[b] = change[b]
    planes = prolong_tile(change_ref[own])
    for z in range(NZ):
        at = slice(z * ROWS, (z + 1) * ROWS)
        corrected_ref[at] = fine_ref[at] + planes[z // 4]
    first = n == 0
    jump_ref[...] = jnp.where(first, 0.0, start_ref[...] - earlier_ref[...])


def local(start_states, velocity, diffusivity):
    bricks, slices = lax.axis_size("space"), lax.axis_size("tm")
    own, n = lax.axis_index("space"), lax.axis_index("tm")
    start = start_states.reshape(FLAT, LANES)
    sds = lambda *shape: jax.ShapeDtypeStruct(shape, f32)
    ring = lambda count, by: [(i, (i + by) % count) for i in range(count)]
    vmem = pl.BlockSpec(memory_space=pltpu.VMEM)
    smem = pl.BlockSpec(memory_space=pltpu.SMEM)

    q, lo, hi, coarse, keep, rstart = pl.pallas_call(
        local_kernel,
        in_specs=[vmem] * 3,
        out_specs=[vmem] * 6,
        out_shape=[
            sds(FLAT, LANES),
            sds(3 * NZ, LANES),
            sds(3 * NZ, LANES),
            sds(4, ROWS, LANES),
            sds(12 * NZ, LANES),
            sds(ROWS, LANES),
        ],
        scratch_shapes=[pltpu.VMEM((FLAT + 2 * ROWS, LANES), f32)] * 2,
        name="local_steps",
    )(start, velocity.reshape(3 * FLAT, LANES), diffusivity.reshape(FLAT, LANES))

    fromlow = lax.ppermute(hi, "space", ring(bricks, 1))
    fromhigh = lax.ppermute(lo, "space", ring(bricks, bricks - 1))
    nextstart = lax.ppermute(rstart, "tm", ring(slices, slices - 1))
    coarse_all = lax.all_gather(coarse, "space")

    edges = jnp.stack([own, bricks - 1 - own]).astype(jnp.int32)
    fine, tiles = pl.pallas_call(
        lambda *refs: finish_kernel(bricks * slices, *refs),
        in_specs=[smem] + [vmem] * 7,
        out_specs=[vmem] * 2,
        out_shape=[sds(FLAT, LANES), sds(bricks * slices, ROWS, LANES)],
        name="finish_steps",
    )(edges, q, lo, hi, fromlow, fromhigh, keep, nextstart)

    earlier = lax.ppermute(fine, "tm", ring(slices, 1))
    jumps = lax.all_to_all(tiles, ("space", "tm"), 0, 0)

    place = jnp.stack([own, n]).astype(jnp.int32)
    corrected, jump = pl.pallas_call(
        lambda *refs: sweep_kernel(bricks, slices, *refs),
        in_specs=[smem] + [vmem] * (bricks + 4),
        out_specs=[vmem] * 2,
        out_shape=[sds(FLAT, LANES)] * 2,
        scratch_shapes=[pltpu.VMEM((bricks, ROWS, LANES), f32)],
        name="sweep",
    )(place, jumps, *[coarse_all[b] for b in range(bricks)], fine, earlier, start)
    shape = (1, NZ, ROWS, LANES)
    return corrected.reshape(shape), jump.reshape(shape)


def solution(mesh):
    in_specs = (
        P(("groups", "tm"), None, "space", None),
        P(None, None, "space", None),
        P(None, "space", None),
    )
    out_specs = (P(("groups", "tm"), None, "space", None), P(("groups", "tm"), None, "space", None))
    return jax.shard_map(local, mesh=mesh, in_specs=in_specs, out_specs=out_specs, check_vma=False)
```

time: 177 us -> 38 us (0.21); the launches traced: 175 us -> 37.7 us
  local copies, waits for them, and re-layouts: 96.6 us -> 1.98 us
  starting transfers between devices: 41.6 us -> 12.1 us
  other arithmetic: 16.1 us -> 1.19 us
  blocking collectives: 13.8 us -> 5.23 us
  Pallas kernels: 0 us -> 8.05 us
  waiting for transfers between devices: 5.44 us -> 8.5 us
    concatenate x4 -> x0, local copies, waits for them, and re-layouts: 60.8 us -> none  [local(): coefficients = jnp.concatenate([velocity, diffusivity[None]], 0)]
    ppermute x15 -> x4, starting transfers between devices: 41.6 us -> 8.6 us  [the longest x1 4.36 us: local(): nextstart = lax.ppermute(rstart, 'tm', ring(slices, slices - 1))]
    reshape x2 -> x0, local copies, waits for them, and re-layouts: 18.2 us -> none  [the longest x1 10 us: restrict(): tracer.reshape(dims_now[:-3] + (dims_now[-3] // 4, 4, dims_now[-2] // 4,...]
    another operation x2 -> x0, local copies, waits for them, and re-layouts: 10.8 us -> none  [the longest x1 10.8 us: restrict(): tracer.reshape(dims_now[:-3] + (dims_now[-3] // 4, 4, dims_now[-2] // 4,...]
    reduce_sum x3 -> x0, other arithmetic: 9.89 us -> none  [restrict(): return jnp.mean(reshaped, axis=(-5, -3, -1))]
    all_gather x1, blocking collectives: 13.8 us -> 5.23 us  [local(): coarse_all = lax.all_gather(coarse, 'space')]
    pallas_call x0 -> x3, Pallas kernels: none -> 8.05 us  [the longest x1 3.78 us: local(): pl.pallas_call(local_kernel, in_specs=[vmem] * 3, out_specs=[vmem] * 6, o...]
    broadcast_in_dim x1 -> x0, local copies, waits for them, and re-layouts: 4.36 us -> none  [prolong(): jnp.broadcast_to(coarse[:, None, :, None, :, None], (depth, 4, rows, 4, c...]
  transfers between devices with their start and end apart: 15 -> 5, of which waited for: 5 -> 2; matrix products, arithmetic and copies ran while one was open for 63% -> 5% of each run, Pallas kernels for 0% -> 0%
where the time goes in v1:
time: 38 us; the launch traced here: 37.7 us
  starting transfers between devices  12.1 us (32%)
  waiting for transfers between devices  8.5 us (22%)
  Pallas kernels  8.05 us (21%)
  blocking collectives  5.23 us (14%)
  local copies, waits for them, and re-layouts  1.98 us (5%)
  other arithmetic  1.19 us (3%)
  between operations  0.67 us (2%)
    all_gather x1, blocking collectives, local(): coarse_all = lax.all_gather(coarse, 'space')  5.23 us
    ppermute x1, waiting for transfers between devices, local(): earlier = lax.ppermute(fine, 'tm', ring(slices, 1))  4.72 us
    ppermute x1, starting transfers between devices, local(): nextstart = lax.ppermute(rstart, 'tm', ring(slices, slices - 1))  4.36 us
    pallas_call x1, Pallas kernels, local(): pl.pallas_call(local_kernel, in_specs=[vmem] * 3, out_specs=[vmem] * 6, o...  3.78 us
    all_to_all x1, waiting for transfers between devices, local(): jumps = lax.all_to_all(tiles, ('space', 'tm'), 0, 0)  3.77 us
    all_to_all x1, starting transfers between devices, local(): jumps = lax.all_to_all(tiles, ('space', 'tm'), 0, 0)  3.48 us
    pallas_call x1, Pallas kernels, local(): pl.pallas_call(lambda *refs: sweep_kernel(bricks, slices, *refs), in_spec...  2.14 us
    pallas_call x1, Pallas kernels, local(): pl.pallas_call(lambda *refs: finish_kernel(bricks * slices, *refs), in_sp...  2.13 us
  transfers between devices with their start and end apart: 5, of which 2 were waited for; matrix products, arithmetic and copies ran while one was open for 5% of the time, Pallas kernels for 0%

profile of v1, /device:TPU:0, one launch (start us, length us, event | category | flops | bytes accessed | tf_op | source)
XLA Modules:
  0.0 37.7 jit_solution(16257935304593983971)
XLA Ops:
  0.6 3.8 %local_steps.1 = (f32[512,128]{1,0:T(8,128)}, f32[192,128]{1,0:T(8,128)}, f32[192,128]{1,0:T(8,128)}, f32[4,8,128]{2,1,0:T(8,128)}, f32[768,128]{1,0:T(8,128)}, /*index=5*/f32[8,128]{1,0:T(8,128)}) custom-call(f32[512,128]{1,0:T(8,128)} %bitcast.8, f32[1536,128]{1,0:T(8,128)} %bitcast.10, f32[512,128]{1,0:T(8,128)} %bitcast.11), custom_call_target="tpu_custom_call" | custom-call | tf_op jit(solution)/shard_map/local_steps/pallas_call | solution.py:215
  4.4 0.0 copy-start.4
  4.4 0.5 %collective-permute-start = (f32[192,128]{1,0:T(8,128)}, f32[192,128]{1,0:T(8,128)S(1)}, u32[]{:S(2)}, u32[]{:S(2)}) collective-permute-start(f32[192,128]{1,0:T(8,128)} %get-tuple-element.14.refs_3_), channel_id=1, source_target_pairs={{0,4},{4,8},{8,12},{12,0},{1,5},{5,9},{9,13},{13,1},{2,6},{6,10},{... | collective-permute-start | bytes 294920 | tf_op jit(solution)/shard_map/ppermute | solution.py:231
  4.9 2.0 %collective-permute-start.1 = (f32[192,128]{1,0:T(8,128)}, f32[192,128]{1,0:T(8,128)S(1)}, u32[]{:S(2)}, u32[]{:S(2)}) collective-permute-start(f32[192,128]{1,0:T(8,128)} %get-tuple-element.13.refs_2_), channel_id=1, source_target_pairs={{0,12},{4,0},{8,4},{12,8},{1,13},{5,1},{9,5},{13,9},{2,14},{6,2},{... | collective-permute-start | bytes 294920 | tf_op jit(solution)/shard_map/ppermute | solution.py:232
  6.8 4.4 %collective-permute-start.2 = (f32[8,128]{1,0:T(8,128)}, f32[8,128]{1,0:T(8,128)S(1)}, u32[]{:S(2)}, u32[]{:S(2)}) collective-permute-start(f32[8,128]{1,0:T(8,128)} %get-tuple-element.16), channel_id=1, source_target_pairs={{0,3},{1,0},{2,1},{3,2},{4,7},{5,4},{6,5},{7,6},{8,11},{9,8},{10,9... | collective-permute-start | bytes 12296 | tf_op jit(solution)/shard_map/ppermute | solution.py:233
  11.2 0.6 %pad_add_fusion.1.refs_0_ = s32[2]{0:T(128)} fusion(s32[1]{0:T(128)} %bitcast.2, s32[1]{0:T(128)} %bitcast), kind=kLoop, calls=%fused_computation.1 | loop fusion | flops 2 | bytes 16 | tf_op jit(solution)/shard_map/stack | solution.py:236
  11.8 0.0 copy-done.4
  11.8 5.2 %all-gather = f32[16,8,128]{2,1,0:T(8,128)S(1)} all-gather(f32[4,8,128]{2,1,0:T(8,128)S(1)} %copy-done.4), channel_id=2, replica_groups=mesh['groups'=2,'space'=4,'tm'=4] {'space'}, dimensions={0}, use_global_device_ids=true | all-gather | bytes 81920 | tf_op jit(solution)/shard_map/all_gather | solution.py:234
  17.1 0.0 collective-permute-done.2.refs_7_
  17.1 0.0 copy-start.5
  17.1 0.0 collective-permute-done.refs_4_
  17.1 0.0 copy-start.2
  17.1 0.0 collective-permute-done.1.refs_5_
  17.1 0.0 copy-start.3
  17.1 0.6 %copy-done.5 = f32[8,128]{1,0:T(8,128)} copy-done((f32[8,128]{1,0:T(8,128)}, f32[8,128]{1,0:T(8,128)S(1)}, u32[]{:S(2)}) %copy-start.5) | copy-done | bytes 4120
  17.7 0.0 copy-done.2
  17.7 0.0 copy-done.3
  17.7 2.1 %finish_steps.1 = (f32[512,128]{1,0:T(8,128)}, f32[16,8,128]{2,1,0:T(8,128)}) custom-call(s32[2]{0:T(128)} %pad_add_fusion.1.refs_0_, f32[512,128]{1,0:T(8,128)} %get-tuple-element.12.refs_1_, f32[192,128]{1,0:T(8,128)} %get-tuple-element.13.refs_2_, f32[192,128]{1,0:T(8,128)} %get-tuple-element.14.refs_3_, f32[192,128]{1,0:T(8,128)} %copy-done.2, ...), custom_call_target="tpu_custom_call" | custom-call | tf_op jit(solution)/shard_map/finish_steps/pallas_call | solution.py:237
  19.9 3.5 %all-to-all-start = ((f32[16,8,128]{2,1,0:T(8,128)}), f32[16,8,128]{2,1,0:T(8,128)S(1)}, u32[]{:S(2)}, u32[]{:S(2)}) async-start(f32[16,8,128]{2,1,0:T(8,128)} %get-tuple-element.17), calls=%async_computation | async-start | bytes 131072 | tf_op jit(solution)/shard_map/all_to_all | solution.py:246
  23.4 1.8 %collective-permute-start.3 = (f32[512,128]{1,0:T(8,128)}, f32[512,128]{1,0:T(8,128)S(1)}, u32[]{:S(2)}, u32[]{:S(2)}) collective-permute-start(f32[512,128]{1,0:T(8,128)} %get-tuple-element.19.refs_6_), channel_id=1, source_target_pairs={{0,1},{1,2},{2,3},{3,0},{4,5},{5,6},{6,7},{7,4},{8,9},{9,10},{10,1... | collective-permute-start | bytes 786440 | tf_op jit(solution)/shard_map/ppermute | solution.py:245
  25.2 0.6 %fusion = (f32[4,8,128]{2,1,0:T(8,128)}, f32[4,8,128]{2,1,0:T(8,128)}, f32[4,8,128]{2,1,0:T(8,128)}, f32[4,8,128]{2,1,0:T(8,128)}) fusion(f32[16,8,128]{2,1,0:T(8,128)S(1)} %all-gather), kind=kLoop, calls=%fused_computation.2 | loop fusion | bytes 131072 | tf_op jit(solution)/shard_map/slice | solution.py:256
  25.8 0.6 %pad_add_fusion.refs_0_ = s32[2]{0:T(128)} fusion(s32[1]{0:T(128)} %bitcast.1, s32[1]{0:T(128)} %bitcast), kind=kLoop, calls=%fused_computation | loop fusion | flops 2 | bytes 16 | tf_op jit(solution)/shard_map/stack | solution.py:248
  26.4 3.8 %all-to-all-done.refs_1_ = f32[16,8,128]{2,1,0:T(8,128)S(1)} async-done(((f32[16,8,128]{2,1,0:T(8,128)}), f32[16,8,128]{2,1,0:T(8,128)S(1)}, u32[]{:S(2)}, u32[]{:S(2)}) %all-to-all-start) | async-done | bytes 65568 | tf_op jit(solution)/shard_map/all_to_all | solution.py:246
  30.1 0.0 copy-start.1
  30.1 4.7 %collective-permute-done.3.refs_7_ = f32[512,128]{1,0:T(8,128)S(1)} collective-permute-done((f32[512,128]{1,0:T(8,128)}, f32[512,128]{1,0:T(8,128)S(1)}, u32[]{:S(2)}, u32[]{:S(2)}) %collective-permute-start.3) | collective-permute-done | bytes 262176 | tf_op jit(solution)/shard_map/ppermute | solution.py:245
  34.9 0.0 copy-start
  34.9 0.0 copy-done.1
  34.9 0.7 %copy-done = f32[512,128]{1,0:T(8,128)} copy-done((f32[512,128]{1,0:T(8,128)}, f32[512,128]{1,0:T(8,128)S(1)}, u32[]{:S(2)}) %copy-start) | copy-done | bytes 262168
  35.6 2.1 %sweep.1 = (f32[512,128]{1,0:T(8,128)}, f32[512,128]{1,0:T(8,128)}) custom-call(s32[2]{0:T(128)} %pad_add_fusion.refs_0_, f32[16,8,128]{2,1,0:T(8,128)} %copy-done.1, f32[4,8,128]{2,1,0:T(8,128)} %get-tuple-element.25.refs_2_, f32[4,8,128]{2,1,0:T(8,128)} %get-tuple-element.24.refs_3_, f32[4,8,128]{2,1,0:T(8,128)} %get-tuple-element.23.refs_4_, ...), custom_call_target="tpu_custom_call" | custom-call | tf_op jit(solution)/shard_map/sweep/pallas_call | solution.py:249
Async XLA Ops:
  4.4 7.4 %copy-start.4 = (f32[4,8,128]{2,1,0:T(8,128)S(1)}, f32[4,8,128]{2,1,0:T(8,128)}, u32[]{:S(2)}) copy-start(f32[4,8,128]{2,1,0:T(8,128)} %get-tuple-element.18) | copy-start | bytes 49156
  4.4 12.7 %collective-permute-start = (f32[192,128]{1,0:T(8,128)}, f32[192,128]{1,0:T(8,128)S(1)}, u32[]{:S(2)}, u32[]{:S(2)}) collective-permute-start(f32[192,128]{1,0:T(8,128)} %get-tuple-element.14.refs_3_), channel_id=1, source_target_pairs={{0,4},{4,8},{8,12},{12,0},{1,5},{5,9},{9,13},{13,1},{2,6},{6,10},{... | collective-permute-start | bytes 294920 | tf_op jit(solution)/shard_map/ppermute | solution.py:231
  4.9 12.2 %collective-permute-start.1 = (f32[192,128]{1,0:T(8,128)}, f32[192,128]{1,0:T(8,128)S(1)}, u32[]{:S(2)}, u32[]{:S(2)}) collective-permute-start(f32[192,128]{1,0:T(8,128)} %get-tuple-element.13.refs_2_), channel_id=1, source_target_pairs={{0,12},{4,0},{8,4},{12,8},{1,13},{5,1},{9,5},{13,9},{2,14},{6,2},{... | collective-permute-start | bytes 294920 | tf_op jit(solution)/shard_map/ppermute | solution.py:232
  6.8 10.2 %collective-permute-start.2 = (f32[8,128]{1,0:T(8,128)}, f32[8,128]{1,0:T(8,128)S(1)}, u32[]{:S(2)}, u32[]{:S(2)}) collective-permute-start(f32[8,128]{1,0:T(8,128)} %get-tuple-element.16), channel_id=1, source_target_pairs={{0,3},{1,0},{2,1},{3,2},{4,7},{5,4},{6,5},{7,6},{8,11},{9,8},{10,9... | collective-permute-start | bytes 12296 | tf_op jit(solution)/shard_map/ppermute | solution.py:233
  17.1 0.6 %copy-start.5 = (f32[8,128]{1,0:T(8,128)}, f32[8,128]{1,0:T(8,128)S(1)}, u32[]{:S(2)}) copy-start(f32[8,128]{1,0:T(8,128)S(1)} %collective-permute-done.2.refs_7_) | copy-start | bytes 12292
  17.1 0.6 %copy-start.2 = (f32[192,128]{1,0:T(8,128)}, f32[192,128]{1,0:T(8,128)S(1)}, u32[]{:S(2)}) copy-start(f32[192,128]{1,0:T(8,128)S(1)} %collective-permute-done.refs_4_) | copy-start | bytes 294916
  17.1 0.7 %copy-start.3 = (f32[192,128]{1,0:T(8,128)}, f32[192,128]{1,0:T(8,128)S(1)}, u32[]{:S(2)}) copy-start(f32[192,128]{1,0:T(8,128)S(1)} %collective-permute-done.1.refs_5_) | copy-start | bytes 294916
  19.9 10.3 %all-to-all-start = ((f32[16,8,128]{2,1,0:T(8,128)}), f32[16,8,128]{2,1,0:T(8,128)S(1)}, u32[]{:S(2)}, u32[]{:S(2)}) async-start(f32[16,8,128]{2,1,0:T(8,128)} %get-tuple-element.17), calls=%async_computation | async-start | bytes 131072 | tf_op jit(solution)/shard_map/all_to_all | solution.py:246
  23.4 11.5 %collective-permute-start.3 = (f32[512,128]{1,0:T(8,128)}, f32[512,128]{1,0:T(8,128)S(1)}, u32[]{:S(2)}, u32[]{:S(2)}) collective-permute-start(f32[512,128]{1,0:T(8,128)} %get-tuple-element.19.refs_6_), channel_id=1, source_target_pairs={{0,1},{1,2},{2,3},{3,0},{4,5},{5,6},{6,7},{7,4},{8,9},{9,10},{10,1... | collective-permute-start | bytes 786440 | tf_op jit(solution)/shard_map/ppermute | solution.py:245
  30.1 4.7 %copy-start.1 = (f32[16,8,128]{2,1,0:T(8,128)}, f32[16,8,128]{2,1,0:T(8,128)S(1)}, u32[]{:S(2)}) copy-start(f32[16,8,128]{2,1,0:T(8,128)S(1)} %all-to-all-done.refs_1_) | copy-start | bytes 196612
  34.9 0.7 %copy-start = (f32[512,128]{1,0:T(8,128)}, f32[512,128]{1,0:T(8,128)S(1)}, u32[]{:S(2)}) copy-start(f32[512,128]{1,0:T(8,128)S(1)} %collective-permute-done.3.refs_7_) | copy-start | bytes 786436

commit v2 on v1

--- a/solution.py
+++ b/solution.py
@@ -72,7 +72,30 @@
     return ref[pl.ds(at, NZ, stride=ROWS), :]
 
 
-def local_kernel(v_ref, vel_ref, d_ref, q_ref, lo_ref, hi_ref, coarse_ref, keep_ref, rstart_ref, p_ref, pv_ref):
+def edges_kernel(v_hbm, vel_hbm, d_hbm, v_ref, vel_ref, d_ref, lo_ref, hi_ref, sems):
+    copies = [
+        pltpu.make_async_copy(src, dst, sems.at[i])
+        for i, (src, dst) in enumerate(((v_hbm, v_ref), (d_hbm, d_ref), (vel_hbm, vel_ref)))
+    ]
+    for copy in copies:
+        copy.start()
+    for copy in copies:
+        copy.wait()
+    sub, lane = iotas((NZ, LANES))
+    for out, face, inner, side in ((lo_ref, 0, 1, 0), (hi_ref, ROWS - 1, ROWS - 2, 1)):
+        w = weights(*(row(vel_ref, d * FLAT + face) for d in range(3)), row(d_ref, face))
+        v = row(v_ref, face)
+        total = w[6] * v + w[3 - side] * row(v_ref, inner)
+        total += jnp.where(sub == 0, 0.0, w[0]) * shifted(v, -1, 0)
+        total += jnp.where(sub == NZ - 1, 0.0, w[1]) * shifted(v, 1, 0)
+        total += jnp.where(lane == 0, 0.0, w[4]) * shifted(v, -1, 1)
+        total += jnp.where(lane == LANES - 1, 0.0, w[5]) * shifted(v, 1, 1)
+        out[0:NZ] = v
+        out[NZ : 2 * NZ] = total
+        out[2 * NZ : 3 * NZ] = w[2 + side]
+
+
+def steps_kernel(v_ref, vel_ref, d_ref, q_ref, coarse_ref, keep_ref, rstart_ref, p_ref, pv_ref):
     zero = jnp.zeros((ROWS, LANES), f32)
     for ref in (p_ref, pv_ref):
         ref[0:ROWS] = zero
@@ -101,23 +124,13 @@
         lax.fori_loop(0, NZ // CHUNK, body, 0)
 
     step(pv_ref, p_ref, ROWS)
-    diff0, diff7 = row(d_ref, 0), row(d_ref, ROWS - 1)
-    cx0, cx7 = row(vel_ref, FLAT), row(vel_ref, FLAT + ROWS - 1)
-    k0 = diff0 + jnp.maximum(cx0, 0.0)
-    k7 = diff7 - jnp.minimum(cx7, 0.0)
-    lo_ref[0:NZ] = row(v_ref, 0)
-    lo_ref[NZ : 2 * NZ] = row(p_ref, ROWS)
-    lo_ref[2 * NZ : 3 * NZ] = k0
-    hi_ref[0:NZ] = row(v_ref, ROWS - 1)
-    hi_ref[NZ : 2 * NZ] = row(p_ref, 2 * ROWS - 1)
-    hi_ref[2 * NZ : 3 * NZ] = k7
+    step(p_ref, q_ref, 0)
     for side, at in enumerate((0, ROWS - 1)):
         w = weights(*(row(vel_ref, d * FLAT + at) for d in range(3)), row(d_ref, at))
         for j, value in enumerate((w[0], w[1], w[4], w[5], w[6])):
             keep_ref[(side * 6 + j) * NZ : (side * 6 + j + 1) * NZ] = value
     keep_ref[5 * NZ : 6 * NZ] = row(d_ref, 1) + jnp.maximum(row(vel_ref, FLAT + 1), 0.0)
     keep_ref[11 * NZ : 12 * NZ] = row(d_ref, ROWS - 2) - jnp.minimum(row(vel_ref, FLAT + ROWS - 2), 0.0)
-    step(p_ref, q_ref, 0)
     for d in range(3):
         sums = restrict_tile(plane_sums(vel_ref.at[d * FLAT : (d + 1) * FLAT]))
         coarse_ref[d] = sums * (0.5 / 64)
@@ -125,9 +138,10 @@
     rstart_ref[...] = restrict_tile(plane_sums(v_ref)) * (1.0 / 64)
 
 
-def finish_kernel(parts, place_ref, q_ref, lo_ref, hi_ref, fromlow_ref, fromhigh_ref, keep_ref, nextstart_ref, fine_ref, tiles_ref):
-    has_low = place_ref[0] > 0
-    has_high = place_ref[1] > 0
+def finish_kernel(parts, bricks, q_ref, lo_ref, hi_ref, fromlow_ref, fromhigh_ref, keep_ref, rstart_ref, fine_ref, tiles_ref):
+    own_brick = lax.axis_index("space")
+    has_low = own_brick > 0
+    has_high = own_brick < bricks - 1
     part = lambda ref, j: ref[j * NZ : (j + 1) * NZ]
     sub, lane = iotas((NZ, LANES))
     fine_ref[...] = q_ref[...]
@@ -147,20 +161,29 @@
         e_at, i_at = (0, 1) if side == 0 else (ROWS - 1, ROWS - 2)
         fine_ref[pl.ds(e_at, NZ, stride=ROWS), :] = row(q_ref, e_at) + edge
         fine_ref[pl.ds(i_at, NZ, stride=ROWS), :] = row(q_ref, i_at) + inner * delta
-    tile = restrict_tile(plane_sums(fine_ref)) * (1.0 / 64) - nextstart_ref[...]
+    tile = restrict_tile(plane_sums(fine_ref)) * (1.0 / 64)
+    rstart = rstart_ref[...]
     for j in range(parts):
-        tiles_ref[j] = tile
-
-
-def sweep_kernel(bricks, slices, place_ref, jumps_ref, *refs):
+        tiles_ref[j, 0:ROWS] = tile
+        tiles_ref[j, ROWS : 2 * ROWS] = rstart
+
+
+def jump_kernel(earlier_ref, start_ref, jump_ref):
+    first = lax.axis_index("tm") == 0
+    jump_ref[...] = jnp.where(first, 0.0, start_ref[...] - earlier_ref[...])
+
+
+def sweep_kernel(bricks, slices, images_ref, fine_ref, *refs):
     coarse_refs = refs[:bricks]
-    fine_ref, earlier_ref, start_ref, corrected_ref, jump_ref, change_ref = refs[bricks:]
-    own, n = place_ref[0], place_ref[1]
+    corrected_ref, change_ref, coef_ref = refs[bricks:]
+    own, n = lax.axis_index("space"), lax.axis_index("tm")
+    for k in range(bricks):
+        coef_ref[(own + bricks - k) % bricks] = coarse_refs[k][...]
     sub, lane = iotas((ROWS, LANES))
     zl, zh, y = lane % 4, sub % 4, lane // 4
     w = []
     for b in range(bricks):
-        c = coarse_refs[b]
+        c = coef_ref.at[b]
         wb = weights(c[0], c[1], c[2], c[3])
         wb[0] = jnp.where((zl == 0) & (zh == 0), 0.0, wb[0])
         wb[1] = jnp.where((zl == 3) & (zh == 3), 0.0, wb[1])
@@ -173,7 +196,10 @@
         w.append(wb)
 
     def coarse_step(m, change):
-        e = [change[b] + jumps_ref[b * slices + m] for b in range(bricks)]
+        e = [
+            change[b] + (images_ref[b * slices + m, 0:ROWS] - images_ref[b * slices + m + 1, ROWS : 2 * ROWS])
+            for b in range(bricks)
+        ]
         half = [shifted(v, 4, 0) for v in e]
         out = []
         for b in range(bricks):
@@ -199,61 +225,82 @@
     for z in range(NZ):
         at = slice(z * ROWS, (z + 1) * ROWS)
         corrected_ref[at] = fine_ref[at] + planes[z // 4]
-    first = n == 0
-    jump_ref[...] = jnp.where(first, 0.0, start_ref[...] - earlier_ref[...])
 
 
 def local(start_states, velocity, diffusivity):
     bricks, slices = lax.axis_size("space"), lax.axis_size("tm")
-    own, n = lax.axis_index("space"), lax.axis_index("tm")
-    start = start_states.reshape(FLAT, LANES)
-    sds = lambda *shape: jax.ShapeDtypeStruct(shape, f32)
+    parts = bricks * slices
     ring = lambda count, by: [(i, (i + by) % count) for i in range(count)]
-    vmem = pl.BlockSpec(memory_space=pltpu.VMEM)
-    smem = pl.BlockSpec(memory_space=pltpu.SMEM)
-
-    q, lo, hi, coarse, keep, rstart = pl.pallas_call(
-        local_kernel,
+    out = lambda *shape: pltpu.VMEM(shape, f32)
+    vmem, anyspace = pl.BlockSpec(memory_space=pltpu.VMEM), pl.BlockSpec(memory_space=pl.ANY)
+    inside = lambda *xs: [pltpu.with_memory_space_constraint(x, pltpu.VMEM) for x in xs]
+
+    v, vel, diff, lo, hi = pl.pallas_call(
+        edges_kernel,
+        in_specs=[anyspace] * 3,
+        out_specs=[vmem] * 5,
+        out_shape=[
+            out(FLAT, LANES),
+            out(3 * FLAT, LANES),
+            out(FLAT, LANES),
+            out(3 * NZ, LANES),
+            out(3 * NZ, LANES),
+        ],
+        scratch_shapes=[pltpu.SemaphoreType.DMA((3,))],
+        name="edges",
+    )(
+        start_states.reshape(FLAT, LANES),
+        velocity.reshape(3 * FLAT, LANES),
+        diffusivity.reshape(FLAT, LANES),
+    )
+    fromlow = lax.ppermute(hi, "space", ring(bricks, 1))
+    fromhigh = lax.ppermute(lo, "space", ring(bricks, bricks - 1))
+
+    q, coarse, keep, rstart = pl.pallas_call(
+        steps_kernel,
         in_specs=[vmem] * 3,
-        out_specs=[vmem] * 6,
+        out_specs=[vmem] * 4,
         out_shape=[
-            sds(FLAT, LANES),
-            sds(3 * NZ, LANES),
-            sds(3 * NZ, LANES),
-            sds(4, ROWS, LANES),
-            sds(12 * NZ, LANES),
-            sds(ROWS, LANES),
+            out(FLAT, LANES),
+            out(4, ROWS, LANES),
+            out(12 * NZ, LANES),
+            out(ROWS, LANES),
         ],
         scratch_shapes=[pltpu.VMEM((FLAT + 2 * ROWS, LANES), f32)] * 2,
-        name="local_steps",
-    )(start, velocity.reshape(3 * FLAT, LANES), diffusivity.reshape(FLAT, LANES))
-
-    fromlow = lax.ppermute(hi, "space", ring(bricks, 1))
-    fromhigh = lax.ppermute(lo, "space", ring(bricks, bricks - 1))
-    nextstart = lax.ppermute(rstart, "tm", ring(slices, slices - 1))
-    coarse_all = lax.all_gather(coarse, "space")
-
-    edges = jnp.stack([own, bricks - 1 - own]).astype(jnp.int32)
+        name="steps",
+    )(*inside(v, vel, diff))
+
     fine, tiles = pl.pallas_call(
-        lambda *refs: finish_kernel(bricks * slices, *refs),
-        in_specs=[smem] + [vmem] * 7,
+        lambda *refs: finish_kernel(parts, bricks, *refs),
+        in_specs=[vmem] * 7,
         out_specs=[vmem] * 2,
-        out_shape=[sds(FLAT, LANES), sds(bricks * slices, ROWS, LANES)],
-        name="finish_steps",
-    )(edges, q, lo, hi, fromlow, fromhigh, keep, nextstart)
+        out_shape=[out(FLAT, LANES), out(parts, 2 * ROWS, LANES)],
+        name="finish",
+    )(*inside(q, lo, hi, fromlow, fromhigh, keep, rstart))
 
     earlier = lax.ppermute(fine, "tm", ring(slices, 1))
-    jumps = lax.all_to_all(tiles, ("space", "tm"), 0, 0)
-
-    place = jnp.stack([own, n]).astype(jnp.int32)
-    corrected, jump = pl.pallas_call(
+    images = lax.all_to_all(tiles, ("space", "tm"), 0, 0)
+    coarse_all = [coarse] + [lax.ppermute(coarse, "space", ring(bricks, k)) for k in range(1, bricks)]
+
+    jump = pl.pallas_call(
+        jump_kernel,
+        in_specs=[vmem] * 2,
+        out_specs=vmem,
+        out_shape=jax.ShapeDtypeStruct((FLAT, LANES), f32),
+        name="jump",
+    )(*inside(earlier, v))
+
+    corrected = pl.pallas_call(
         lambda *refs: sweep_kernel(bricks, slices, *refs),
-        in_specs=[smem] + [vmem] * (bricks + 4),
-        out_specs=[vmem] * 2,
-        out_shape=[sds(FLAT, LANES)] * 2,
-        scratch_shapes=[pltpu.VMEM((bricks, ROWS, LANES), f32)],
+        in_specs=[vmem] * (bricks + 2),
+        out_specs=vmem,
+        out_shape=jax.ShapeDtypeStruct((FLAT, LANES), f32),
+        scratch_shapes=[
+            pltpu.VMEM((bricks, ROWS, LANES), f32),
+            pltpu.VMEM((bricks, 4, ROWS, LANES), f32),
+        ],
         name="sweep",
-    )(place, jumps, *[coarse_all[b] for b in range(bricks)], fine, earlier, start)
+    )(*inside(images, fine, *coarse_all))
     shape = (1, NZ, ROWS, LANES)
     return corrected.reshape(shape), jump.reshape(shape)
 

time: 38 us -> 25.4 us (0.67)
  blocking collectives: 5.23 us -> 0 us
  Pallas kernels: 8.05 us -> 5.75 us
  local copies, waits for them, and re-layouts: 1.98 us -> 0 us
  other arithmetic: 1.19 us -> 0 us
  starting transfers between devices: 12.1 us -> 11.1 us
  waiting for transfers between devices: 8.5 us -> 7.64 us
    all_gather x1 -> x0, blocking collectives: 5.23 us -> none  [local(): coarse_all = lax.all_gather(coarse, 'space')]
    ppermute x1, waiting for transfers between devices: 4.72 us -> 0.01 us  [local(): earlier = lax.ppermute(fine, 'tm', ring(slices, 1))]
    ppermute x1 -> x3, waiting for transfers between devices: 0.01 us -> 3.33 us  [local(): lax.ppermute(coarse, 'space', ring(bricks, k))]
    ppermute x1 -> x3, starting transfers between devices: 4.36 us -> 2.19 us  [local(): lax.ppermute(coarse, 'space', ring(bricks, k))]
    all_to_all x1, waiting for transfers between devices: 3.77 us -> 1.83 us  [local(): images = lax.all_to_all(tiles, ('space', 'tm'), 0, 0)]
    ppermute x1, waiting for transfers between devices: 0.01 us -> 1.4 us  [local(): fromhigh = lax.ppermute(lo, 'space', ring(bricks, bricks - 1))]
    all_to_all x1, starting transfers between devices: 3.48 us -> 4.87 us  [local(): images = lax.all_to_all(tiles, ('space', 'tm'), 0, 0)]
    unnamed x12 -> x0, local copies, waits for them, and re-layouts: 1.36 us -> none
  transfers between devices with their start and end apart: 5 -> 7, of which waited for: 2 -> 5; matrix products, arithmetic and copies ran while one was open for 5% -> 0% of each run, Pallas kernels for 0% -> 10%
where the time goes in v2:
time: 25.4 us; the launch traced here: 25.1 us
  starting transfers between devices  11.1 us (44%)
  waiting for transfers between devices  7.64 us (30%)
  Pallas kernels  5.75 us (23%)
  between operations  0.66 us (3%)
    all_to_all x1, starting transfers between devices, local(): images = lax.all_to_all(tiles, ('space', 'tm'), 0, 0)  4.87 us
    ppermute x3, waiting for transfers between devices, local(): lax.ppermute(coarse, 'space', ring(bricks, k))  3.33 us
    ppermute x1, starting transfers between devices, local(): fromhigh = lax.ppermute(lo, 'space', ring(bricks, bricks - 1))  2.43 us
    ppermute x3, starting transfers between devices, local(): lax.ppermute(coarse, 'space', ring(bricks, k))  2.19 us
    all_to_all x1, waiting for transfers between devices, local(): images = lax.all_to_all(tiles, ('space', 'tm'), 0, 0)  1.83 us
    pallas_call x1, Pallas kernels, local(): pl.pallas_call(steps_kernel, in_specs=[vmem] * 3, out_specs=[vmem] * 4, o...  1.72 us
    ppermute x1, starting transfers between devices, local(): earlier = lax.ppermute(fine, 'tm', ring(slices, 1))  1.58 us
    pallas_call x1, Pallas kernels, local(): pl.pallas_call(edges_kernel, in_specs=[anyspace] * 3, out_specs=[vmem] *...  1.43 us
  transfers between devices with their start and end apart: 7, of which 5 were waited for; matrix products, arithmetic and copies ran while one was open for 0% of the time, Pallas kernels for 10%

profile of v2, /device:TPU:0, one launch (start us, length us, event | category | flops | bytes accessed | tf_op | source)
XLA Modules:
  0.0 25.1 jit_solution(3260260330233288953)
XLA Ops:
  0.6 1.4 %edges.1 = (f32[512,128]{1,0:T(8,128)S(1)}, f32[1536,128]{1,0:T(8,128)S(1)}, f32[512,128]{1,0:T(8,128)S(1)}, f32[192,128]{1,0:T(8,128)S(1)}, f32[192,128]{1,0:T(8,128)S(1)}) custom-call(f32[512,128]{1,0:T(8,128)} %bitcast.6, f32[1536,128]{1,0:T(8,128)} %bitcast.5, f32[512,128]{1,0:T(8,128)} %bitcast.7), custom_call_target="tpu_custom_call" | custom-call | tf_op jit(solution)/shard_map/edges/pallas_call | solution.py:238
  2.1 2.4 %collective-permute-start.1 = (f32[192,128]{1,0:T(8,128)S(1)}, f32[192,128]{1,0:T(8,128)S(1)}, u32[]{:S(2)}, u32[]{:S(2)}) collective-permute-start(f32[192,128]{1,0:T(8,128)S(1)} %get-tuple-element.17.refs_1_), channel_id=1, source_target_pairs={{0,12},{4,0},{8,4},{12,8},{1,13},{5,1},{9,5},{13,9},{2,14},{6,2},{... | collective-permute-start | bytes 294920 | tf_op jit(solution)/shard_map/ppermute | solution.py:257
  4.5 0.0 collective-permute-start
  4.5 1.7 %steps.1 = (f32[512,128]{1,0:T(8,128)S(1)}, f32[4,8,128]{2,1,0:T(8,128)S(1)}, f32[768,128]{1,0:T(8,128)S(1)}, f32[8,128]{1,0:T(8,128)S(1)}) custom-call(f32[512,128]{1,0:T(8,128)S(1)} %get-tuple-element.13.v_ref.start_ref, f32[1536,128]{1,0:T(8,128)S(1)} %get-tuple-element.14.vel_ref, f32[512,128]{1,0:T(8,128)S(1)} %get-tuple-element.15.d_ref), custom_call_target="tpu_custom_call" | custom-call | tf_op jit(solution)/shard_map/steps/pallas_call | solution.py:259
  6.2 1.4 %collective-permute-done.1.refs_4_ = f32[192,128]{1,0:T(8,128)S(1)} collective-permute-done((f32[192,128]{1,0:T(8,128)S(1)}, f32[192,128]{1,0:T(8,128)S(1)}, u32[]{:S(2)}, u32[]{:S(2)}) %collective-permute-start.1) | collective-permute-done | bytes 98336 | tf_op jit(solution)/shard_map/ppermute | solution.py:257
  7.6 1.1 %collective-permute-done.refs_3_ = f32[192,128]{1,0:T(8,128)S(1)} collective-permute-done((f32[192,128]{1,0:T(8,128)S(1)}, f32[192,128]{1,0:T(8,128)S(1)}, u32[]{:S(2)}, u32[]{:S(2)}) %collective-permute-start) | collective-permute-done | bytes 98336 | tf_op jit(solution)/shard_map/ppermute | solution.py:256
  8.7 1.0 %finish.1 = (f32[512,128]{1,0:T(8,128)S(1)}, f32[16,16,128]{2,1,0:T(8,128)}) custom-call(f32[512,128]{1,0:T(8,128)S(1)} %get-tuple-element.16.refs_0_, f32[192,128]{1,0:T(8,128)S(1)} %get-tuple-element.17.refs_1_, f32[192,128]{1,0:T(8,128)S(1)} %get-tuple-element.18.refs_2_, f32[192,128]{1,0:T(8,128)S(1)} %collective-permute-done.refs_3_, ...), custom_call_target="tpu_custom_call" | custom-call | tf_op jit(solution)/shard_map/finish/pallas_call | solution.py:273
  9.7 1.6 %collective-permute-start.5 = (f32[512,128]{1,0:T(8,128)S(1)}, f32[512,128]{1,0:T(8,128)S(1)}, u32[]{:S(2)}, u32[]{:S(2)}) collective-permute-start(f32[512,128]{1,0:T(8,128)S(1)} %get-tuple-element.22.refs_1_), channel_id=1, source_target_pairs={{0,1},{1,2},{2,3},{3,0},{4,5},{5,6},{6,7},{7,4},{8,9},{9,10},{10,1... | collective-permute-start | bytes 786440 | tf_op jit(solution)/shard_map/ppermute | solution.py:281
  11.2 4.9 %all-to-all-start = ((f32[16,16,128]{2,1,0:T(8,128)}), f32[16,16,128]{2,1,0:T(8,128)S(1)}, u32[]{:S(2)}, u32[]{:S(2)}) async-start(f32[16,16,128]{2,1,0:T(8,128)} %get-tuple-element.21), calls=%async_computation | async-start | bytes 262144 | tf_op jit(solution)/shard_map/all_to_all | solution.py:282
  16.1 1.7 %collective-permute-start.4 = (f32[4,8,128]{2,1,0:T(8,128)S(1)}, f32[4,8,128]{2,1,0:T(8,128)S(1)}, u32[]{:S(2)}, u32[]{:S(2)}) collective-permute-start(f32[4,8,128]{2,1,0:T(8,128)S(1)} %get-tuple-element.23.refs_2_), channel_id=1, source_target_pairs={{0,12},{4,0},{8,4},{12,8},{1,13},{5,1},{9,5},{13,9},{2,14},{6,2},{... | collective-permute-start | bytes 49160 | tf_op jit(solution)/shard_map/ppermute | solution.py:283
  17.8 0.4 %collective-permute-start.3 = (f32[4,8,128]{2,1,0:T(8,128)S(1)}, f32[4,8,128]{2,1,0:T(8,128)S(1)}, u32[]{:S(2)}, u32[]{:S(2)}) collective-permute-start(f32[4,8,128]{2,1,0:T(8,128)S(1)} %get-tuple-element.23.refs_2_), channel_id=1, source_target_pairs={{0,8},{4,12},{8,0},{12,4},{1,9},{5,13},{9,1},{13,5},{2,10},{6,14},... | collective-permute-start | bytes 49160 | tf_op jit(solution)/shard_map/ppermute | solution.py:283
  18.2 0.1 collective-permute-start.2
  18.3 0.9 %collective-permute-done.4.refs_5_ = f32[4,8,128]{2,1,0:T(8,128)S(1)} collective-permute-done((f32[4,8,128]{2,1,0:T(8,128)S(1)}, f32[4,8,128]{2,1,0:T(8,128)S(1)}, u32[]{:S(2)}, u32[]{:S(2)}) %collective-permute-start.4) | collective-permute-done | bytes 16416 | tf_op jit(solution)/shard_map/ppermute | solution.py:283
  19.3 2.4 %collective-permute-done.3.refs_4_ = f32[4,8,128]{2,1,0:T(8,128)S(1)} collective-permute-done((f32[4,8,128]{2,1,0:T(8,128)S(1)}, f32[4,8,128]{2,1,0:T(8,128)S(1)}, u32[]{:S(2)}, u32[]{:S(2)}) %collective-permute-start.3) | collective-permute-done | bytes 16416 | tf_op jit(solution)/shard_map/ppermute | solution.py:283
  21.6 0.0 collective-permute-done.2.refs_3_
  21.6 1.8 %all-to-all-done.refs_0_ = f32[16,16,128]{2,1,0:T(8,128)S(1)} async-done(((f32[16,16,128]{2,1,0:T(8,128)}), f32[16,16,128]{2,1,0:T(8,128)S(1)}, u32[]{:S(2)}, u32[]{:S(2)}) %all-to-all-start) | async-done | bytes 131104 | tf_op jit(solution)/shard_map/all_to_all | solution.py:282
  23.5 0.9 %sweep.1 = f32[512,128]{1,0:T(8,128)} custom-call(f32[16,16,128]{2,1,0:T(8,128)S(1)} %all-to-all-done.refs_0_, f32[512,128]{1,0:T(8,128)S(1)} %get-tuple-element.22.refs_1_, f32[4,8,128]{2,1,0:T(8,128)S(1)} %get-tuple-element.23.refs_2_, f32[4,8,128]{2,1,0:T(8,128)S(1)} %collective-permute-done.2.refs_3_, f32[4,8,128]{2,1,0:T(8,128)S(1)} %collective-permute-done.3.refs_4_, ...), custom_call_target="tpu_custom_call" | custom-call | tf_op jit(solution)/shard_map/sweep/pallas_call | solution.py:293
  24.4 0.0 collective-permute-done.5.earlier_ref
  24.4 0.7 %jump.1 = f32[512,128]{1,0:T(8,128)} custom-call(f32[512,128]{1,0:T(8,128)S(1)} %collective-permute-done.5.earlier_ref, f32[512,128]{1,0:T(8,128)S(1)} %get-tuple-element.13.v_ref.start_ref), custom_call_target="tpu_custom_call" | custom-call | tf_op jit(solution)/shard_map/jump/pallas_call | solution.py:285
Async XLA Ops:
  2.1 5.6 %collective-permute-start.1 = (f32[192,128]{1,0:T(8,128)S(1)}, f32[192,128]{1,0:T(8,128)S(1)}, u32[]{:S(2)}, u32[]{:S(2)}) collective-permute-start(f32[192,128]{1,0:T(8,128)S(1)} %get-tuple-element.17.refs_1_), channel_id=1, source_target_pairs={{0,12},{4,0},{8,4},{12,8},{1,13},{5,1},{9,5},{13,9},{2,14},{6,2},{... | collective-permute-start | bytes 294920 | tf_op jit(solution)/shard_map/ppermute | solution.py:257
  4.5 4.2 %collective-permute-start = (f32[192,128]{1,0:T(8,128)S(1)}, f32[192,128]{1,0:T(8,128)S(1)}, u32[]{:S(2)}, u32[]{:S(2)}) collective-permute-start(f32[192,128]{1,0:T(8,128)S(1)} %get-tuple-element.18.refs_2_), channel_id=1, source_target_pairs={{0,4},{4,8},{8,12},{12,0},{1,5},{5,9},{9,13},{13,1},{2,6},{6,10},{... | collective-permute-start | bytes 294920 | tf_op jit(solution)/shard_map/ppermute | solution.py:256
  9.7 14.7 %collective-permute-start.5 = (f32[512,128]{1,0:T(8,128)S(1)}, f32[512,128]{1,0:T(8,128)S(1)}, u32[]{:S(2)}, u32[]{:S(2)}) collective-permute-start(f32[512,128]{1,0:T(8,128)S(1)} %get-tuple-element.22.refs_1_), channel_id=1, source_target_pairs={{0,1},{1,2},{2,3},{3,0},{4,5},{5,6},{6,7},{7,4},{8,9},{9,10},{10,1... | collective-permute-start | bytes 786440 | tf_op jit(solution)/shard_map/ppermute | solution.py:281
  11.2 12.2 %all-to-all-start = ((f32[16,16,128]{2,1,0:T(8,128)}), f32[16,16,128]{2,1,0:T(8,128)S(1)}, u32[]{:S(2)}, u32[]{:S(2)}) async-start(f32[16,16,128]{2,1,0:T(8,128)} %get-tuple-element.21), calls=%async_computation | async-start | bytes 262144 | tf_op jit(solution)/shard_map/all_to_all | solution.py:282
  16.1 3.1 %collective-permute-start.4 = (f32[4,8,128]{2,1,0:T(8,128)S(1)}, f32[4,8,128]{2,1,0:T(8,128)S(1)}, u32[]{:S(2)}, u32[]{:S(2)}) collective-permute-start(f32[4,8,128]{2,1,0:T(8,128)S(1)} %get-tuple-element.23.refs_2_), channel_id=1, source_target_pairs={{0,12},{4,0},{8,4},{12,8},{1,13},{5,1},{9,5},{13,9},{2,14},{6,2},{... | collective-permute-start | bytes 49160 | tf_op jit(solution)/shard_map/ppermute | solution.py:283
  17.8 3.8 %collective-permute-start.3 = (f32[4,8,128]{2,1,0:T(8,128)S(1)}, f32[4,8,128]{2,1,0:T(8,128)S(1)}, u32[]{:S(2)}, u32[]{:S(2)}) collective-permute-start(f32[4,8,128]{2,1,0:T(8,128)S(1)} %get-tuple-element.23.refs_2_), channel_id=1, source_target_pairs={{0,8},{4,12},{8,0},{12,4},{1,9},{5,13},{9,1},{13,5},{2,10},{6,14},... | collective-permute-start | bytes 49160 | tf_op jit(solution)/shard_map/ppermute | solution.py:283
  18.2 3.5 %collective-permute-start.2 = (f32[4,8,128]{2,1,0:T(8,128)S(1)}, f32[4,8,128]{2,1,0:T(8,128)S(1)}, u32[]{:S(2)}, u32[]{:S(2)}) collective-permute-start(f32[4,8,128]{2,1,0:T(8,128)S(1)} %get-tuple-element.23.refs_2_), channel_id=1, source_target_pairs={{0,4},{4,8},{8,12},{12,0},{1,5},{5,9},{9,13},{13,1},{2,6},{6,10},{... | collective-permute-start | bytes 49160 | tf_op jit(solution)/shard_map/ppermute | solution.py:283

commit v3 on v2

--- a/solution.py
+++ b/solution.py
@@ -72,17 +72,21 @@
     return ref[pl.ds(at, NZ, stride=ROWS), :]
 
 
-def edges_kernel(v_hbm, vel_hbm, d_hbm, v_ref, vel_ref, d_ref, lo_ref, hi_ref, sems):
+def edges_kernel(v_hbm, vel_hbm, d_hbm, v_ref, vel_ref, d_ref, pair_ref, cross_ref, sems):
     copies = [
         pltpu.make_async_copy(src, dst, sems.at[i])
         for i, (src, dst) in enumerate(((v_hbm, v_ref), (d_hbm, d_ref), (vel_hbm, vel_ref)))
     ]
     for copy in copies:
         copy.start()
-    for copy in copies:
+    copies[0].wait()
+    odd = lax.axis_index("space") % 2 == 1
+    image = restrict_tile(plane_sums(v_ref)) * (1.0 / 64)
+    for copy in copies[1:]:
         copy.wait()
     sub, lane = iotas((NZ, LANES))
-    for out, face, inner, side in ((lo_ref, 0, 1, 0), (hi_ref, ROWS - 1, ROWS - 2, 1)):
+    rows = []
+    for face, inner, side in ((0, 1, 0), (ROWS - 1, ROWS - 2, 1)):
         w = weights(*(row(vel_ref, d * FLAT + face) for d in range(3)), row(d_ref, face))
         v = row(v_ref, face)
         total = w[6] * v + w[3 - side] * row(v_ref, inner)
@@ -90,12 +94,15 @@
         total += jnp.where(sub == NZ - 1, 0.0, w[1]) * shifted(v, 1, 0)
         total += jnp.where(lane == 0, 0.0, w[4]) * shifted(v, -1, 1)
         total += jnp.where(lane == LANES - 1, 0.0, w[5]) * shifted(v, 1, 1)
-        out[0:NZ] = v
-        out[NZ : 2 * NZ] = total
-        out[2 * NZ : 3 * NZ] = w[2 + side]
-
-
-def steps_kernel(v_ref, vel_ref, d_ref, q_ref, coarse_ref, keep_ref, rstart_ref, p_ref, pv_ref):
+        rows.append((v, total, w[2 + side]))
+    for j, (low, high) in enumerate(zip(*rows)):
+        pair_ref[j * NZ : (j + 1) * NZ] = jnp.where(odd, low, high)
+        cross_ref[j * NZ : (j + 1) * NZ] = jnp.where(odd, high, low)
+    for ref in (pair_ref, cross_ref):
+        ref[3 * NZ : 3 * NZ + ROWS] = image
+
+
+def steps_kernel(v_ref, vel_ref, d_ref, q_ref, coarse_ref, keep_ref, p_ref, pv_ref):
     zero = jnp.zeros((ROWS, LANES), f32)
     for ref in (p_ref, pv_ref):
         ref[0:ROWS] = zero
@@ -135,24 +142,55 @@
         sums = restrict_tile(plane_sums(vel_ref.at[d * FLAT : (d + 1) * FLAT]))
         coarse_ref[d] = sums * (0.5 / 64)
     coarse_ref[3] = restrict_tile(plane_sums(d_ref)) * (0.125 / 64)
-    rstart_ref[...] = restrict_tile(plane_sums(v_ref)) * (1.0 / 64)
-
-
-def finish_kernel(parts, bricks, q_ref, lo_ref, hi_ref, fromlow_ref, fromhigh_ref, keep_ref, rstart_ref, fine_ref, tiles_ref):
-    own_brick = lax.axis_index("space")
-    has_low = own_brick > 0
-    has_high = own_brick < bricks - 1
+
+
+def coarse_weights(c, first, last):
+    sub, lane = iotas((ROWS, LANES))
+    zl, zh, y = lane % 4, sub % 4, lane // 4
+    w = weights(c[0], c[1], c[2], c[3])
+    w[0] = jnp.where((zl == 0) & (zh == 0), 0.0, w[0])
+    w[1] = jnp.where((zl == 3) & (zh == 3), 0.0, w[1])
+    w[4] = jnp.where(y == 0, 0.0, w[4])
+    w[5] = jnp.where(y == LANES // 4 - 1, 0.0, w[5])
+    w[2] = jnp.where((sub < 4) & first, 0.0, w[2])
+    w[3] = jnp.where((sub >= 4) & last, 0.0, w[3])
+    return w
+
+
+def coarse_apply(w, v, own, lower, upper):
+    sub, lane = iotas((ROWS, LANES))
+    zl = lane % 4
+    zb = jnp.where(zl == 0, shifted(shifted(v, 3, 1), -1, 0), shifted(v, -1, 1))
+    za = jnp.where(zl == 3, shifted(shifted(v, -3, 1), 1, 0), shifted(v, 1, 1))
+    xb = jnp.where(sub < 4, lower, own)
+    xa = jnp.where(sub < 4, own, upper)
+    return (
+        (w[6] * v + w[0] * zb + w[1] * za)
+        + (w[2] * xb + w[3] * xa)
+        + (w[4] * shifted(v, -4, 1) + w[5] * shifted(v, 4, 1))
+    )
+
+
+def finish_kernel(parts, bricks, q_ref, mine_pair_ref, mine_cross_ref, pair_ref, cross_ref, keep_ref, coarse_ref, fine_ref, tiles_ref, old_ref):
+    brick = lax.axis_index("space")
+    odd = brick % 2 == 1
+    has_low = brick > 0
+    has_high = brick < bricks - 1
     part = lambda ref, j: ref[j * NZ : (j + 1) * NZ]
+
+    def sides(pair, cross, j):
+        a, b = part(pair, j), part(cross, j)
+        return jnp.where(odd, a, b), jnp.where(odd, b, a)
+
+    own = [sides(mine_pair_ref, mine_cross_ref, j) for j in (0, 2)]
+    far = [sides(pair_ref, cross_ref, j) for j in range(3)]
     sub, lane = iotas((NZ, LANES))
     fine_ref[...] = q_ref[...]
     for side in range(2):
-        far, own, there = (
-            (fromlow_ref, lo_ref, has_low) if side == 0 else (fromhigh_ref, hi_ref, has_high)
-        )
         wbz, waz, wby, way, centre, inner = (part(keep_ref, side * 6 + j) for j in range(6))
-        k = jnp.where(there, part(own, 2), 0.0)
-        delta = k * part(far, 0)
-        beyond = part(far, 1) + part(far, 2) * part(own, 0)
+        k = jnp.where(has_high if side else has_low, own[1][side], 0.0)
+        delta = k * far[0][side]
+        beyond = far[1][side] + far[2][side] * own[0][side]
         edge = centre * delta + k * beyond
         edge += jnp.where(sub == 0, 0.0, wbz) * shifted(delta, -1, 0)
         edge += jnp.where(sub == NZ - 1, 0.0, waz) * shifted(delta, 1, 0)
@@ -161,11 +199,17 @@
         e_at, i_at = (0, 1) if side == 0 else (ROWS - 1, ROWS - 2)
         fine_ref[pl.ds(e_at, NZ, stride=ROWS), :] = row(q_ref, e_at) + edge
         fine_ref[pl.ds(i_at, NZ, stride=ROWS), :] = row(q_ref, i_at) + inner * delta
-    tile = restrict_tile(plane_sums(fine_ref)) * (1.0 / 64)
-    rstart = rstart_ref[...]
+    at = slice(3 * NZ, 3 * NZ + ROWS)
+    v = mine_pair_ref[at]
+    lower = jnp.where(odd, pair_ref[at], cross_ref[at])
+    upper = jnp.where(odd, cross_ref[at], pair_ref[at])
+    w = coarse_weights(coarse_ref, jnp.logical_not(has_low), jnp.logical_not(has_high))
+    old = coarse_apply(w, v, *(shifted(x, 4, 0) for x in (v, lower, upper)))
+    old_ref[...] = old
+    image = restrict_tile(plane_sums(fine_ref)) * (1.0 / 64)
+    tile = jnp.where(lax.axis_index("tm") == 0, image, image - old)
     for j in range(parts):
-        tiles_ref[j, 0:ROWS] = tile
-        tiles_ref[j, ROWS : 2 * ROWS] = rstart
+        tiles_ref[j] = tile
 
 
 def jump_kernel(earlier_ref, start_ref, jump_ref):
@@ -173,55 +217,28 @@
     jump_ref[...] = jnp.where(first, 0.0, start_ref[...] - earlier_ref[...])
 
 
-def sweep_kernel(bricks, slices, images_ref, fine_ref, *refs):
+def sweep_kernel(bricks, slices, tiles_ref, fine_ref, old_ref, *refs):
     coarse_refs = refs[:bricks]
     corrected_ref, change_ref, coef_ref = refs[bricks:]
     own, n = lax.axis_index("space"), lax.axis_index("tm")
     for k in range(bricks):
         coef_ref[(own + bricks - k) % bricks] = coarse_refs[k][...]
-    sub, lane = iotas((ROWS, LANES))
-    zl, zh, y = lane % 4, sub % 4, lane // 4
-    w = []
+    w = [coarse_weights(coef_ref.at[b], b == 0, b == bricks - 1) for b in range(bricks)]
+
+    def coarse_step(m, image):
+        c = [image[b] + tiles_ref[b * slices + m] for b in range(bricks)]
+        half = [shifted(v, 4, 0) for v in c]
+        return tuple(
+            coarse_apply(w[b], c[b], half[b], half[max(b - 1, 0)], half[min(b + 1, bricks - 1)])
+            for b in range(bricks)
+        )
+
+    zero = tuple(jnp.zeros((ROWS, LANES), f32) for _ in range(bricks))
+    image = lax.fori_loop(0, n, coarse_step, zero)
     for b in range(bricks):
-        c = coef_ref.at[b]
-        wb = weights(c[0], c[1], c[2], c[3])
-        wb[0] = jnp.where((zl == 0) & (zh == 0), 0.0, wb[0])
-        wb[1] = jnp.where((zl == 3) & (zh == 3), 0.0, wb[1])
-        wb[4] = jnp.where(y == 0, 0.0, wb[4])
-        wb[5] = jnp.where(y == LANES // 4 - 1, 0.0, wb[5])
-        if b == 0:
-            wb[2] = jnp.where(sub < 4, 0.0, wb[2])
-        if b == bricks - 1:
-            wb[3] = jnp.where(sub < 4, wb[3], 0.0)
-        w.append(wb)
-
-    def coarse_step(m, change):
-        e = [
-            change[b] + (images_ref[b * slices + m, 0:ROWS] - images_ref[b * slices + m + 1, ROWS : 2 * ROWS])
-            for b in range(bricks)
-        ]
-        half = [shifted(v, 4, 0) for v in e]
-        out = []
-        for b in range(bricks):
-            v = e[b]
-            lower = half[max(b - 1, 0)]
-            upper = half[min(b + 1, bricks - 1)]
-            zb = jnp.where(zl == 0, shifted(shifted(v, 3, 1), -1, 0), shifted(v, -1, 1))
-            za = jnp.where(zl == 3, shifted(shifted(v, -3, 1), 1, 0), shifted(v, 1, 1))
-            xb = jnp.where(sub < 4, lower, half[b])
-            xa = jnp.where(sub < 4, half[b], upper)
-            out.append(
-                (w[b][6] * v + w[b][0] * zb + w[b][1] * za)
-                + (w[b][2] * xb + w[b][3] * xa)
-                + (w[b][4] * shifted(v, -4, 1) + w[b][5] * shifted(v, 4, 1))
-            )
-        return tuple(out)
-
-    zero = tuple(jnp.zeros((ROWS, LANES), f32) for _ in range(bricks))
-    change = lax.fori_loop(0, n, coarse_step, zero)
-    for b in range(bricks):
-        change_ref[b] = change[b]
-    planes = prolong_tile(change_ref[own])
+        change_ref[b] = image[b]
+    change = jnp.where(n == 0, 0.0, change_ref[own] - old_ref[...])
+    planes = prolong_tile(change)
     for z in range(NZ):
         at = slice(z * ROWS, (z + 1) * ROWS)
         corrected_ref[at] = fine_ref[at] + planes[z // 4]
@@ -235,7 +252,7 @@
     vmem, anyspace = pl.BlockSpec(memory_space=pltpu.VMEM), pl.BlockSpec(memory_space=pl.ANY)
     inside = lambda *xs: [pltpu.with_memory_space_constraint(x, pltpu.VMEM) for x in xs]
 
-    v, vel, diff, lo, hi = pl.pallas_call(
+    v, vel, diff, mine_pair, mine_cross = pl.pallas_call(
         edges_kernel,
         in_specs=[anyspace] * 3,
         out_specs=[vmem] * 5,
@@ -243,8 +260,8 @@
             out(FLAT, LANES),
             out(3 * FLAT, LANES),
             out(FLAT, LANES),
-            out(3 * NZ, LANES),
-            out(3 * NZ, LANES),
+            out(3 * NZ + ROWS, LANES),
+            out(3 * NZ + ROWS, LANES),
         ],
         scratch_shapes=[pltpu.SemaphoreType.DMA((3,))],
         name="edges",
@@ -253,33 +270,29 @@
         velocity.reshape(3 * FLAT, LANES),
         diffusivity.reshape(FLAT, LANES),
     )
-    fromlow = lax.ppermute(hi, "space", ring(bricks, 1))
-    fromhigh = lax.ppermute(lo, "space", ring(bricks, bricks - 1))
-
-    q, coarse, keep, rstart = pl.pallas_call(
+    pair = lax.ppermute(mine_pair, "space", [(i, i ^ 1) for i in range(bricks)])
+    across = [(i, min(max(((i + 1) ^ 1) - 1, 0), bricks - 1)) for i in range(bricks)]
+    cross = lax.ppermute(mine_cross, "space", across)
+
+    q, coarse, keep = pl.pallas_call(
         steps_kernel,
         in_specs=[vmem] * 3,
-        out_specs=[vmem] * 4,
-        out_shape=[
-            out(FLAT, LANES),
-            out(4, ROWS, LANES),
-            out(12 * NZ, LANES),
-            out(ROWS, LANES),
-        ],
+        out_specs=[vmem] * 3,
+        out_shape=[out(FLAT, LANES), out(4, ROWS, LANES), out(12 * NZ, LANES)],
         scratch_shapes=[pltpu.VMEM((FLAT + 2 * ROWS, LANES), f32)] * 2,
         name="steps",
     )(*inside(v, vel, diff))
 
-    fine, tiles = pl.pallas_call(
+    fine, tiles, old = pl.pallas_call(
         lambda *refs: finish_kernel(parts, bricks, *refs),
         in_specs=[vmem] * 7,
-        out_specs=[vmem] * 2,
-        out_shape=[out(FLAT, LANES), out(parts, 2 * ROWS, LANES)],
+        out_specs=[vmem] * 3,
+        out_shape=[out(FLAT, LANES), out(parts, ROWS, LANES), out(ROWS, LANES)],
         name="finish",
-    )(*inside(q, lo, hi, fromlow, fromhigh, keep, rstart))
+    )(*inside(q, mine_pair, mine_cross, pair, cross, keep, coarse))
 
     earlier = lax.ppermute(fine, "tm", ring(slices, 1))
-    images = lax.all_to_all(tiles, ("space", "tm"), 0, 0)
+    defects = lax.all_to_all(tiles, ("space", "tm"), 0, 0)
     coarse_all = [coarse] + [lax.ppermute(coarse, "space", ring(bricks, k)) for k in range(1, bricks)]
 
     jump = pl.pallas_call(
@@ -289,10 +302,11 @@
         out_shape=jax.ShapeDtypeStruct((FLAT, LANES), f32),
         name="jump",
     )(*inside(earlier, v))
+    defects, jump = lax.optimization_barrier((defects, jump))
 
     corrected = pl.pallas_call(
         lambda *refs: sweep_kernel(bricks, slices, *refs),
-        in_specs=[vmem] * (bricks + 2),
+        in_specs=[vmem] * (bricks + 3),
         out_specs=vmem,
         out_shape=jax.ShapeDtypeStruct((FLAT, LANES), f32),
         scratch_shapes=[
@@ -300,7 +314,7 @@
             pltpu.VMEM((bricks, 4, ROWS, LANES), f32),
         ],
         name="sweep",
-    )(*inside(images, fine, *coarse_all))
+    )(*inside(defects, fine, old, *coarse_all))
     shape = (1, NZ, ROWS, LANES)
     return corrected.reshape(shape), jump.reshape(shape)
 

time: 25.4 us -> 24.8 us (0.976)
  waiting for transfers between devices: 7.64 us -> 3.72 us
  starting transfers between devices: 11.1 us -> 14.5 us
    all_to_all x1, starting transfers between devices: 4.87 us -> 8.5 us  [local(): defects = lax.all_to_all(tiles, ('space', 'tm'), 0, 0)]
    ppermute x3, waiting for transfers between devices: 3.33 us -> 0.01 us  [local(): lax.ppermute(coarse, 'space', ring(bricks, k))]
    ppermute x2, waiting for transfers between devices: 2.48 us -> 0.01 us  [the longest x1 0.01 us: local(): pair = lax.ppermute(mine_pair, 'space', [(i, i ^ 1) for i in range(bricks)])]
    all_to_all x1, waiting for transfers between devices: 1.83 us -> 3.7 us  [local(): defects = lax.all_to_all(tiles, ('space', 'tm'), 0, 0)]
    ppermute x2, starting transfers between devices: 2.43 us -> 1.17 us  [the longest x1 0.66 us: local(): cross = lax.ppermute(mine_cross, 'space', across)]
    ppermute x1, starting transfers between devices: 1.58 us -> 2.6 us  [local(): earlier = lax.ppermute(fine, 'tm', ring(slices, 1))]
  transfers between devices with their start and end apart: 7 -> 7, of which waited for: 5 -> 1; matrix products, arithmetic and copies ran while one was open for 0% -> 0% of each run, Pallas kernels for 10% -> 10%
where the time goes in v3:
time: 24.8 us; the launch traced here: 24.6 us
  starting transfers between devices  14.5 us (58%)
  Pallas kernels  5.7 us (23%)
  waiting for transfers between devices  3.72 us (15%)
  between operations  0.69 us (3%)
    all_to_all x1, starting transfers between devices, local(): defects = lax.all_to_all(tiles, ('space', 'tm'), 0, 0)  8.5 us
    all_to_all x1, waiting for transfers between devices, local(): defects = lax.all_to_all(tiles, ('space', 'tm'), 0, 0)  3.7 us
    ppermute x1, starting transfers between devices, local(): earlier = lax.ppermute(fine, 'tm', ring(slices, 1))  2.6 us
    ppermute x3, starting transfers between devices, local(): lax.ppermute(coarse, 'space', ring(bricks, k))  2.19 us
    pallas_call x1, Pallas kernels, local(): pl.pallas_call(steps_kernel, in_specs=[vmem] * 3, out_specs=[vmem] * 3, o...  1.68 us
    pallas_call x1, Pallas kernels, local(): pl.pallas_call(edges_kernel, in_specs=[anyspace] * 3, out_specs=[vmem] *...  1.44 us
    pallas_call x1, Pallas kernels, local(): pl.pallas_call(lambda *refs: finish_kernel(parts, bricks, *refs), in_spec...  0.94 us
    pallas_call x1, Pallas kernels, local(): pl.pallas_call(lambda *refs: sweep_kernel(bricks, slices, *refs), in_spec...  0.91 us
  transfers between devices with their start and end apart: 7, of which 1 were waited for; matrix products, arithmetic and copies ran while one was open for 0% of the time, Pallas kernels for 10%

profile of v3, /device:TPU:0, one launch (start us, length us, event | category | flops | bytes accessed | tf_op | source)
XLA Modules:
  0.0 24.6 jit_solution(16563759417969042502)
XLA Ops:
  0.6 1.4 %edges.1 = (f32[512,128]{1,0:T(8,128)S(1)}, f32[1536,128]{1,0:T(8,128)S(1)}, f32[512,128]{1,0:T(8,128)S(1)}, f32[200,128]{1,0:T(8,128)S(1)}, f32[200,128]{1,0:T(8,128)S(1)}) custom-call(f32[512,128]{1,0:T(8,128)} %bitcast.6, f32[1536,128]{1,0:T(8,128)} %bitcast.5, f32[512,128]{1,0:T(8,128)} %bitcast.7), custom_call_target="tpu_custom_call" | custom-call | tf_op jit(solution)/shard_map/edges/pallas_call | solution.py:255
  2.1 0.5 %collective-permute-start = (f32[200,128]{1,0:T(8,128)S(1)}, f32[200,128]{1,0:T(8,128)S(1)}, u32[]{:S(2)}, u32[]{:S(2)}) collective-permute-start(f32[200,128]{1,0:T(8,128)S(1)} %get-tuple-element.19.refs_1_), channel_id=1, source_target_pairs={{0,4},{4,0},{8,12},{12,8},{1,5},{5,1},{9,13},{13,9},{2,6},{6,2},{1... | collective-permute-start | bytes 307208 | tf_op jit(solution)/shard_map/ppermute | solution.py:273
  2.6 0.7 %collective-permute-start.1 = (f32[200,128]{1,0:T(8,128)S(1)}, f32[200,128]{1,0:T(8,128)S(1)}, u32[]{:S(2)}, u32[]{:S(2)}) collective-permute-start(f32[200,128]{1,0:T(8,128)S(1)} %get-tuple-element.20.refs_2_), channel_id=1, source_target_pairs={{0,0},{4,8},{8,4},{12,12},{1,1},{5,9},{9,5},{13,13},{2,2},{6,10},{... | collective-permute-start | bytes 307208 | tf_op jit(solution)/shard_map/ppermute | solution.py:275
  3.3 1.7 %steps.1 = (f32[512,128]{1,0:T(8,128)S(1)}, f32[4,8,128]{2,1,0:T(8,128)S(1)}, f32[768,128]{1,0:T(8,128)S(1)}) custom-call(f32[512,128]{1,0:T(8,128)S(1)} %get-tuple-element.15.v_ref.start_ref, f32[1536,128]{1,0:T(8,128)S(1)} %get-tuple-element.16.vel_ref, f32[512,128]{1,0:T(8,128)S(1)} %get-tuple-element.17.d_ref), custom_call_target="tpu_custom_call" | custom-call | tf_op jit(solution)/shard_map/steps/pallas_call | solution.py:277
  4.9 0.0 collective-permute-done.refs_3_
  4.9 0.0 collective-permute-done.1.refs_4_
  5.0 0.9 %finish.1 = (f32[512,128]{1,0:T(8,128)S(1)}, f32[16,8,128]{2,1,0:T(8,128)}, f32[8,128]{1,0:T(8,128)S(1)}) custom-call(f32[512,128]{1,0:T(8,128)S(1)} %get-tuple-element.18.refs_0_, f32[200,128]{1,0:T(8,128)S(1)} %get-tuple-element.19.refs_1_, f32[200,128]{1,0:T(8,128)S(1)} %get-tuple-element.20.refs_2_, f32[200,128]{1,0:T(8,128)S(1)} %collective-permute-done.refs_3_, ...), custom_call_target="tpu_custom_call" | custom-call | tf_op jit(solution)/shard_map/finish/pallas_call | solution.py:286
  5.9 2.6 %collective-permute-start.2 = (f32[512,128]{1,0:T(8,128)S(1)}, f32[512,128]{1,0:T(8,128)S(1)}, u32[]{:S(2)}, u32[]{:S(2)}) collective-permute-start(f32[512,128]{1,0:T(8,128)S(1)} %get-tuple-element.24.refs_1_), channel_id=1, source_target_pairs={{0,1},{1,2},{2,3},{3,0},{4,5},{5,6},{6,7},{7,4},{8,9},{9,10},{10,1... | collective-permute-start | bytes 786440 | tf_op jit(solution)/shard_map/ppermute | solution.py:294
  8.5 8.5 %all-to-all-start = ((f32[16,8,128]{2,1,0:T(8,128)}), f32[16,8,128]{2,1,0:T(8,128)S(1)}, u32[]{:S(2)}, u32[]{:S(2)}) async-start(f32[16,8,128]{2,1,0:T(8,128)} %get-tuple-element.23), calls=%async_computation | async-start | bytes 131072 | tf_op jit(solution)/shard_map/all_to_all | solution.py:295
  17.0 1.7 %collective-permute-start.5 = (f32[4,8,128]{2,1,0:T(8,128)S(1)}, f32[4,8,128]{2,1,0:T(8,128)S(1)}, u32[]{:S(2)}, u32[]{:S(2)}) collective-permute-start(f32[4,8,128]{2,1,0:T(8,128)S(1)} %get-tuple-element.22.refs_6_.refs_3_), channel_id=1, source_target_pairs={{0,12},{4,0},{8,4},{12,8},{1,13},{5,1},{9,5},{13,9},{2,14},{6,2},{... | collective-permute-start | bytes 49160 | tf_op jit(solution)/shard_map/ppermute | solution.py:296
  18.7 0.4 %collective-permute-start.4 = (f32[4,8,128]{2,1,0:T(8,128)S(1)}, f32[4,8,128]{2,1,0:T(8,128)S(1)}, u32[]{:S(2)}, u32[]{:S(2)}) collective-permute-start(f32[4,8,128]{2,1,0:T(8,128)S(1)} %get-tuple-element.22.refs_6_.refs_3_), channel_id=1, source_target_pairs={{0,8},{4,12},{8,0},{12,4},{1,9},{5,13},{9,1},{13,5},{2,10},{6,14},... | collective-permute-start | bytes 49160 | tf_op jit(solution)/shard_map/ppermute | solution.py:296
  19.0 0.1 collective-permute-start.3
  19.2 0.0 collective-permute-done.2.earlier_ref
  19.2 0.7 %jump.1 = f32[512,128]{1,0:T(8,128)} custom-call(f32[512,128]{1,0:T(8,128)S(1)} %collective-permute-done.2.earlier_ref, f32[512,128]{1,0:T(8,128)S(1)} %get-tuple-element.15.v_ref.start_ref), custom_call_target="tpu_custom_call" | custom-call | tf_op jit(solution)/shard_map/jump/pallas_call | solution.py:298
  19.9 3.7 %all-to-all-done.refs_0_ = f32[16,8,128]{2,1,0:T(8,128)S(1)} async-done(((f32[16,8,128]{2,1,0:T(8,128)}), f32[16,8,128]{2,1,0:T(8,128)S(1)}, u32[]{:S(2)}, u32[]{:S(2)}) %all-to-all-start) | async-done | bytes 65568 | tf_op jit(solution)/shard_map/all_to_all | solution.py:295
  23.6 0.0 collective-permute-done.5.refs_6_
  23.6 0.0 collective-permute-done.4.refs_5_
  23.6 0.0 collective-permute-done.3.refs_4_
  23.6 0.9 %sweep.1 = f32[512,128]{1,0:T(8,128)} custom-call(f32[16,8,128]{2,1,0:T(8,128)S(1)} %all-to-all-done.refs_0_, f32[512,128]{1,0:T(8,128)S(1)} %get-tuple-element.24.refs_1_, f32[8,128]{1,0:T(8,128)S(1)} %get-tuple-element.26.refs_2_, f32[4,8,128]{2,1,0:T(8,128)S(1)} %get-tuple-element.22.refs_6_.refs_3_, f32[4,8,128]{2,1,0:T(8,128)S(1)} %collective-permute-done.3.refs_4_, ...), custom_call_target="tpu_custom_call" | custom-call | tf_op jit(solution)/shard_map/sweep/pallas_call | solution.py:307
Async XLA Ops:
  2.1 2.9 %collective-permute-start = (f32[200,128]{1,0:T(8,128)S(1)}, f32[200,128]{1,0:T(8,128)S(1)}, u32[]{:S(2)}, u32[]{:S(2)}) collective-permute-start(f32[200,128]{1,0:T(8,128)S(1)} %get-tuple-element.19.refs_1_), channel_id=1, source_target_pairs={{0,4},{4,0},{8,12},{12,8},{1,5},{5,1},{9,13},{13,9},{2,6},{6,2},{1... | collective-permute-start | bytes 307208 | tf_op jit(solution)/shard_map/ppermute | solution.py:273
  2.6 2.4 %collective-permute-start.1 = (f32[200,128]{1,0:T(8,128)S(1)}, f32[200,128]{1,0:T(8,128)S(1)}, u32[]{:S(2)}, u32[]{:S(2)}) collective-permute-start(f32[200,128]{1,0:T(8,128)S(1)} %get-tuple-element.20.refs_2_), channel_id=1, source_target_pairs={{0,0},{4,8},{8,4},{12,12},{1,1},{5,9},{9,5},{13,13},{2,2},{6,10},{... | collective-permute-start | bytes 307208 | tf_op jit(solution)/shard_map/ppermute | solution.py:275
  5.9 13.3 %collective-permute-start.2 = (f32[512,128]{1,0:T(8,128)S(1)}, f32[512,128]{1,0:T(8,128)S(1)}, u32[]{:S(2)}, u32[]{:S(2)}) collective-permute-start(f32[512,128]{1,0:T(8,128)S(1)} %get-tuple-element.24.refs_1_), channel_id=1, source_target_pairs={{0,1},{1,2},{2,3},{3,0},{4,5},{5,6},{6,7},{7,4},{8,9},{9,10},{10,1... | collective-permute-start | bytes 786440 | tf_op jit(solution)/shard_map/ppermute | solution.py:294
  8.5 15.1 %all-to-all-start = ((f32[16,8,128]{2,1,0:T(8,128)}), f32[16,8,128]{2,1,0:T(8,128)S(1)}, u32[]{:S(2)}, u32[]{:S(2)}) async-start(f32[16,8,128]{2,1,0:T(8,128)} %get-tuple-element.23), calls=%async_computation | async-start | bytes 131072 | tf_op jit(solution)/shard_map/all_to_all | solution.py:295
  17.0 6.6 %collective-permute-start.5 = (f32[4,8,128]{2,1,0:T(8,128)S(1)}, f32[4,8,128]{2,1,0:T(8,128)S(1)}, u32[]{:S(2)}, u32[]{:S(2)}) collective-permute-start(f32[4,8,128]{2,1,0:T(8,128)S(1)} %get-tuple-element.22.refs_6_.refs_3_), channel_id=1, source_target_pairs={{0,12},{4,0},{8,4},{12,8},{1,13},{5,1},{9,5},{13,9},{2,14},{6,2},{... | collective-permute-start | bytes 49160 | tf_op jit(solution)/shard_map/ppermute | solution.py:296
  18.7 5.0 %collective-permute-start.4 = (f32[4,8,128]{2,1,0:T(8,128)S(1)}, f32[4,8,128]{2,1,0:T(8,128)S(1)}, u32[]{:S(2)}, u32[]{:S(2)}) collective-permute-start(f32[4,8,128]{2,1,0:T(8,128)S(1)} %get-tuple-element.22.refs_6_.refs_3_), channel_id=1, source_target_pairs={{0,8},{4,12},{8,0},{12,4},{1,9},{5,13},{9,1},{13,5},{2,10},{6,14},... | collective-permute-start | bytes 49160 | tf_op jit(solution)/shard_map/ppermute | solution.py:296
  19.0 4.6 %collective-permute-start.3 = (f32[4,8,128]{2,1,0:T(8,128)S(1)}, f32[4,8,128]{2,1,0:T(8,128)S(1)}, u32[]{:S(2)}, u32[]{:S(2)}) collective-permute-start(f32[4,8,128]{2,1,0:T(8,128)S(1)} %get-tuple-element.22.refs_6_.refs_3_), channel_id=1, source_target_pairs={{0,4},{4,8},{8,12},{12,0},{1,5},{5,9},{9,13},{13,1},{2,6},{6,10},{... | collective-permute-start | bytes 49160 | tf_op jit(solution)/shard_map/ppermute | solution.py:296

commit v4 on v3

--- a/solution.py
+++ b/solution.py
@@ -8,6 +8,7 @@
 NZ, ROWS, LANES = 64, 8, 128
 FLAT = NZ * ROWS
 CHUNK = 8
+EDGE = 3 * NZ + ROWS
 BITS = ((1, 1), (1, 2), (0, 1), (0, 2))
 
 f32 = jnp.float32
@@ -73,17 +74,27 @@
 
 
 def edges_kernel(v_hbm, vel_hbm, d_hbm, v_ref, vel_ref, d_ref, pair_ref, cross_ref, sems):
-    copies = [
-        pltpu.make_async_copy(src, dst, sems.at[i])
-        for i, (src, dst) in enumerate(((v_hbm, v_ref), (d_hbm, d_ref), (vel_hbm, vel_ref)))
-    ]
+    copies = [pltpu.make_async_copy(v_hbm, v_ref, sems.at[0])]
+    for d in range(3):
+        at = pl.ds(d * FLAT, FLAT)
+        copies.append(pltpu.make_async_copy(vel_hbm.at[at], vel_ref.at[at], sems.at[1 + d]))
+    copies.append(pltpu.make_async_copy(d_hbm, d_ref, sems.at[4]))
     for copy in copies:
         copy.start()
-    copies[0].wait()
     odd = lax.axis_index("space") % 2 == 1
-    image = restrict_tile(plane_sums(v_ref)) * (1.0 / 64)
-    for copy in copies[1:]:
+    fields = (
+        (v_ref, 1.0),
+        (vel_ref.at[0:FLAT], 0.5),
+        (vel_ref.at[FLAT : 2 * FLAT], 0.5),
+        (vel_ref.at[2 * FLAT : 3 * FLAT], 0.5),
+        (d_ref, 0.125),
+    )
+    for j, (copy, (ref, factor)) in enumerate(zip(copies, fields)):
         copy.wait()
+        tile = restrict_tile(plane_sums(ref)) * (factor / 64)
+        pair_ref[3 * NZ + j * ROWS : 3 * NZ + (j + 1) * ROWS] = tile
+        if j == 0:
+            cross_ref[3 * NZ : EDGE] = tile
     sub, lane = iotas((NZ, LANES))
     rows = []
     for face, inner, side in ((0, 1, 0), (ROWS - 1, ROWS - 2, 1)):
@@ -98,11 +109,9 @@
     for j, (low, high) in enumerate(zip(*rows)):
         pair_ref[j * NZ : (j + 1) * NZ] = jnp.where(odd, low, high)
         cross_ref[j * NZ : (j + 1) * NZ] = jnp.where(odd, high, low)
-    for ref in (pair_ref, cross_ref):
-        ref[3 * NZ : 3 * NZ + ROWS] = image
-
-
-def steps_kernel(v_ref, vel_ref, d_ref, q_ref, coarse_ref, keep_ref, p_ref, pv_ref):
+
+
+def steps_kernel(v_ref, vel_ref, d_ref, q_ref, keep_ref, p_ref, pv_ref):
     zero = jnp.zeros((ROWS, LANES), f32)
     for ref in (p_ref, pv_ref):
         ref[0:ROWS] = zero
@@ -138,10 +147,6 @@
             keep_ref[(side * 6 + j) * NZ : (side * 6 + j + 1) * NZ] = value
     keep_ref[5 * NZ : 6 * NZ] = row(d_ref, 1) + jnp.maximum(row(vel_ref, FLAT + 1), 0.0)
     keep_ref[11 * NZ : 12 * NZ] = row(d_ref, ROWS - 2) - jnp.minimum(row(vel_ref, FLAT + ROWS - 2), 0.0)
-    for d in range(3):
-        sums = restrict_tile(plane_sums(vel_ref.at[d * FLAT : (d + 1) * FLAT]))
-        coarse_ref[d] = sums * (0.5 / 64)
-    coarse_ref[3] = restrict_tile(plane_sums(d_ref)) * (0.125 / 64)
 
 
 def coarse_weights(c, first, last):
@@ -171,7 +176,7 @@
     )
 
 
-def finish_kernel(parts, bricks, q_ref, mine_pair_ref, mine_cross_ref, pair_ref, cross_ref, keep_ref, coarse_ref, fine_ref, tiles_ref, old_ref):
+def finish_kernel(parts, bricks, q_ref, mine_pair_ref, mine_cross_ref, pair_ref, cross_ref, keep_ref, fine_ref, tiles_ref, old_ref, both_ref):
     brick = lax.axis_index("space")
     odd = brick % 2 == 1
     has_low = brick > 0
@@ -199,11 +204,14 @@
         e_at, i_at = (0, 1) if side == 0 else (ROWS - 1, ROWS - 2)
         fine_ref[pl.ds(e_at, NZ, stride=ROWS), :] = row(q_ref, e_at) + edge
         fine_ref[pl.ds(i_at, NZ, stride=ROWS), :] = row(q_ref, i_at) + inner * delta
-    at = slice(3 * NZ, 3 * NZ + ROWS)
+    at = slice(3 * NZ, EDGE)
     v = mine_pair_ref[at]
     lower = jnp.where(odd, pair_ref[at], cross_ref[at])
     upper = jnp.where(odd, cross_ref[at], pair_ref[at])
-    w = coarse_weights(coarse_ref, jnp.logical_not(has_low), jnp.logical_not(has_high))
+    mine, other = mine_pair_ref[EDGE:], pair_ref[EDGE:]
+    both_ref[0] = jnp.where(odd, other, mine)
+    both_ref[1] = jnp.where(odd, mine, other)
+    w = coarse_weights(mine.reshape(4, ROWS, LANES), jnp.logical_not(has_low), jnp.logical_not(has_high))
     old = coarse_apply(w, v, *(shifted(x, 4, 0) for x in (v, lower, upper)))
     old_ref[...] = old
     image = restrict_tile(plane_sums(fine_ref)) * (1.0 / 64)
@@ -213,17 +221,20 @@
 
 
 def jump_kernel(earlier_ref, start_ref, jump_ref):
-    first = lax.axis_index("tm") == 0
-    jump_ref[...] = jnp.where(first, 0.0, start_ref[...] - earlier_ref[...])
+    keep = jnp.where(lax.axis_index("tm") == 0, 0.0, 1.0)
+    jump_ref[...] = keep * (start_ref[...] - earlier_ref[...])
 
 
 def sweep_kernel(bricks, slices, tiles_ref, fine_ref, old_ref, *refs):
-    coarse_refs = refs[:bricks]
-    corrected_ref, change_ref, coef_ref = refs[bricks:]
+    coarse_refs = refs[: bricks // 2]
+    corrected_ref, change_ref, coef_ref = refs[bricks // 2 :]
     own, n = lax.axis_index("space"), lax.axis_index("tm")
-    for k in range(bricks):
-        coef_ref[(own + bricks - k) % bricks] = coarse_refs[k][...]
-    w = [coarse_weights(coef_ref.at[b], b == 0, b == bricks - 1) for b in range(bricks)]
+    for k, ref in enumerate(coarse_refs):
+        coef_ref[(own // 2 + bricks // 2 - k) % (bricks // 2)] = ref[...]
+    w = [
+        coarse_weights(coef_ref[b // 2, b % 2].reshape(4, ROWS, LANES), b == 0, b == bricks - 1)
+        for b in range(bricks)
+    ]
 
     def coarse_step(m, image):
         c = [image[b] + tiles_ref[b * slices + m] for b in range(bricks)]
@@ -246,7 +257,7 @@
 
 def local(start_states, velocity, diffusivity):
     bricks, slices = lax.axis_size("space"), lax.axis_size("tm")
-    parts = bricks * slices
+    groups, parts = lax.axis_size("groups"), bricks * slices
     ring = lambda count, by: [(i, (i + by) % count) for i in range(count)]
     out = lambda *shape: pltpu.VMEM(shape, f32)
     vmem, anyspace = pl.BlockSpec(memory_space=pltpu.VMEM), pl.BlockSpec(memory_space=pl.ANY)
@@ -260,40 +271,53 @@
             out(FLAT, LANES),
             out(3 * FLAT, LANES),
             out(FLAT, LANES),
-            out(3 * NZ + ROWS, LANES),
-            out(3 * NZ + ROWS, LANES),
+            out(EDGE + 4 * ROWS, LANES),
+            out(EDGE, LANES),
         ],
-        scratch_shapes=[pltpu.SemaphoreType.DMA((3,))],
+        scratch_shapes=[pltpu.SemaphoreType.DMA((5,))],
         name="edges",
     )(
         start_states.reshape(FLAT, LANES),
         velocity.reshape(3 * FLAT, LANES),
         diffusivity.reshape(FLAT, LANES),
     )
+    partner = {}
+    for g in range(groups):
+        for i in range(bricks):
+            j, h = i + 1 if i % 2 else i - 1, g
+            if j < 0 or j >= bricks:
+                j, h = (i, g ^ 1) if groups % 2 == 0 else (j % bricks, g)
+            partner[g * bricks + i] = h * bricks + j
+    cross = lax.ppermute(mine_cross, ("groups", "space"), list(partner.items()))
+
     pair = lax.ppermute(mine_pair, "space", [(i, i ^ 1) for i in range(bricks)])
-    across = [(i, min(max(((i + 1) ^ 1) - 1, 0), bricks - 1)) for i in range(bricks)]
-    cross = lax.ppermute(mine_cross, "space", across)
-
-    q, coarse, keep = pl.pallas_call(
+
+    q, keep = pl.pallas_call(
         steps_kernel,
         in_specs=[vmem] * 3,
-        out_specs=[vmem] * 3,
-        out_shape=[out(FLAT, LANES), out(4, ROWS, LANES), out(12 * NZ, LANES)],
+        out_specs=[vmem] * 2,
+        out_shape=[out(FLAT, LANES), out(12 * NZ, LANES)],
         scratch_shapes=[pltpu.VMEM((FLAT + 2 * ROWS, LANES), f32)] * 2,
         name="steps",
     )(*inside(v, vel, diff))
-
-    fine, tiles, old = pl.pallas_call(
+    fine, tiles, old, both = pl.pallas_call(
         lambda *refs: finish_kernel(parts, bricks, *refs),
-        in_specs=[vmem] * 7,
-        out_specs=[vmem] * 3,
-        out_shape=[out(FLAT, LANES), out(parts, ROWS, LANES), out(ROWS, LANES)],
+        in_specs=[vmem] * 6,
+        out_specs=[vmem] * 4,
+        out_shape=[
+            out(FLAT, LANES),
+            out(parts, ROWS, LANES),
+            out(ROWS, LANES),
+            out(2, 4 * ROWS, LANES),
+        ],
         name="finish",
-    )(*inside(q, mine_pair, mine_cross, pair, cross, keep, coarse))
+    )(*inside(q, mine_pair, mine_cross, pair, cross, keep))
 
     earlier = lax.ppermute(fine, "tm", ring(slices, 1))
     defects = lax.all_to_all(tiles, ("space", "tm"), 0, 0)
-    coarse_all = [coarse] + [lax.ppermute(coarse, "space", ring(bricks, k)) for k in range(1, bricks)]
+    coarse_all = [both] + [
+        lax.ppermute(both, "space", ring(bricks, k)) for k in range(2, bricks, 2)
+    ]
 
     jump = pl.pallas_call(
         jump_kernel,
@@ -306,12 +330,12 @@
 
     corrected = pl.pallas_call(
         lambda *refs: sweep_kernel(bricks, slices, *refs),
-        in_specs=[vmem] * (bricks + 3),
+        in_specs=[vmem] * (bricks // 2 + 3),
         out_specs=vmem,
         out_shape=jax.ShapeDtypeStruct((FLAT, LANES), f32),
         scratch_shapes=[
             pltpu.VMEM((bricks, ROWS, LANES), f32),
-            pltpu.VMEM((bricks, 4, ROWS, LANES), f32),
+            pltpu.VMEM((bricks // 2, 2, 4 * ROWS, LANES), f32),
         ],
         name="sweep",
     )(*inside(defects, fine, old, *coarse_all))

time: 24.8 us -> 23.3 us (0.940)
  starting transfers between devices: 14.5 us -> 11.4 us
  waiting for transfers between devices: 3.72 us -> 5.11 us
    all_to_all x1, starting transfers between devices: 8.5 us -> 4.32 us  [local(): defects = lax.all_to_all(tiles, ('space', 'tm'), 0, 0)]
    ppermute x1, waiting for transfers between devices: 0.01 us -> 2.47 us  [local(): earlier = lax.ppermute(fine, 'tm', ring(slices, 1))]
    all_to_all x1, waiting for transfers between devices: 3.7 us -> 1.5 us  [local(): defects = lax.all_to_all(tiles, ('space', 'tm'), 0, 0)]
    ppermute x4 -> x2, starting transfers between devices: 2.85 us -> 4.52 us  [the longest x1 2.59 us: local(): cross = lax.ppermute(mine_cross, ('groups', 'space'), list(partner.items()))]
    ppermute x4 -> x2, waiting for transfers between devices: 0.01 us -> 1.14 us  [the longest x1 1.14 us: local(): cross = lax.ppermute(mine_cross, ('groups', 'space'), list(partner.items()))]
    ppermute x1, starting transfers between devices: 2.6 us -> 2.08 us  [local(): earlier = lax.ppermute(fine, 'tm', ring(slices, 1))]
    pallas_call x1, Pallas kernels: 1.44 us -> 1.82 us  [local(): pl.pallas_call(edges_kernel, in_specs=[anyspace] * 3, out_specs=[vmem] *...]
  transfers between devices with their start and end apart: 7 -> 5, of which waited for: 1 -> 3; matrix products, arithmetic and copies ran while one was open for 0% -> 0% of each run, Pallas kernels for 10% -> 10%
where the time goes in v4:
time: 23.3 us; the launch traced here: 23.1 us
  starting transfers between devices  11.4 us (49%)
  Pallas kernels  5.9 us (25%)
  waiting for transfers between devices  5.11 us (22%)
  between operations  0.65 us (3%)
    all_to_all x1, starting transfers between devices, local(): defects = lax.all_to_all(tiles, ('space', 'tm'), 0, 0)  4.32 us
    ppermute x1, starting transfers between devices, local(): cross = lax.ppermute(mine_cross, ('groups', 'space'), list(partner.items()))  2.59 us
    ppermute x1, waiting for transfers between devices, local(): earlier = lax.ppermute(fine, 'tm', ring(slices, 1))  2.47 us
    ppermute x1, starting transfers between devices, local(): earlier = lax.ppermute(fine, 'tm', ring(slices, 1))  2.08 us
    ppermute x1, starting transfers between devices, local(): lax.ppermute(both, 'space', ring(bricks, k))  1.93 us
    pallas_call x1, Pallas kernels, local(): pl.pallas_call(edges_kernel, in_specs=[anyspace] * 3, out_specs=[vmem] *...  1.82 us
    pallas_call x1, Pallas kernels, local(): pl.pallas_call(steps_kernel, in_specs=[vmem] * 3, out_specs=[vmem] * 2, o...  1.5 us
    all_to_all x1, waiting for transfers between devices, local(): defects = lax.all_to_all(tiles, ('space', 'tm'), 0, 0)  1.5 us
  transfers between devices with their start and end apart: 5, of which 3 were waited for; matrix products, arithmetic and copies ran while one was open for 0% of the time, Pallas kernels for 10%

profile of v4, /device:TPU:0, one launch (start us, length us, event | category | flops | bytes accessed | tf_op | source)
XLA Modules:
  0.0 23.1 jit_solution(7473127075815241820)
XLA Ops:
  0.6 1.8 %edges.1 = (f32[512,128]{1,0:T(8,128)S(1)}, f32[1536,128]{1,0:T(8,128)S(1)}, f32[512,128]{1,0:T(8,128)S(1)}, f32[232,128]{1,0:T(8,128)S(1)}, f32[200,128]{1,0:T(8,128)S(1)}) custom-call(f32[512,128]{1,0:T(8,128)} %bitcast.6, f32[1536,128]{1,0:T(8,128)} %bitcast.5, f32[512,128]{1,0:T(8,128)} %bitcast.7), custom_call_target="tpu_custom_call" | custom-call | tf_op jit(solution)/shard_map/edges/pallas_call | solution.py:266
  2.5 0.5 %collective-permute-start = (f32[232,128]{1,0:T(8,128)S(1)}, f32[232,128]{1,0:T(8,128)S(1)}, u32[]{:S(2)}, u32[]{:S(2)}) collective-permute-start(f32[232,128]{1,0:T(8,128)S(1)} %get-tuple-element.19.refs_1_), channel_id=1, source_target_pairs={{0,4},{4,0},{8,12},{12,8},{1,5},{5,1},{9,13},{13,9},{2,6},{6,2},{1... | collective-permute-start | bytes 356360 | tf_op jit(solution)/shard_map/ppermute | solution.py:293
  3.0 2.6 %collective-permute-start.1 = (f32[200,128]{1,0:T(8,128)S(1)}, f32[200,128]{1,0:T(8,128)S(1)}, u32[]{:S(2)}, u32[]{:S(2)}) collective-permute-start(f32[200,128]{1,0:T(8,128)S(1)} %get-tuple-element.20.refs_2_), channel_id=1, source_target_pairs={{0,16},{4,8},{8,4},{12,28},{16,0},{20,24},{24,20},{28,12},{1,17},{... | collective-permute-start | bytes 307208 | tf_op jit(solution)/shard_map/ppermute | solution.py:291
  5.6 1.5 %steps.1 = (f32[512,128]{1,0:T(8,128)S(1)}, f32[768,128]{1,0:T(8,128)S(1)}) custom-call(f32[512,128]{1,0:T(8,128)S(1)} %get-tuple-element.15.v_ref.start_ref, f32[1536,128]{1,0:T(8,128)S(1)} %get-tuple-element.16.vel_ref, f32[512,128]{1,0:T(8,128)S(1)} %get-tuple-element.17.d_ref), custom_call_target="tpu_custom_call" | custom-call | tf_op jit(solution)/shard_map/steps/pallas_call | solution.py:295
  7.1 1.1 %collective-permute-done.1.refs_4_ = f32[200,128]{1,0:T(8,128)S(1)} collective-permute-done((f32[200,128]{1,0:T(8,128)S(1)}, f32[200,128]{1,0:T(8,128)S(1)}, u32[]{:S(2)}, u32[]{:S(2)}) %collective-permute-start.1) | collective-permute-done | bytes 102432 | tf_op jit(solution)/shard_map/ppermute | solution.py:291
  8.2 0.0 collective-permute-done.refs_3_
  8.2 0.9 %finish.1 = (f32[512,128]{1,0:T(8,128)S(1)}, f32[16,8,128]{2,1,0:T(8,128)}, f32[8,128]{1,0:T(8,128)S(1)}, f32[2,32,128]{2,1,0:T(8,128)S(1)}) custom-call(f32[512,128]{1,0:T(8,128)S(1)} %get-tuple-element.18.refs_0_, f32[232,128]{1,0:T(8,128)S(1)} %get-tuple-element.19.refs_1_, f32[200,128]{1,0:T(8,128)S(1)} %get-tuple-element.20.refs_2_, ...), custom_call_target="tpu_custom_call" | custom-call | tf_op jit(solution)/shard_map/finish/pallas_call | solution.py:303
  9.2 2.1 %collective-permute-start.2 = (f32[512,128]{1,0:T(8,128)S(1)}, f32[512,128]{1,0:T(8,128)S(1)}, u32[]{:S(2)}, u32[]{:S(2)}) collective-permute-start(f32[512,128]{1,0:T(8,128)S(1)} %get-tuple-element.23.refs_1_), channel_id=1, source_target_pairs={{0,1},{1,2},{2,3},{3,0},{4,5},{5,6},{6,7},{7,4},{8,9},{9,10},{10,1... | collective-permute-start | bytes 786440 | tf_op jit(solution)/shard_map/ppermute | solution.py:316
  11.2 4.3 %all-to-all-start = ((f32[16,8,128]{2,1,0:T(8,128)}), f32[16,8,128]{2,1,0:T(8,128)S(1)}, u32[]{:S(2)}, u32[]{:S(2)}) async-start(f32[16,8,128]{2,1,0:T(8,128)} %get-tuple-element.22), calls=%async_computation | async-start | bytes 131072 | tf_op jit(solution)/shard_map/all_to_all | solution.py:317
  15.6 1.9 %collective-permute-start.3 = (f32[2,32,128]{2,1,0:T(8,128)S(1)}, f32[2,32,128]{2,1,0:T(8,128)S(1)}, u32[]{:S(2)}, u32[]{:S(2)}) collective-permute-start(f32[2,32,128]{2,1,0:T(8,128)S(1)} %get-tuple-element.26.refs_3_), channel_id=1, source_target_pairs={{0,8},{4,12},{8,0},{12,4},{1,9},{5,13},{9,1},{13,5},{2,10},{6,14},... | collective-permute-start | bytes 98312 | tf_op jit(solution)/shard_map/ppermute | solution.py:319
  17.5 2.5 %collective-permute-done.2.earlier_ref = f32[512,128]{1,0:T(8,128)S(1)} collective-permute-done((f32[512,128]{1,0:T(8,128)S(1)}, f32[512,128]{1,0:T(8,128)S(1)}, u32[]{:S(2)}, u32[]{:S(2)}) %collective-permute-start.2) | collective-permute-done | bytes 262176 | tf_op jit(solution)/shard_map/ppermute | solution.py:316
  20.0 0.7 %jump.1 = f32[512,128]{1,0:T(8,128)} custom-call(f32[512,128]{1,0:T(8,128)S(1)} %collective-permute-done.2.earlier_ref, f32[512,128]{1,0:T(8,128)S(1)} %get-tuple-element.15.v_ref.start_ref), custom_call_target="tpu_custom_call" | custom-call | tf_op jit(solution)/shard_map/jump/pallas_call | solution.py:322
  20.7 1.5 %all-to-all-done.refs_0_ = f32[16,8,128]{2,1,0:T(8,128)S(1)} async-done(((f32[16,8,128]{2,1,0:T(8,128)}), f32[16,8,128]{2,1,0:T(8,128)S(1)}, u32[]{:S(2)}, u32[]{:S(2)}) %all-to-all-start) | async-done | bytes 65568 | tf_op jit(solution)/shard_map/all_to_all | solution.py:317
  22.2 0.0 collective-permute-done.3.refs_4_
  22.2 0.9 %sweep.1 = f32[512,128]{1,0:T(8,128)} custom-call(f32[16,8,128]{2,1,0:T(8,128)S(1)} %all-to-all-done.refs_0_, f32[512,128]{1,0:T(8,128)S(1)} %get-tuple-element.23.refs_1_, f32[8,128]{1,0:T(8,128)S(1)} %get-tuple-element.25.refs_2_, f32[2,32,128]{2,1,0:T(8,128)S(1)} %get-tuple-element.26.refs_3_, f32[2,32,128]{2,1,0:T(8,128)S(1)} %collective-permute-done.3.refs_4_), custom_call_target="tpu_custom_call" | custom-call | tf_op jit(solution)/shard_map/sweep/pallas_call | solution.py:331
Async XLA Ops:
  2.5 5.8 %collective-permute-start = (f32[232,128]{1,0:T(8,128)S(1)}, f32[232,128]{1,0:T(8,128)S(1)}, u32[]{:S(2)}, u32[]{:S(2)}) collective-permute-start(f32[232,128]{1,0:T(8,128)S(1)} %get-tuple-element.19.refs_1_), channel_id=1, source_target_pairs={{0,4},{4,0},{8,12},{12,8},{1,5},{5,1},{9,13},{13,9},{2,6},{6,2},{1... | collective-permute-start | bytes 356360 | tf_op jit(solution)/shard_map/ppermute | solution.py:293
  3.0 5.2 %collective-permute-start.1 = (f32[200,128]{1,0:T(8,128)S(1)}, f32[200,128]{1,0:T(8,128)S(1)}, u32[]{:S(2)}, u32[]{:S(2)}) collective-permute-start(f32[200,128]{1,0:T(8,128)S(1)} %get-tuple-element.20.refs_2_), channel_id=1, source_target_pairs={{0,16},{4,8},{8,4},{12,28},{16,0},{20,24},{24,20},{28,12},{1,17},{... | collective-permute-start | bytes 307208 | tf_op jit(solution)/shard_map/ppermute | solution.py:291
  9.2 10.8 %collective-permute-start.2 = (f32[512,128]{1,0:T(8,128)S(1)}, f32[512,128]{1,0:T(8,128)S(1)}, u32[]{:S(2)}, u32[]{:S(2)}) collective-permute-start(f32[512,128]{1,0:T(8,128)S(1)} %get-tuple-element.23.refs_1_), channel_id=1, source_target_pairs={{0,1},{1,2},{2,3},{3,0},{4,5},{5,6},{6,7},{7,4},{8,9},{9,10},{10,1... | collective-permute-start | bytes 786440 | tf_op jit(solution)/shard_map/ppermute | solution.py:316
  11.2 11.0 %all-to-all-start = ((f32[16,8,128]{2,1,0:T(8,128)}), f32[16,8,128]{2,1,0:T(8,128)S(1)}, u32[]{:S(2)}, u32[]{:S(2)}) async-start(f32[16,8,128]{2,1,0:T(8,128)} %get-tuple-element.22), calls=%async_computation | async-start | bytes 131072 | tf_op jit(solution)/shard_map/all_to_all | solution.py:317
  15.6 6.6 %collective-permute-start.3 = (f32[2,32,128]{2,1,0:T(8,128)S(1)}, f32[2,32,128]{2,1,0:T(8,128)S(1)}, u32[]{:S(2)}, u32[]{:S(2)}) collective-permute-start(f32[2,32,128]{2,1,0:T(8,128)S(1)} %get-tuple-element.26.refs_3_), channel_id=1, source_target_pairs={{0,8},{4,12},{8,0},{12,4},{1,9},{5,13},{9,1},{13,5},{2,10},{6,14},... | collective-permute-start | bytes 98312 | tf_op jit(solution)/shard_map/ppermute | solution.py:319

commit v5 on v3

--- a/solution.py
+++ b/solution.py
@@ -8,6 +8,7 @@
 NZ, ROWS, LANES = 64, 8, 128
 FLAT = NZ * ROWS
 CHUNK = 8
+EDGE = 3 * NZ + ROWS
 BITS = ((1, 1), (1, 2), (0, 1), (0, 2))
 
 f32 = jnp.float32
@@ -72,22 +73,26 @@
     return ref[pl.ds(at, NZ, stride=ROWS), :]
 
 
-def edges_kernel(v_hbm, vel_hbm, d_hbm, v_ref, vel_ref, d_ref, pair_ref, cross_ref, sems):
-    copies = [
-        pltpu.make_async_copy(src, dst, sems.at[i])
-        for i, (src, dst) in enumerate(((v_hbm, v_ref), (d_hbm, d_ref), (vel_hbm, vel_ref)))
-    ]
+def edges_kernel(v_hbm, vel_hbm, d_hbm, v_ref, pair_ref, cross_ref, face_ref, sems):
+    copies = [pltpu.make_async_copy(v_hbm, v_ref, sems.at[0])]
+    for side, face in enumerate((0, ROWS - 1)):
+        for d in range(4):
+            src = d_hbm if d == 3 else vel_hbm.at[d]
+            j = 4 * side + d
+            copies.append(pltpu.make_async_copy(src.at[:, face, :], face_ref.at[j], sems.at[1 + j]))
     for copy in copies:
         copy.start()
+    odd = lax.axis_index("space") % 2 == 1
     copies[0].wait()
-    odd = lax.axis_index("space") % 2 == 1
     image = restrict_tile(plane_sums(v_ref)) * (1.0 / 64)
+    for ref in (pair_ref, cross_ref):
+        ref[3 * NZ : EDGE] = image
     for copy in copies[1:]:
         copy.wait()
     sub, lane = iotas((NZ, LANES))
     rows = []
     for face, inner, side in ((0, 1, 0), (ROWS - 1, ROWS - 2, 1)):
-        w = weights(*(row(vel_ref, d * FLAT + face) for d in range(3)), row(d_ref, face))
+        w = weights(*(face_ref[4 * side + d] for d in range(4)))
         v = row(v_ref, face)
         total = w[6] * v + w[3 - side] * row(v_ref, inner)
         total += jnp.where(sub == 0, 0.0, w[0]) * shifted(v, -1, 0)
@@ -98,11 +103,15 @@
     for j, (low, high) in enumerate(zip(*rows)):
         pair_ref[j * NZ : (j + 1) * NZ] = jnp.where(odd, low, high)
         cross_ref[j * NZ : (j + 1) * NZ] = jnp.where(odd, high, low)
-    for ref in (pair_ref, cross_ref):
-        ref[3 * NZ : 3 * NZ + ROWS] = image
-
-
-def steps_kernel(v_ref, vel_ref, d_ref, q_ref, coarse_ref, keep_ref, p_ref, pv_ref):
+
+
+def steps_kernel(v_ref, vel_hbm, d_hbm, q_ref, keep_ref, coarse_ref, p_ref, pv_ref, vel_ref, d_ref, sems):
+    copies = [
+        pltpu.make_async_copy(src, dst, sems.at[i])
+        for i, (src, dst) in enumerate(((d_hbm, d_ref), (vel_hbm, vel_ref)))
+    ]
+    for copy in copies:
+        copy.start()
     zero = jnp.zeros((ROWS, LANES), f32)
     for ref in (p_ref, pv_ref):
         ref[0:ROWS] = zero
@@ -130,6 +139,8 @@
 
         lax.fori_loop(0, NZ // CHUNK, body, 0)
 
+    for copy in copies:
+        copy.wait()
     step(pv_ref, p_ref, ROWS)
     step(p_ref, q_ref, 0)
     for side, at in enumerate((0, ROWS - 1)):
@@ -199,7 +210,7 @@
         e_at, i_at = (0, 1) if side == 0 else (ROWS - 1, ROWS - 2)
         fine_ref[pl.ds(e_at, NZ, stride=ROWS), :] = row(q_ref, e_at) + edge
         fine_ref[pl.ds(i_at, NZ, stride=ROWS), :] = row(q_ref, i_at) + inner * delta
-    at = slice(3 * NZ, 3 * NZ + ROWS)
+    at = slice(3 * NZ, EDGE)
     v = mine_pair_ref[at]
     lower = jnp.where(odd, pair_ref[at], cross_ref[at])
     upper = jnp.where(odd, cross_ref[at], pair_ref[at])
@@ -213,17 +224,20 @@
 
 
 def jump_kernel(earlier_ref, start_ref, jump_ref):
-    first = lax.axis_index("tm") == 0
-    jump_ref[...] = jnp.where(first, 0.0, start_ref[...] - earlier_ref[...])
+    keep = jnp.where(lax.axis_index("tm") == 0, 0.0, 1.0)
+    jump_ref[...] = keep * (start_ref[...] - earlier_ref[...])
 
 
 def sweep_kernel(bricks, slices, tiles_ref, fine_ref, old_ref, *refs):
     coarse_refs = refs[:bricks]
     corrected_ref, change_ref, coef_ref = refs[bricks:]
     own, n = lax.axis_index("space"), lax.axis_index("tm")
-    for k in range(bricks):
-        coef_ref[(own + bricks - k) % bricks] = coarse_refs[k][...]
-    w = [coarse_weights(coef_ref.at[b], b == 0, b == bricks - 1) for b in range(bricks)]
+    for k, ref in enumerate(coarse_refs):
+        coef_ref[(own + bricks - k) % bricks] = ref[...]
+    w = [
+        coarse_weights(coef_ref.at[b], b == 0, b == bricks - 1)
+        for b in range(bricks)
+    ]
 
     def coarse_step(m, image):
         c = [image[b] + tiles_ref[b * slices + m] for b in range(bricks)]
@@ -246,54 +260,69 @@
 
 def local(start_states, velocity, diffusivity):
     bricks, slices = lax.axis_size("space"), lax.axis_size("tm")
-    parts = bricks * slices
+    groups, parts = lax.axis_size("groups"), bricks * slices
     ring = lambda count, by: [(i, (i + by) % count) for i in range(count)]
     out = lambda *shape: pltpu.VMEM(shape, f32)
     vmem, anyspace = pl.BlockSpec(memory_space=pltpu.VMEM), pl.BlockSpec(memory_space=pl.ANY)
     inside = lambda *xs: [pltpu.with_memory_space_constraint(x, pltpu.VMEM) for x in xs]
 
-    v, vel, diff, mine_pair, mine_cross = pl.pallas_call(
+    v, mine_pair, mine_cross = pl.pallas_call(
         edges_kernel,
         in_specs=[anyspace] * 3,
-        out_specs=[vmem] * 5,
+        out_specs=[vmem] * 3,
         out_shape=[
             out(FLAT, LANES),
-            out(3 * FLAT, LANES),
-            out(FLAT, LANES),
-            out(3 * NZ + ROWS, LANES),
-            out(3 * NZ + ROWS, LANES),
+            out(EDGE, LANES),
+            out(EDGE, LANES),
         ],
-        scratch_shapes=[pltpu.SemaphoreType.DMA((3,))],
+        scratch_shapes=[pltpu.VMEM((8, NZ, LANES), f32), pltpu.SemaphoreType.DMA((9,))],
         name="edges",
     )(
         start_states.reshape(FLAT, LANES),
-        velocity.reshape(3 * FLAT, LANES),
-        diffusivity.reshape(FLAT, LANES),
+        velocity,
+        diffusivity,
     )
+    partner = {}
+    for g in range(groups):
+        for i in range(bricks):
+            j, h = i + 1 if i % 2 else i - 1, g
+            if j < 0 or j >= bricks:
+                j, h = (i, g ^ 1) if groups % 2 == 0 else (j % bricks, g)
+            partner[g * bricks + i] = h * bricks + j
+    cross = lax.ppermute(mine_cross, ("groups", "space"), list(partner.items()))
+
     pair = lax.ppermute(mine_pair, "space", [(i, i ^ 1) for i in range(bricks)])
-    across = [(i, min(max(((i + 1) ^ 1) - 1, 0), bricks - 1)) for i in range(bricks)]
-    cross = lax.ppermute(mine_cross, "space", across)
-
-    q, coarse, keep = pl.pallas_call(
+
+    q, keep, coarse = pl.pallas_call(
         steps_kernel,
-        in_specs=[vmem] * 3,
+        in_specs=[vmem, anyspace, anyspace],
         out_specs=[vmem] * 3,
-        out_shape=[out(FLAT, LANES), out(4, ROWS, LANES), out(12 * NZ, LANES)],
-        scratch_shapes=[pltpu.VMEM((FLAT + 2 * ROWS, LANES), f32)] * 2,
+        out_shape=[out(FLAT, LANES), out(12 * NZ, LANES), out(4, ROWS, LANES)],
+        scratch_shapes=[pltpu.VMEM((FLAT + 2 * ROWS, LANES), f32)] * 2
+        + [
+            pltpu.VMEM((3 * FLAT, LANES), f32),
+            pltpu.VMEM((FLAT, LANES), f32),
+            pltpu.SemaphoreType.DMA((2,)),
+        ],
         name="steps",
-    )(*inside(v, vel, diff))
-
+    )(*inside(v), velocity.reshape(3 * FLAT, LANES), diffusivity.reshape(FLAT, LANES))
     fine, tiles, old = pl.pallas_call(
         lambda *refs: finish_kernel(parts, bricks, *refs),
         in_specs=[vmem] * 7,
         out_specs=[vmem] * 3,
-        out_shape=[out(FLAT, LANES), out(parts, ROWS, LANES), out(ROWS, LANES)],
+        out_shape=[
+            out(FLAT, LANES),
+            out(parts, ROWS, LANES),
+            out(ROWS, LANES),
+        ],
         name="finish",
     )(*inside(q, mine_pair, mine_cross, pair, cross, keep, coarse))
 
     earlier = lax.ppermute(fine, "tm", ring(slices, 1))
     defects = lax.all_to_all(tiles, ("space", "tm"), 0, 0)
-    coarse_all = [coarse] + [lax.ppermute(coarse, "space", ring(bricks, k)) for k in range(1, bricks)]
+    coarse_all = [coarse] + [
+        lax.ppermute(coarse, "space", ring(bricks, k)) for k in range(1, bricks)
+    ]
 
     jump = pl.pallas_call(
         jump_kernel,

time: 24.8 us -> 22.8 us (0.919)
  starting transfers between devices: 14.5 us -> 11.4 us
  Pallas kernels: 5.7 us -> 6.8 us
    all_to_all x1, starting transfers between devices: 8.5 us -> 4.32 us  [local(): defects = lax.all_to_all(tiles, ('space', 'tm'), 0, 0)]
    ppermute x1, waiting for transfers between devices: 0.01 us -> 2.21 us  [local(): earlier = lax.ppermute(fine, 'tm', ring(slices, 1))]
    all_to_all x1, waiting for transfers between devices: 3.7 us -> 1.5 us  [local(): defects = lax.all_to_all(tiles, ('space', 'tm'), 0, 0)]
    ppermute x1, starting transfers between devices: 0.66 us -> 2.59 us  [local(): cross = lax.ppermute(mine_cross, ('groups', 'space'), list(partner.items()))]
    pallas_call x1, Pallas kernels: 1.68 us -> 2.88 us  [local(): pl.pallas_call(steps_kernel, in_specs=[vmem, anyspace, anyspace], out_spe...]
    ppermute x1, starting transfers between devices: 2.6 us -> 1.81 us  [local(): earlier = lax.ppermute(fine, 'tm', ring(slices, 1))]
  transfers between devices with their start and end apart: 7 -> 7, of which waited for: 1 -> 2; matrix products, arithmetic and copies ran while one was open for 0% -> 0% of each run, Pallas kernels for 10% -> 16%
where the time goes in v5:
time: 22.8 us; the launch traced here: 22.6 us
  starting transfers between devices  11.4 us (50%)
  Pallas kernels  6.8 us (30%)
  waiting for transfers between devices  3.72 us (16%)
  between operations  0.68 us (3%)
    all_to_all x1, starting transfers between devices, local(): defects = lax.all_to_all(tiles, ('space', 'tm'), 0, 0)  4.32 us
    pallas_call x1, Pallas kernels, local(): pl.pallas_call(steps_kernel, in_specs=[vmem, anyspace, anyspace], out_spe...  2.88 us
    ppermute x1, starting transfers between devices, local(): cross = lax.ppermute(mine_cross, ('groups', 'space'), list(partner.items()))  2.59 us
    ppermute x1, waiting for transfers between devices, local(): earlier = lax.ppermute(fine, 'tm', ring(slices, 1))  2.21 us
    ppermute x3, starting transfers between devices, local(): lax.ppermute(coarse, 'space', ring(bricks, k))  2.19 us
    ppermute x1, starting transfers between devices, local(): earlier = lax.ppermute(fine, 'tm', ring(slices, 1))  1.81 us
    all_to_all x1, waiting for transfers between devices, local(): defects = lax.all_to_all(tiles, ('space', 'tm'), 0, 0)  1.5 us
    pallas_call x1, Pallas kernels, local(): pl.pallas_call(edges_kernel, in_specs=[anyspace] * 3, out_specs=[vmem] *...  1.31 us
  transfers between devices with their start and end apart: 7, of which 2 were waited for; matrix products, arithmetic and copies ran while one was open for 0% of the time, Pallas kernels for 16%

profile of v5, /device:TPU:0, one launch (start us, length us, event | category | flops | bytes accessed | tf_op | source)
XLA Modules:
  0.0 22.6 jit_solution(4032589724259049946)
XLA Ops:
  0.6 1.3 %edges.1 = (f32[512,128]{1,0:T(8,128)S(1)}, f32[200,128]{1,0:T(8,128)S(1)}, f32[200,128]{1,0:T(8,128)S(1)}) custom-call(f32[512,128]{1,0:T(8,128)} %bitcast.7, f32[3,64,8,128]{3,2,1,0:T(8,128)} %vel_hbm.1, f32[64,8,128]{2,1,0:T(8,128)} %d_hbm.1), custom_call_target="tpu_custom_call" | custom-call | tf_op jit(solution)/shard_map/edges/pallas_call | solution.py:269
  1.9 0.5 %collective-permute-start = (f32[200,128]{1,0:T(8,128)S(1)}, f32[200,128]{1,0:T(8,128)S(1)}, u32[]{:S(2)}, u32[]{:S(2)}) collective-permute-start(f32[200,128]{1,0:T(8,128)S(1)} %get-tuple-element.15.refs_1_), channel_id=1, source_target_pairs={{0,4},{4,0},{8,12},{12,8},{1,5},{5,1},{9,13},{13,9},{2,6},{6,2},{1... | collective-permute-start | bytes 307208 | tf_op jit(solution)/shard_map/ppermute | solution.py:294
  2.5 2.6 %collective-permute-start.1 = (f32[200,128]{1,0:T(8,128)S(1)}, f32[200,128]{1,0:T(8,128)S(1)}, u32[]{:S(2)}, u32[]{:S(2)}) collective-permute-start(f32[200,128]{1,0:T(8,128)S(1)} %get-tuple-element.16.refs_2_), channel_id=1, source_target_pairs={{0,16},{4,8},{8,4},{12,28},{16,0},{20,24},{24,20},{28,12},{1,17},{... | collective-permute-start | bytes 307208 | tf_op jit(solution)/shard_map/ppermute | solution.py:292
  5.1 2.9 %steps.1 = (f32[512,128]{1,0:T(8,128)S(1)}, f32[768,128]{1,0:T(8,128)S(1)}, f32[4,8,128]{2,1,0:T(8,128)S(1)}) custom-call(f32[512,128]{1,0:T(8,128)S(1)} %get-tuple-element.13.v_ref.start_ref, f32[1536,128]{1,0:T(8,128)} %bitcast.5, f32[512,128]{1,0:T(8,128)} %bitcast.6), custom_call_target="tpu_custom_call" | custom-call | tf_op jit(solution)/shard_map/steps/pallas_call | solution.py:296
  7.9 0.0 collective-permute-done.refs_3_
  8.0 0.0 collective-permute-done.1.refs_4_
  8.0 1.0 %finish.1 = (f32[512,128]{1,0:T(8,128)S(1)}, f32[16,8,128]{2,1,0:T(8,128)}, f32[8,128]{1,0:T(8,128)S(1)}) custom-call(f32[512,128]{1,0:T(8,128)S(1)} %get-tuple-element.14.refs_0_, f32[200,128]{1,0:T(8,128)S(1)} %get-tuple-element.15.refs_1_, f32[200,128]{1,0:T(8,128)S(1)} %get-tuple-element.16.refs_2_, f32[200,128]{1,0:T(8,128)S(1)} %collective-permute-done.refs_3_, ...), custom_call_target="tpu_custom_call" | custom-call | tf_op jit(solution)/shard_map/finish/pallas_call | solution.py:309
  8.9 1.8 %collective-permute-start.2 = (f32[512,128]{1,0:T(8,128)S(1)}, f32[512,128]{1,0:T(8,128)S(1)}, u32[]{:S(2)}, u32[]{:S(2)}) collective-permute-start(f32[512,128]{1,0:T(8,128)S(1)} %get-tuple-element.20.refs_1_), channel_id=1, source_target_pairs={{0,1},{1,2},{2,3},{3,0},{4,5},{5,6},{6,7},{7,4},{8,9},{9,10},{10,1... | collective-permute-start | bytes 786440 | tf_op jit(solution)/shard_map/ppermute | solution.py:321
  10.7 4.3 %all-to-all-start = ((f32[16,8,128]{2,1,0:T(8,128)}), f32[16,8,128]{2,1,0:T(8,128)S(1)}, u32[]{:S(2)}, u32[]{:S(2)}) async-start(f32[16,8,128]{2,1,0:T(8,128)} %get-tuple-element.19), calls=%async_computation | async-start | bytes 131072 | tf_op jit(solution)/shard_map/all_to_all | solution.py:322
  15.1 1.7 %collective-permute-start.5 = (f32[4,8,128]{2,1,0:T(8,128)S(1)}, f32[4,8,128]{2,1,0:T(8,128)S(1)}, u32[]{:S(2)}, u32[]{:S(2)}) collective-permute-start(f32[4,8,128]{2,1,0:T(8,128)S(1)} %get-tuple-element.18.refs_6_.refs_3_), channel_id=1, source_target_pairs={{0,12},{4,0},{8,4},{12,8},{1,13},{5,1},{9,5},{13,9},{2,14},{6,2},{... | collective-permute-start | bytes 49160 | tf_op jit(solution)/shard_map/ppermute | solution.py:324
  16.7 0.4 %collective-permute-start.4 = (f32[4,8,128]{2,1,0:T(8,128)S(1)}, f32[4,8,128]{2,1,0:T(8,128)S(1)}, u32[]{:S(2)}, u32[]{:S(2)}) collective-permute-start(f32[4,8,128]{2,1,0:T(8,128)S(1)} %get-tuple-element.18.refs_6_.refs_3_), channel_id=1, source_target_pairs={{0,8},{4,12},{8,0},{12,4},{1,9},{5,13},{9,1},{13,5},{2,10},{6,14},... | collective-permute-start | bytes 49160 | tf_op jit(solution)/shard_map/ppermute | solution.py:324
  17.1 0.1 collective-permute-start.3
  17.3 2.2 %collective-permute-done.2.earlier_ref = f32[512,128]{1,0:T(8,128)S(1)} collective-permute-done((f32[512,128]{1,0:T(8,128)S(1)}, f32[512,128]{1,0:T(8,128)S(1)}, u32[]{:S(2)}, u32[]{:S(2)}) %collective-permute-start.2) | collective-permute-done | bytes 262176 | tf_op jit(solution)/shard_map/ppermute | solution.py:321
  19.5 0.7 %jump.1 = f32[512,128]{1,0:T(8,128)} custom-call(f32[512,128]{1,0:T(8,128)S(1)} %collective-permute-done.2.earlier_ref, f32[512,128]{1,0:T(8,128)S(1)} %get-tuple-element.13.v_ref.start_ref), custom_call_target="tpu_custom_call" | custom-call | tf_op jit(solution)/shard_map/jump/pallas_call | solution.py:327
  20.2 1.5 %all-to-all-done.refs_0_ = f32[16,8,128]{2,1,0:T(8,128)S(1)} async-done(((f32[16,8,128]{2,1,0:T(8,128)}), f32[16,8,128]{2,1,0:T(8,128)S(1)}, u32[]{:S(2)}, u32[]{:S(2)}) %all-to-all-start) | async-done | bytes 65568 | tf_op jit(solution)/shard_map/all_to_all | solution.py:322
  21.7 0.0 collective-permute-done.5.refs_6_
  21.7 0.0 collective-permute-done.4.refs_5_
  21.7 0.0 collective-permute-done.3.refs_4_
  21.7 0.9 %sweep.1 = f32[512,128]{1,0:T(8,128)} custom-call(f32[16,8,128]{2,1,0:T(8,128)S(1)} %all-to-all-done.refs_0_, f32[512,128]{1,0:T(8,128)S(1)} %get-tuple-element.20.refs_1_, f32[8,128]{1,0:T(8,128)S(1)} %get-tuple-element.22.refs_2_, f32[4,8,128]{2,1,0:T(8,128)S(1)} %get-tuple-element.18.refs_6_.refs_3_, f32[4,8,128]{2,1,0:T(8,128)S(1)} %collective-permute-done.3.refs_4_, ...), custom_call_target="tpu_custom_call" | custom-call | tf_op jit(solution)/shard_map/sweep/pallas_call | solution.py:336
Async XLA Ops:
  1.9 6.0 %collective-permute-start = (f32[200,128]{1,0:T(8,128)S(1)}, f32[200,128]{1,0:T(8,128)S(1)}, u32[]{:S(2)}, u32[]{:S(2)}) collective-permute-start(f32[200,128]{1,0:T(8,128)S(1)} %get-tuple-element.15.refs_1_), channel_id=1, source_target_pairs={{0,4},{4,0},{8,12},{12,8},{1,5},{5,1},{9,13},{13,9},{2,6},{6,2},{1... | collective-permute-start | bytes 307208 | tf_op jit(solution)/shard_map/ppermute | solution.py:294
  2.5 5.5 %collective-permute-start.1 = (f32[200,128]{1,0:T(8,128)S(1)}, f32[200,128]{1,0:T(8,128)S(1)}, u32[]{:S(2)}, u32[]{:S(2)}) collective-permute-start(f32[200,128]{1,0:T(8,128)S(1)} %get-tuple-element.16.refs_2_), channel_id=1, source_target_pairs={{0,16},{4,8},{8,4},{12,28},{16,0},{20,24},{24,20},{28,12},{1,17},{... | collective-permute-start | bytes 307208 | tf_op jit(solution)/shard_map/ppermute | solution.py:292
  8.9 10.5 %collective-permute-start.2 = (f32[512,128]{1,0:T(8,128)S(1)}, f32[512,128]{1,0:T(8,128)S(1)}, u32[]{:S(2)}, u32[]{:S(2)}) collective-permute-start(f32[512,128]{1,0:T(8,128)S(1)} %get-tuple-element.20.refs_1_), channel_id=1, source_target_pairs={{0,1},{1,2},{2,3},{3,0},{4,5},{5,6},{6,7},{7,4},{8,9},{9,10},{10,1... | collective-permute-start | bytes 786440 | tf_op jit(solution)/shard_map/ppermute | solution.py:321
  10.7 11.0 %all-to-all-start = ((f32[16,8,128]{2,1,0:T(8,128)}), f32[16,8,128]{2,1,0:T(8,128)S(1)}, u32[]{:S(2)}, u32[]{:S(2)}) async-start(f32[16,8,128]{2,1,0:T(8,128)} %get-tuple-element.19), calls=%async_computation | async-start | bytes 131072 | tf_op jit(solution)/shard_map/all_to_all | solution.py:322
  15.1 6.6 %collective-permute-start.5 = (f32[4,8,128]{2,1,0:T(8,128)S(1)}, f32[4,8,128]{2,1,0:T(8,128)S(1)}, u32[]{:S(2)}, u32[]{:S(2)}) collective-permute-start(f32[4,8,128]{2,1,0:T(8,128)S(1)} %get-tuple-element.18.refs_6_.refs_3_), channel_id=1, source_target_pairs={{0,12},{4,0},{8,4},{12,8},{1,13},{5,1},{9,5},{13,9},{2,14},{6,2},{... | collective-permute-start | bytes 49160 | tf_op jit(solution)/shard_map/ppermute | solution.py:324
  16.7 5.0 %collective-permute-start.4 = (f32[4,8,128]{2,1,0:T(8,128)S(1)}, f32[4,8,128]{2,1,0:T(8,128)S(1)}, u32[]{:S(2)}, u32[]{:S(2)}) collective-permute-start(f32[4,8,128]{2,1,0:T(8,128)S(1)} %get-tuple-element.18.refs_6_.refs_3_), channel_id=1, source_target_pairs={{0,8},{4,12},{8,0},{12,4},{1,9},{5,13},{9,1},{13,5},{2,10},{6,14},... | collective-permute-start | bytes 49160 | tf_op jit(solution)/shard_map/ppermute | solution.py:324
  17.1 4.6 %collective-permute-start.3 = (f32[4,8,128]{2,1,0:T(8,128)S(1)}, f32[4,8,128]{2,1,0:T(8,128)S(1)}, u32[]{:S(2)}, u32[]{:S(2)}) collective-permute-start(f32[4,8,128]{2,1,0:T(8,128)S(1)} %get-tuple-element.18.refs_6_.refs_3_), channel_id=1, source_target_pairs={{0,4},{4,8},{8,12},{12,0},{1,5},{5,9},{9,13},{13,1},{2,6},{6,10},{... | collective-permute-start | bytes 49160 | tf_op jit(solution)/shard_map/ppermute | solution.py:324

commit v6 on v5

--- a/solution.py
+++ b/solution.py
@@ -9,7 +9,7 @@
 FLAT = NZ * ROWS
 CHUNK = 8
 EDGE = 3 * NZ + ROWS
-BITS = ((1, 1), (1, 2), (0, 1), (0, 2))
+BITS = ((0, 1), (0, 2), (1, 1), (1, 2))
 
 f32 = jnp.float32
 
@@ -83,12 +83,11 @@
     for copy in copies:
         copy.start()
     odd = lax.axis_index("space") % 2 == 1
-    copies[0].wait()
+    for copy in copies:
+        copy.wait()
     image = restrict_tile(plane_sums(v_ref)) * (1.0 / 64)
     for ref in (pair_ref, cross_ref):
         ref[3 * NZ : EDGE] = image
-    for copy in copies[1:]:
-        copy.wait()
     sub, lane = iotas((NZ, LANES))
     rows = []
     for face, inner, side in ((0, 1, 0), (ROWS - 1, ROWS - 2, 1)):
@@ -157,7 +156,7 @@
 
 def coarse_weights(c, first, last):
     sub, lane = iotas((ROWS, LANES))
-    zl, zh, y = lane % 4, sub % 4, lane // 4
+    zl, zh, y = sub % 4, lane % 4, lane // 4
     w = weights(c[0], c[1], c[2], c[3])
     w[0] = jnp.where((zl == 0) & (zh == 0), 0.0, w[0])
     w[1] = jnp.where((zl == 3) & (zh == 3), 0.0, w[1])
@@ -170,9 +169,9 @@
 
 def coarse_apply(w, v, own, lower, upper):
     sub, lane = iotas((ROWS, LANES))
-    zl = lane % 4
-    zb = jnp.where(zl == 0, shifted(shifted(v, 3, 1), -1, 0), shifted(v, -1, 1))
-    za = jnp.where(zl == 3, shifted(shifted(v, -3, 1), 1, 0), shifted(v, 1, 1))
+    zl = sub % 4
+    zb = jnp.where(zl == 0, shifted(shifted(v, -1, 1), 3, 0), shifted(v, -1, 0))
+    za = jnp.where(zl == 3, shifted(shifted(v, 1, 1), -3, 0), shifted(v, 1, 0))
     xb = jnp.where(sub < 4, lower, own)
     xa = jnp.where(sub < 4, own, upper)
     return (

time: 22.8 us -> 22.7 us (level)
  no operation moved by 1% of the time
where the time goes in v6:
time: 22.7 us; the launch traced here: 22.5 us
  starting transfers between devices  11.5 us (51%)
  Pallas kernels  6.66 us (29%)
  waiting for transfers between devices  3.72 us (16%)
  between operations  0.68 us (3%)
    all_to_all x1, starting transfers between devices, local(): defects = lax.all_to_all(tiles, ('space', 'tm'), 0, 0)  4.32 us
    pallas_call x1, Pallas kernels, local(): pl.pallas_call(steps_kernel, in_specs=[vmem, anyspace, anyspace], out_spe...  2.85 us
    ppermute x1, starting transfers between devices, local(): cross = lax.ppermute(mine_cross, ('groups', 'space'), list(partner.items()))  2.59 us
    ppermute x1, waiting for transfers between devices, local(): earlier = lax.ppermute(fine, 'tm', ring(slices, 1))  2.21 us
    ppermute x3, starting transfers between devices, local(): lax.ppermute(coarse, 'space', ring(bricks, k))  2.19 us
    ppermute x1, starting transfers between devices, local(): earlier = lax.ppermute(fine, 'tm', ring(slices, 1))  1.83 us
    all_to_all x1, waiting for transfers between devices, local(): defects = lax.all_to_all(tiles, ('space', 'tm'), 0, 0)  1.5 us
    pallas_call x1, Pallas kernels, local(): pl.pallas_call(edges_kernel, in_specs=[anyspace] * 3, out_specs=[vmem] *...  1.21 us
  transfers between devices with their start and end apart: 7, of which 2 were waited for; matrix products, arithmetic and copies ran while one was open for 0% of the time, Pallas kernels for 16%

profile of v6, /device:TPU:0, one launch (start us, length us, event | category | flops | bytes accessed | tf_op | source)
XLA Modules:
  0.0 22.5 jit_solution(12354272688195180828)
XLA Ops:
  0.6 1.2 %edges.1 = (f32[512,128]{1,0:T(8,128)S(1)}, f32[200,128]{1,0:T(8,128)S(1)}, f32[200,128]{1,0:T(8,128)S(1)}) custom-call(f32[512,128]{1,0:T(8,128)} %bitcast.7, f32[3,64,8,128]{3,2,1,0:T(8,128)} %vel_hbm.1, f32[64,8,128]{2,1,0:T(8,128)} %d_hbm.1), custom_call_target="tpu_custom_call" | custom-call | tf_op jit(solution)/shard_map/edges/pallas_call | solution.py:268
  1.8 0.5 %collective-permute-start = (f32[200,128]{1,0:T(8,128)S(1)}, f32[200,128]{1,0:T(8,128)S(1)}, u32[]{:S(2)}, u32[]{:S(2)}) collective-permute-start(f32[200,128]{1,0:T(8,128)S(1)} %get-tuple-element.15.refs_1_), channel_id=1, source_target_pairs={{0,4},{4,0},{8,12},{12,8},{1,5},{5,1},{9,13},{13,9},{2,6},{6,2},{1... | collective-permute-start | bytes 307208 | tf_op jit(solution)/shard_map/ppermute | solution.py:293
  2.4 2.6 %collective-permute-start.1 = (f32[200,128]{1,0:T(8,128)S(1)}, f32[200,128]{1,0:T(8,128)S(1)}, u32[]{:S(2)}, u32[]{:S(2)}) collective-permute-start(f32[200,128]{1,0:T(8,128)S(1)} %get-tuple-element.16.refs_2_), channel_id=1, source_target_pairs={{0,16},{4,8},{8,4},{12,28},{16,0},{20,24},{24,20},{28,12},{1,17},{... | collective-permute-start | bytes 307208 | tf_op jit(solution)/shard_map/ppermute | solution.py:291
  5.0 2.9 %steps.1 = (f32[512,128]{1,0:T(8,128)S(1)}, f32[768,128]{1,0:T(8,128)S(1)}, f32[4,8,128]{2,1,0:T(8,128)S(1)}) custom-call(f32[512,128]{1,0:T(8,128)S(1)} %get-tuple-element.13.v_ref.start_ref, f32[1536,128]{1,0:T(8,128)} %bitcast.5, f32[512,128]{1,0:T(8,128)} %bitcast.6), custom_call_target="tpu_custom_call" | custom-call | tf_op jit(solution)/shard_map/steps/pallas_call | solution.py:295
  7.8 0.0 collective-permute-done.refs_3_
  7.8 0.0 collective-permute-done.1.refs_4_
  7.8 1.0 %finish.1 = (f32[512,128]{1,0:T(8,128)S(1)}, f32[16,8,128]{2,1,0:T(8,128)}, f32[8,128]{1,0:T(8,128)S(1)}) custom-call(f32[512,128]{1,0:T(8,128)S(1)} %get-tuple-element.14.refs_0_, f32[200,128]{1,0:T(8,128)S(1)} %get-tuple-element.15.refs_1_, f32[200,128]{1,0:T(8,128)S(1)} %get-tuple-element.16.refs_2_, f32[200,128]{1,0:T(8,128)S(1)} %collective-permute-done.refs_3_, ...), custom_call_target="tpu_custom_call" | custom-call | tf_op jit(solution)/shard_map/finish/pallas_call | solution.py:308
  8.8 1.8 %collective-permute-start.2 = (f32[512,128]{1,0:T(8,128)S(1)}, f32[512,128]{1,0:T(8,128)S(1)}, u32[]{:S(2)}, u32[]{:S(2)}) collective-permute-start(f32[512,128]{1,0:T(8,128)S(1)} %get-tuple-element.20.refs_1_), channel_id=1, source_target_pairs={{0,1},{1,2},{2,3},{3,0},{4,5},{5,6},{6,7},{7,4},{8,9},{9,10},{10,1... | collective-permute-start | bytes 786440 | tf_op jit(solution)/shard_map/ppermute | solution.py:320
  10.6 4.3 %all-to-all-start = ((f32[16,8,128]{2,1,0:T(8,128)}), f32[16,8,128]{2,1,0:T(8,128)S(1)}, u32[]{:S(2)}, u32[]{:S(2)}) async-start(f32[16,8,128]{2,1,0:T(8,128)} %get-tuple-element.19), calls=%async_computation | async-start | bytes 131072 | tf_op jit(solution)/shard_map/all_to_all | solution.py:321
  15.0 1.7 %collective-permute-start.5 = (f32[4,8,128]{2,1,0:T(8,128)S(1)}, f32[4,8,128]{2,1,0:T(8,128)S(1)}, u32[]{:S(2)}, u32[]{:S(2)}) collective-permute-start(f32[4,8,128]{2,1,0:T(8,128)S(1)} %get-tuple-element.18.refs_6_.refs_3_), channel_id=1, source_target_pairs={{0,12},{4,0},{8,4},{12,8},{1,13},{5,1},{9,5},{13,9},{2,14},{6,2},{... | collective-permute-start | bytes 49160 | tf_op jit(solution)/shard_map/ppermute | solution.py:323
  16.6 0.4 %collective-permute-start.4 = (f32[4,8,128]{2,1,0:T(8,128)S(1)}, f32[4,8,128]{2,1,0:T(8,128)S(1)}, u32[]{:S(2)}, u32[]{:S(2)}) collective-permute-start(f32[4,8,128]{2,1,0:T(8,128)S(1)} %get-tuple-element.18.refs_6_.refs_3_), channel_id=1, source_target_pairs={{0,8},{4,12},{8,0},{12,4},{1,9},{5,13},{9,1},{13,5},{2,10},{6,14},... | collective-permute-start | bytes 49160 | tf_op jit(solution)/shard_map/ppermute | solution.py:323
  17.0 0.1 collective-permute-start.3
  17.1 2.2 %collective-permute-done.2.earlier_ref = f32[512,128]{1,0:T(8,128)S(1)} collective-permute-done((f32[512,128]{1,0:T(8,128)S(1)}, f32[512,128]{1,0:T(8,128)S(1)}, u32[]{:S(2)}, u32[]{:S(2)}) %collective-permute-start.2) | collective-permute-done | bytes 262176 | tf_op jit(solution)/shard_map/ppermute | solution.py:320
  19.4 0.7 %jump.1 = f32[512,128]{1,0:T(8,128)} custom-call(f32[512,128]{1,0:T(8,128)S(1)} %collective-permute-done.2.earlier_ref, f32[512,128]{1,0:T(8,128)S(1)} %get-tuple-element.13.v_ref.start_ref), custom_call_target="tpu_custom_call" | custom-call | tf_op jit(solution)/shard_map/jump/pallas_call | solution.py:326
  20.1 1.5 %all-to-all-done.refs_0_ = f32[16,8,128]{2,1,0:T(8,128)S(1)} async-done(((f32[16,8,128]{2,1,0:T(8,128)}), f32[16,8,128]{2,1,0:T(8,128)S(1)}, u32[]{:S(2)}, u32[]{:S(2)}) %all-to-all-start) | async-done | bytes 65568 | tf_op jit(solution)/shard_map/all_to_all | solution.py:321
  21.6 0.0 collective-permute-done.5.refs_6_
  21.6 0.0 collective-permute-done.4.refs_5_
  21.6 0.0 collective-permute-done.3.refs_4_
  21.6 0.9 %sweep.1 = f32[512,128]{1,0:T(8,128)} custom-call(f32[16,8,128]{2,1,0:T(8,128)S(1)} %all-to-all-done.refs_0_, f32[512,128]{1,0:T(8,128)S(1)} %get-tuple-element.20.refs_1_, f32[8,128]{1,0:T(8,128)S(1)} %get-tuple-element.22.refs_2_, f32[4,8,128]{2,1,0:T(8,128)S(1)} %get-tuple-element.18.refs_6_.refs_3_, f32[4,8,128]{2,1,0:T(8,128)S(1)} %collective-permute-done.3.refs_4_, ...), custom_call_target="tpu_custom_call" | custom-call | tf_op jit(solution)/shard_map/sweep/pallas_call | solution.py:335
Async XLA Ops:
  1.8 6.0 %collective-permute-start = (f32[200,128]{1,0:T(8,128)S(1)}, f32[200,128]{1,0:T(8,128)S(1)}, u32[]{:S(2)}, u32[]{:S(2)}) collective-permute-start(f32[200,128]{1,0:T(8,128)S(1)} %get-tuple-element.15.refs_1_), channel_id=1, source_target_pairs={{0,4},{4,0},{8,12},{12,8},{1,5},{5,1},{9,13},{13,9},{2,6},{6,2},{1... | collective-permute-start | bytes 307208 | tf_op jit(solution)/shard_map/ppermute | solution.py:293
  2.4 5.5 %collective-permute-start.1 = (f32[200,128]{1,0:T(8,128)S(1)}, f32[200,128]{1,0:T(8,128)S(1)}, u32[]{:S(2)}, u32[]{:S(2)}) collective-permute-start(f32[200,128]{1,0:T(8,128)S(1)} %get-tuple-element.16.refs_2_), channel_id=1, source_target_pairs={{0,16},{4,8},{8,4},{12,28},{16,0},{20,24},{24,20},{28,12},{1,17},{... | collective-permute-start | bytes 307208 | tf_op jit(solution)/shard_map/ppermute | solution.py:291
  8.8 10.6 %collective-permute-start.2 = (f32[512,128]{1,0:T(8,128)S(1)}, f32[512,128]{1,0:T(8,128)S(1)}, u32[]{:S(2)}, u32[]{:S(2)}) collective-permute-start(f32[512,128]{1,0:T(8,128)S(1)} %get-tuple-element.20.refs_1_), channel_id=1, source_target_pairs={{0,1},{1,2},{2,3},{3,0},{4,5},{5,6},{6,7},{7,4},{8,9},{9,10},{10,1... | collective-permute-start | bytes 786440 | tf_op jit(solution)/shard_map/ppermute | solution.py:320
  10.6 11.0 %all-to-all-start = ((f32[16,8,128]{2,1,0:T(8,128)}), f32[16,8,128]{2,1,0:T(8,128)S(1)}, u32[]{:S(2)}, u32[]{:S(2)}) async-start(f32[16,8,128]{2,1,0:T(8,128)} %get-tuple-element.19), calls=%async_computation | async-start | bytes 131072 | tf_op jit(solution)/shard_map/all_to_all | solution.py:321
  15.0 6.6 %collective-permute-start.5 = (f32[4,8,128]{2,1,0:T(8,128)S(1)}, f32[4,8,128]{2,1,0:T(8,128)S(1)}, u32[]{:S(2)}, u32[]{:S(2)}) collective-permute-start(f32[4,8,128]{2,1,0:T(8,128)S(1)} %get-tuple-element.18.refs_6_.refs_3_), channel_id=1, source_target_pairs={{0,12},{4,0},{8,4},{12,8},{1,13},{5,1},{9,5},{13,9},{2,14},{6,2},{... | collective-permute-start | bytes 49160 | tf_op jit(solution)/shard_map/ppermute | solution.py:323
  16.6 5.0 %collective-permute-start.4 = (f32[4,8,128]{2,1,0:T(8,128)S(1)}, f32[4,8,128]{2,1,0:T(8,128)S(1)}, u32[]{:S(2)}, u32[]{:S(2)}) collective-permute-start(f32[4,8,128]{2,1,0:T(8,128)S(1)} %get-tuple-element.18.refs_6_.refs_3_), channel_id=1, source_target_pairs={{0,8},{4,12},{8,0},{12,4},{1,9},{5,13},{9,1},{13,5},{2,10},{6,14},... | collective-permute-start | bytes 49160 | tf_op jit(solution)/shard_map/ppermute | solution.py:323
  17.0 4.6 %collective-permute-start.3 = (f32[4,8,128]{2,1,0:T(8,128)S(1)}, f32[4,8,128]{2,1,0:T(8,128)S(1)}, u32[]{:S(2)}, u32[]{:S(2)}) collective-permute-start(f32[4,8,128]{2,1,0:T(8,128)S(1)} %get-tuple-element.18.refs_6_.refs_3_), channel_id=1, source_target_pairs={{0,4},{4,8},{8,12},{12,0},{1,5},{5,9},{9,13},{13,1},{2,6},{6,10},{... | collective-permute-start | bytes 49160 | tf_op jit(solution)/shard_map/ppermute | solution.py:323

commit v7 on v6

--- a/solution.py
+++ b/solution.py
@@ -104,13 +104,7 @@
         cross_ref[j * NZ : (j + 1) * NZ] = jnp.where(odd, high, low)
 
 
-def steps_kernel(v_ref, vel_hbm, d_hbm, q_ref, keep_ref, coarse_ref, p_ref, pv_ref, vel_ref, d_ref, sems):
-    copies = [
-        pltpu.make_async_copy(src, dst, sems.at[i])
-        for i, (src, dst) in enumerate(((d_hbm, d_ref), (vel_hbm, vel_ref)))
-    ]
-    for copy in copies:
-        copy.start()
+def two_steps(v_ref, c_ref, q_ref, p_ref, pv_ref):
     zero = jnp.zeros((ROWS, LANES), f32)
     for ref in (p_ref, pv_ref):
         ref[0:ROWS] = zero
@@ -124,9 +118,7 @@
         def body(c, carry):
             at = pl.multiple_of(c * size, size)
             load = lambda ref, off: ref[pl.ds(at + off, size), :].reshape(shape)
-            w = weights(
-                load(vel_ref, 0), load(vel_ref, FLAT), load(vel_ref, 2 * FLAT), load(d_ref, 0)
-            )
+            w = weights(*(load(c_ref, d * FLAT) for d in range(4)))
             v = load(src, ROWS)
             total = w[6] * v + w[0] * load(src, 0) + w[1] * load(src, 2 * ROWS)
             total += jnp.where(sub == 0, 0.0, w[2]) * shifted(v, -1, 1)
@@ -138,20 +130,29 @@
 
         lax.fori_loop(0, NZ // CHUNK, body, 0)
 
+    step(pv_ref, p_ref, ROWS)
+    step(p_ref, q_ref, 0)
+
+
+def steps_kernel(v_ref, vel_hbm, d_hbm, q_ref, keep_ref, coarse_ref, c_ref, p_ref, pv_ref, sems):
+    parts = ((d_hbm, pl.ds(3 * FLAT, FLAT)), (vel_hbm, pl.ds(0, 3 * FLAT)))
+    copies = [
+        pltpu.make_async_copy(src, c_ref.at[at], sems.at[i]) for i, (src, at) in enumerate(parts)
+    ]
+    for copy in copies:
+        copy.start()
     for copy in copies:
         copy.wait()
-    step(pv_ref, p_ref, ROWS)
-    step(p_ref, q_ref, 0)
+    two_steps(v_ref, c_ref, q_ref, p_ref, pv_ref)
     for side, at in enumerate((0, ROWS - 1)):
-        w = weights(*(row(vel_ref, d * FLAT + at) for d in range(3)), row(d_ref, at))
+        w = weights(*(row(c_ref, d * FLAT + at) for d in range(4)))
         for j, value in enumerate((w[0], w[1], w[4], w[5], w[6])):
             keep_ref[(side * 6 + j) * NZ : (side * 6 + j + 1) * NZ] = value
-    keep_ref[5 * NZ : 6 * NZ] = row(d_ref, 1) + jnp.maximum(row(vel_ref, FLAT + 1), 0.0)
-    keep_ref[11 * NZ : 12 * NZ] = row(d_ref, ROWS - 2) - jnp.minimum(row(vel_ref, FLAT + ROWS - 2), 0.0)
-    for d in range(3):
-        sums = restrict_tile(plane_sums(vel_ref.at[d * FLAT : (d + 1) * FLAT]))
-        coarse_ref[d] = sums * (0.5 / 64)
-    coarse_ref[3] = restrict_tile(plane_sums(d_ref)) * (0.125 / 64)
+    keep_ref[5 * NZ : 6 * NZ] = row(c_ref, 3 * FLAT + 1) + jnp.maximum(row(c_ref, FLAT + 1), 0.0)
+    keep_ref[11 * NZ : 12 * NZ] = row(c_ref, 3 * FLAT + ROWS - 2) - jnp.minimum(row(c_ref, FLAT + ROWS - 2), 0.0)
+    for d, factor in enumerate((0.5, 0.5, 0.5, 0.125)):
+        sums = restrict_tile(plane_sums(c_ref.at[d * FLAT : (d + 1) * FLAT]))
+        coarse_ref[d] = sums * (factor / 64)
 
 
 def coarse_weights(c, first, last):
@@ -181,7 +182,7 @@
     )
 
 
-def finish_kernel(parts, bricks, q_ref, mine_pair_ref, mine_cross_ref, pair_ref, cross_ref, keep_ref, coarse_ref, fine_ref, tiles_ref, old_ref):
+def finish_kernel(bricks, q_ref, mine_pair_ref, mine_cross_ref, pair_ref, cross_ref, keep_ref, coarse_ref, fine_ref, message_ref, old_ref, added_ref):
     brick = lax.axis_index("space")
     odd = brick % 2 == 1
     has_low = brick > 0
@@ -207,8 +208,9 @@
         edge += jnp.where(lane == 0, 0.0, wby) * shifted(delta, -1, 1)
         edge += jnp.where(lane == LANES - 1, 0.0, way) * shifted(delta, 1, 1)
         e_at, i_at = (0, 1) if side == 0 else (ROWS - 1, ROWS - 2)
-        fine_ref[pl.ds(e_at, NZ, stride=ROWS), :] = row(q_ref, e_at) + edge
-        fine_ref[pl.ds(i_at, NZ, stride=ROWS), :] = row(q_ref, i_at) + inner * delta
+        for j, (at, extra) in enumerate(((e_at, edge), (i_at, inner * delta))):
+            fine_ref[pl.ds(at, NZ, stride=ROWS), :] = row(q_ref, at) + extra
+            added_ref[(2 * side + j) * NZ : (2 * side + j + 1) * NZ] = extra
     at = slice(3 * NZ, EDGE)
     v = mine_pair_ref[at]
     lower = jnp.where(odd, pair_ref[at], cross_ref[at])
@@ -217,29 +219,33 @@
     old = coarse_apply(w, v, *(shifted(x, 4, 0) for x in (v, lower, upper)))
     old_ref[...] = old
     image = restrict_tile(plane_sums(fine_ref)) * (1.0 / 64)
-    tile = jnp.where(lax.axis_index("tm") == 0, image, image - old)
-    for j in range(parts):
-        tiles_ref[j] = tile
-
-
-def jump_kernel(earlier_ref, start_ref, jump_ref):
-    keep = jnp.where(lax.axis_index("tm") == 0, 0.0, 1.0)
-    jump_ref[...] = keep * (start_ref[...] - earlier_ref[...])
-
-
-def sweep_kernel(bricks, slices, tiles_ref, fine_ref, old_ref, *refs):
-    coarse_refs = refs[:bricks]
-    corrected_ref, change_ref, coef_ref = refs[bricks:]
+    message_ref[0] = jnp.where(lax.axis_index("tm") == 0, image, image - old)
+    message_ref[1:5] = coarse_ref[...]
+
+
+def sweep_kernel(bricks, slices, message_ref, partner_ref, got_ref, swapped_ref, fine_ref, old_ref, earlier_ref, added_ref, start_ref, corrected_ref, jump_ref, change_ref, tiles_ref, coef_ref):
     own, n = lax.axis_index("space"), lax.axis_index("tm")
-    for k, ref in enumerate(coarse_refs):
-        coef_ref[(own + bricks - k) % bricks] = ref[...]
+    chips, chip, core = bricks // 2, own // 2, own % 2
+    coef_ref[own] = message_ref[1:5]
+    coef_ref[2 * chip + 1 - core] = partner_ref[1:5]
+    for ref, c in ((got_ref, core), (swapped_ref, 1 - core)):
+        at = 0
+        for group in range(pl.cdiv(chips, 2)):
+            source = (chip + 2 * chips - 2 * group - c) % chips
+            for k in range(1, slices):
+                for j in range(2):
+                    brick = 2 * source + (c if j == 0 else 1 - c)
+                    tiles_ref[k, brick] = ref[at]
+                    if k == 1:
+                        coef_ref[brick] = ref[at + 1 : at + 5]
+                    at += 5 if k == 1 else 1
     w = [
         coarse_weights(coef_ref.at[b], b == 0, b == bricks - 1)
         for b in range(bricks)
     ]
 
     def coarse_step(m, image):
-        c = [image[b] + tiles_ref[b * slices + m] for b in range(bricks)]
+        c = [image[b] + tiles_ref[n - m, b] for b in range(bricks)]
         half = [shifted(v, 4, 0) for v in c]
         return tuple(
             coarse_apply(w[b], c[b], half[b], half[max(b - 1, 0)], half[min(b + 1, bricks - 1)])
@@ -255,11 +261,16 @@
     for z in range(NZ):
         at = slice(z * ROWS, (z + 1) * ROWS)
         corrected_ref[at] = fine_ref[at] + planes[z // 4]
+    keep = jnp.where(n == 0, 0.0, 1.0)
+    jump_ref[...] = keep * (start_ref[...] - earlier_ref[...])
+    for j, at in enumerate((0, 1, ROWS - 1, ROWS - 2)):
+        extra = added_ref[j * NZ : (j + 1) * NZ]
+        jump_ref[pl.ds(at, NZ, stride=ROWS), :] = row(jump_ref, at) - keep * extra
 
 
 def local(start_states, velocity, diffusivity):
     bricks, slices = lax.axis_size("space"), lax.axis_size("tm")
-    groups, parts = lax.axis_size("groups"), bricks * slices
+    groups = lax.axis_size("groups")
     ring = lambda count, by: [(i, (i + by) % count) for i in range(count)]
     out = lambda *shape: pltpu.VMEM(shape, f32)
     vmem, anyspace = pl.BlockSpec(memory_space=pltpu.VMEM), pl.BlockSpec(memory_space=pl.ANY)
@@ -292,57 +303,78 @@
 
     pair = lax.ppermute(mine_pair, "space", [(i, i ^ 1) for i in range(bricks)])
 
-    q, keep, coarse = pl.pallas_call(
+    start_before = lax.ppermute(v, "tm", ring(slices, 1))
+
+    q, keep, coarse, fields = pl.pallas_call(
         steps_kernel,
         in_specs=[vmem, anyspace, anyspace],
-        out_specs=[vmem] * 3,
-        out_shape=[out(FLAT, LANES), out(12 * NZ, LANES), out(4, ROWS, LANES)],
+        out_specs=[vmem] * 4,
+        out_shape=[
+            out(FLAT, LANES),
+            out(12 * NZ, LANES),
+            out(4, ROWS, LANES),
+            out(4 * FLAT, LANES),
+        ],
         scratch_shapes=[pltpu.VMEM((FLAT + 2 * ROWS, LANES), f32)] * 2
-        + [
-            pltpu.VMEM((3 * FLAT, LANES), f32),
-            pltpu.VMEM((FLAT, LANES), f32),
-            pltpu.SemaphoreType.DMA((2,)),
-        ],
+        + [pltpu.SemaphoreType.DMA((2,))],
         name="steps",
     )(*inside(v), velocity.reshape(3 * FLAT, LANES), diffusivity.reshape(FLAT, LANES))
-    fine, tiles, old = pl.pallas_call(
-        lambda *refs: finish_kernel(parts, bricks, *refs),
+    fine, message, old, added = pl.pallas_call(
+        lambda *refs: finish_kernel(bricks, *refs),
         in_specs=[vmem] * 7,
-        out_specs=[vmem] * 3,
+        out_specs=[vmem] * 4,
         out_shape=[
             out(FLAT, LANES),
-            out(parts, ROWS, LANES),
+            out(5, ROWS, LANES),
             out(ROWS, LANES),
+            out(4 * NZ, LANES),
         ],
         name="finish",
     )(*inside(q, mine_pair, mine_cross, pair, cross, keep, coarse))
 
-    earlier = lax.ppermute(fine, "tm", ring(slices, 1))
-    defects = lax.all_to_all(tiles, ("space", "tm"), 0, 0)
-    coarse_all = [coarse] + [
-        lax.ppermute(coarse, "space", ring(bricks, k)) for k in range(1, bricks)
-    ]
-
-    jump = pl.pallas_call(
-        jump_kernel,
+    chips = bricks // 2
+    swap = [(i, i ^ 1) for i in range(bricks)]
+
+    def send(value, group, k):
+        pairs = []
+        for i in range(bricks):
+            to = 2 * ((i // 2 + 2 * group + i % 2) % chips) + i % 2
+            pairs += [(i * slices + t, to * slices + (t + k) % slices) for t in range(slices)]
+        return lax.ppermute(value, ("space", "tm"), pairs)
+
+    partner = lax.ppermute(message, "space", swap)
+    added = lax.ppermute(added, "tm", ring(slices, 1))
+    earlier = pl.pallas_call(
+        two_steps,
         in_specs=[vmem] * 2,
         out_specs=vmem,
-        out_shape=jax.ShapeDtypeStruct((FLAT, LANES), f32),
-        name="jump",
-    )(*inside(earlier, v))
-    defects, jump = lax.optimization_barrier((defects, jump))
-
-    corrected = pl.pallas_call(
+        out_shape=out(FLAT, LANES),
+        scratch_shapes=[pltpu.VMEM((FLAT + 2 * ROWS, LANES), f32)] * 2,
+        name="steps_before",
+    )(*inside(start_before, fields))
+    both = jnp.concatenate([message, partner])
+    tiles = jnp.stack([message[0], partner[0]])
+    got = [
+        send(both if k == 1 else tiles, group, k)
+        for group in range(pl.cdiv(chips, 2))
+        for k in range(1, slices)
+    ]
+    got[0], earlier = lax.optimization_barrier((got[0], earlier))
+    got = jnp.concatenate(got)
+    swapped = lax.ppermute(got, "space", swap)
+
+    corrected, jump = pl.pallas_call(
         lambda *refs: sweep_kernel(bricks, slices, *refs),
-        in_specs=[vmem] * (bricks + 3),
-        out_specs=vmem,
-        out_shape=jax.ShapeDtypeStruct((FLAT, LANES), f32),
+        in_specs=[vmem] * 9,
+        out_specs=[vmem] * 2,
+        out_shape=[jax.ShapeDtypeStruct((FLAT, LANES), f32)] * 2,
         scratch_shapes=[
             pltpu.VMEM((bricks, ROWS, LANES), f32),
+            pltpu.VMEM((slices, bricks, ROWS, LANES), f32),
             pltpu.VMEM((bricks, 4, ROWS, LANES), f32),
         ],
         name="sweep",
-    )(*inside(defects, fine, old, *coarse_all))
+    )(*inside(message, partner, got, swapped, fine, old, earlier, added, v))
     shape = (1, NZ, ROWS, LANES)
     return corrected.reshape(shape), jump.reshape(shape)
 

time: 22.7 us -> 21.6 us (0.952)
  waiting for transfers between devices: 3.72 us -> 2.24 us
    ppermute x4 -> x7, starting transfers between devices: 4.03 us -> 8.6 us  [the longest x3 5.05 us: send(): return lax.ppermute(value, ('space', 'tm'), pairs)]
    all_to_all x1 -> x0, starting transfers between devices: 4.32 us -> none  [local(): defects = lax.all_to_all(tiles, ('space', 'tm'), 0, 0)]
    all_to_all x1 -> x0, waiting for transfers between devices: 1.5 us -> none  [local(): defects = lax.all_to_all(tiles, ('space', 'tm'), 0, 0)]
    ppermute x4 -> x7, waiting for transfers between devices: 2.21 us -> 2.24 us  [the longest x3 1.25 us: send(): return lax.ppermute(value, ('space', 'tm'), pairs)]
  transfers between devices with their start and end apart: 7 -> 9, of which waited for: 2 -> 3; matrix products, arithmetic and copies ran while one was open for 0% -> 0% of each run, Pallas kernels for 16% -> 22%
where the time goes in v7:
time: 21.6 us; the launch traced here: 21.4 us
  starting transfers between devices  11.7 us (54%)
  Pallas kernels  6.79 us (31%)
  waiting for transfers between devices  2.24 us (10%)
  between operations  0.69 us (3%)
    ppermute x3, starting transfers between devices, send(): return lax.ppermute(value, ('space', 'tm'), pairs)  5.05 us
    pallas_call x1, Pallas kernels, local(): pl.pallas_call(steps_kernel, in_specs=[vmem, anyspace, anyspace], out_spe...  2.88 us
    ppermute x1, starting transfers between devices, local(): cross = lax.ppermute(mine_cross, ('groups', 'space'), list(partner.items()))  2.59 us
    ppermute x1, starting transfers between devices, local(): added = lax.ppermute(added, 'tm', ring(slices, 1))  1.63 us
    ppermute x1, starting transfers between devices, local(): start_before = lax.ppermute(v, 'tm', ring(slices, 1))  1.58 us
    pallas_call x1, Pallas kernels, local(): pl.pallas_call(two_steps, in_specs=[vmem] * 2, out_specs=vmem, out_shape=...  1.42 us
    ppermute x3, waiting for transfers between devices, send(): return lax.ppermute(value, ('space', 'tm'), pairs)  1.25 us
    pallas_call x1, Pallas kernels, local(): pl.pallas_call(edges_kernel, in_specs=[anyspace] * 3, out_specs=[vmem] *...  1.21 us
  transfers between devices with their start and end apart: 9, of which 3 were waited for; matrix products, arithmetic and copies ran while one was open for 0% of the time, Pallas kernels for 22%

profile of v7, /device:TPU:0, one launch (start us, length us, event | category | flops | bytes accessed | tf_op | source)
XLA Modules:
  0.0 21.4 jit_solution(8701048053781434992)
XLA Ops:
  0.6 1.2 %edges.1 = (f32[512,128]{1,0:T(8,128)S(1)}, f32[200,128]{1,0:T(8,128)S(1)}, f32[200,128]{1,0:T(8,128)S(1)}) custom-call(f32[512,128]{1,0:T(8,128)} %bitcast.7, f32[3,64,8,128]{3,2,1,0:T(8,128)} %vel_hbm.1, f32[64,8,128]{2,1,0:T(8,128)} %d_hbm.1), custom_call_target="tpu_custom_call" | custom-call | tf_op jit(solution)/shard_map/edges/pallas_call | solution.py:279
  1.8 0.5 %collective-permute-start = (f32[200,128]{1,0:T(8,128)S(1)}, f32[200,128]{1,0:T(8,128)S(1)}, u32[]{:S(2)}, u32[]{:S(2)}) collective-permute-start(f32[200,128]{1,0:T(8,128)S(1)} %get-tuple-element.19.refs_1_), channel_id=1, source_target_pairs={{0,4},{4,0},{8,12},{12,8},{1,5},{5,1},{9,13},{13,9},{2,6},{6,2},{1... | collective-permute-start | bytes 307208 | tf_op jit(solution)/shard_map/ppermute | solution.py:304
  2.4 2.6 %collective-permute-start.1 = (f32[200,128]{1,0:T(8,128)S(1)}, f32[200,128]{1,0:T(8,128)S(1)}, u32[]{:S(2)}, u32[]{:S(2)}) collective-permute-start(f32[200,128]{1,0:T(8,128)S(1)} %get-tuple-element.20.refs_2_), channel_id=1, source_target_pairs={{0,16},{4,8},{8,4},{12,28},{16,0},{20,24},{24,20},{28,12},{1,17},{... | collective-permute-start | bytes 307208 | tf_op jit(solution)/shard_map/ppermute | solution.py:302
  5.0 1.6 %collective-permute-start.4 = (f32[512,128]{1,0:T(8,128)S(1)}, f32[512,128]{1,0:T(8,128)S(1)}, u32[]{:S(2)}, u32[]{:S(2)}) collective-permute-start(f32[512,128]{1,0:T(8,128)S(1)} %get-tuple-element.17.v_ref.refs_8_), channel_id=1, source_target_pairs={{0,1},{1,2},{2,3},{3,0},{4,5},{5,6},{6,7},{7,4},{8,9},{9,10},{10,1... | collective-permute-start | bytes 786440 | tf_op jit(solution)/shard_map/ppermute | solution.py:306
  6.5 2.9 %steps.1 = (f32[512,128]{1,0:T(8,128)S(1)}, f32[768,128]{1,0:T(8,128)S(1)}, f32[4,8,128]{2,1,0:T(8,128)S(1)}, f32[2048,128]{1,0:T(8,128)S(1)}) custom-call(f32[512,128]{1,0:T(8,128)S(1)} %get-tuple-element.17.v_ref.refs_8_, f32[1536,128]{1,0:T(8,128)} %bitcast.5, f32[512,128]{1,0:T(8,128)} %bitcast.6), custom_call_target="tpu_custom_call" | custom-call | tf_op jit(solution)/shard_map/steps/pallas_call | solution.py:308
  9.4 0.0 collective-permute-done.refs_3_
  9.4 0.0 collective-permute-done.1.refs_4_
  9.4 0.3 %finish.1 = (f32[512,128]{1,0:T(8,128)S(1)}, f32[5,8,128]{2,1,0:T(8,128)S(1)}, f32[8,128]{1,0:T(8,128)S(1)}, f32[256,128]{1,0:T(8,128)S(1)}) custom-call(f32[512,128]{1,0:T(8,128)S(1)} %get-tuple-element.18.refs_0_, f32[200,128]{1,0:T(8,128)S(1)} %get-tuple-element.19.refs_1_, f32[200,128]{1,0:T(8,128)S(1)} %get-tuple-element.20.refs_2_, ...), custom_call_target="tpu_custom_call" | custom-call | tf_op jit(solution)/shard_map/finish/pallas_call | solution.py:322
  9.8 0.0 collective-permute-start.2
  9.8 1.6 %collective-permute-start.8 = (f32[256,128]{1,0:T(8,128)S(1)}, f32[256,128]{1,0:T(8,128)S(1)}, u32[]{:S(2)}, u32[]{:S(2)}) collective-permute-start(f32[256,128]{1,0:T(8,128)S(1)} %get-tuple-element.29), channel_id=1, source_target_pairs={{0,1},{1,2},{2,3},{3,0},{4,5},{5,6},{6,7},{7,4},{8,9},{9,10},{10,1... | collective-permute-start | bytes 393224 | tf_op jit(solution)/shard_map/ppermute | solution.py:346
  11.4 0.0 collective-permute-done.2.refs_1_
  11.4 1.6 %collective-permute-start.3 = (f32[10,8,128]{2,1,0:T(8,128)S(1)}, f32[10,8,128]{2,1,0:T(8,128)S(1)}, u32[]{:S(2)}, u32[]{:S(2)}) collective-permute-start(f32[10,8,128]{2,1,0:T(8,128)S(1)} %pad_maximum_fusion), channel_id=1, source_target_pairs={{0,1},{1,2},{2,3},{3,0},{4,13},{5,14},{6,15},{7,12},{8,9},{9,10},{... | collective-permute-start | bytes 122888 | tf_op jit(solution)/shard_map/ppermute | solution.py:343
  13.0 1.2 %collective-permute-start.5 = (f32[2,8,128]{2,1,0:T(8,128)S(1)}, f32[2,8,128]{2,1,0:T(8,128)S(1)}, u32[]{:S(2)}, u32[]{:S(2)}) collective-permute-start(f32[2,8,128]{2,1,0:T(8,128)S(1)} %pad_maximum_fusion.1), channel_id=1, source_target_pairs={{0,2},{1,3},{2,0},{3,1},{4,14},{5,15},{6,12},{7,13},{8,10},{9,11},... | collective-permute-start | bytes 24584 | tf_op jit(solution)/shard_map/ppermute | solution.py:343
  14.2 2.2 %collective-permute-start.6 = (f32[2,8,128]{2,1,0:T(8,128)S(1)}, f32[2,8,128]{2,1,0:T(8,128)S(1)}, u32[]{:S(2)}, u32[]{:S(2)}) collective-permute-start(f32[2,8,128]{2,1,0:T(8,128)S(1)} %pad_maximum_fusion.1), channel_id=1, source_target_pairs={{0,3},{1,0},{2,1},{3,2},{4,15},{5,12},{6,13},{7,14},{8,11},{9,8},{... | collective-permute-start | bytes 24584 | tf_op jit(solution)/shard_map/ppermute | solution.py:343
  16.5 0.0 collective-permute-done.4.v_ref
  16.5 1.4 %steps_before.1.refs_6_ = f32[512,128]{1,0:T(8,128)S(1)} custom-call(f32[512,128]{1,0:T(8,128)S(1)} %collective-permute-done.4.v_ref, f32[2048,128]{1,0:T(8,128)S(1)} %get-tuple-element.24.c_ref), custom_call_target="tpu_custom_call" | custom-call | tf_op jit(solution)/shard_map/steps_before/pallas_call | solution.py:347
  17.9 1.1 %collective-permute-done.3 = f32[10,8,128]{2,1,0:T(8,128)S(1)} collective-permute-done((f32[10,8,128]{2,1,0:T(8,128)S(1)}, f32[10,8,128]{2,1,0:T(8,128)S(1)}, u32[]{:S(2)}, u32[]{:S(2)}) %collective-permute-start.3) | collective-permute-done | bytes 40992 | tf_op jit(solution)/shard_map/ppermute | solution.py:343
  19.0 0.2 collective-permute-done.5
  19.2 0.0 collective-permute-done.6
  19.2 0.3 %collective-permute-start.7 = (f32[14,8,128]{2,1,0:T(8,128)S(1)}, f32[14,8,128]{2,1,0:T(8,128)S(1)}, u32[]{:S(2)}, u32[]{:S(2)}) collective-permute-start(f32[14,8,128]{2,1,0:T(8,128)S(1)} %constant_dynamic-update-slice_fusion.refs_2_), channel_id=1, source_target_pairs={{0,4},{4,0},{8,12},{12,8},{1,5},{5,1},{9,13},{13,9},{2,6},{6,2},{1... | collective-permute-start | bytes 172040 | tf_op jit(solution)/shard_map/ppermute | solution.py:364
  19.5 0.0 collective-permute-done.8.refs_7_
  19.5 1.0 %collective-permute-done.7.refs_3_ = f32[14,8,128]{2,1,0:T(8,128)S(1)} collective-permute-done((f32[14,8,128]{2,1,0:T(8,128)S(1)}, f32[14,8,128]{2,1,0:T(8,128)S(1)}, u32[]{:S(2)}, u32[]{:S(2)}) %collective-permute-start.7) | collective-permute-done | bytes 57376 | tf_op jit(solution)/shard_map/ppermute | solution.py:364
  20.5 1.0 %sweep.1 = (f32[512,128]{1,0:T(8,128)}, f32[512,128]{1,0:T(8,128)}) custom-call(f32[5,8,128]{2,1,0:T(8,128)S(1)} %get-tuple-element.23.refs_0_, f32[5,8,128]{2,1,0:T(8,128)S(1)} %collective-permute-done.2.refs_1_, f32[14,8,128]{2,1,0:T(8,128)S(1)} %constant_dynamic-update-slice_fusion.refs_2_, f32[14,8,128]{2,1,0:T(8,128)S(1)} %collective-permute-done.7.refs_3_, ...), custom_call_target="tpu_custom_call" | custom-call | tf_op jit(solution)/shard_map/sweep/pallas_call | solution.py:366
  (7 shorter events, 0.0 us)
Async XLA Ops:
  1.8 7.6 %collective-permute-start = (f32[200,128]{1,0:T(8,128)S(1)}, f32[200,128]{1,0:T(8,128)S(1)}, u32[]{:S(2)}, u32[]{:S(2)}) collective-permute-start(f32[200,128]{1,0:T(8,128)S(1)} %get-tuple-element.19.refs_1_), channel_id=1, source_target_pairs={{0,4},{4,0},{8,12},{12,8},{1,5},{5,1},{9,13},{13,9},{2,6},{6,2},{1... | collective-permute-start | bytes 307208 | tf_op jit(solution)/shard_map/ppermute | solution.py:304
  2.4 7.1 %collective-permute-start.1 = (f32[200,128]{1,0:T(8,128)S(1)}, f32[200,128]{1,0:T(8,128)S(1)}, u32[]{:S(2)}, u32[]{:S(2)}) collective-permute-start(f32[200,128]{1,0:T(8,128)S(1)} %get-tuple-element.20.refs_2_), channel_id=1, source_target_pairs={{0,16},{4,8},{8,4},{12,28},{16,0},{20,24},{24,20},{28,12},{1,17},{... | collective-permute-start | bytes 307208 | tf_op jit(solution)/shard_map/ppermute | solution.py:302
  5.0 11.5 %collective-permute-start.4 = (f32[512,128]{1,0:T(8,128)S(1)}, f32[512,128]{1,0:T(8,128)S(1)}, u32[]{:S(2)}, u32[]{:S(2)}) collective-permute-start(f32[512,128]{1,0:T(8,128)S(1)} %get-tuple-element.17.v_ref.refs_8_), channel_id=1, source_target_pairs={{0,1},{1,2},{2,3},{3,0},{4,5},{5,6},{6,7},{7,4},{8,9},{9,10},{10,1... | collective-permute-start | bytes 786440 | tf_op jit(solution)/shard_map/ppermute | solution.py:306
  9.8 1.7 %collective-permute-start.2 = (f32[5,8,128]{2,1,0:T(8,128)S(1)}, f32[5,8,128]{2,1,0:T(8,128)S(1)}, u32[]{:S(2)}, u32[]{:S(2)}) collective-permute-start(f32[5,8,128]{2,1,0:T(8,128)S(1)} %get-tuple-element.23.refs_0_), channel_id=1, source_target_pairs={{0,4},{4,0},{8,12},{12,8},{1,5},{5,1},{9,13},{13,9},{2,6},{6,2},{1... | collective-permute-start | bytes 61448 | tf_op jit(solution)/shard_map/ppermute | solution.py:345
  9.8 9.7 %collective-permute-start.8 = (f32[256,128]{1,0:T(8,128)S(1)}, f32[256,128]{1,0:T(8,128)S(1)}, u32[]{:S(2)}, u32[]{:S(2)}) collective-permute-start(f32[256,128]{1,0:T(8,128)S(1)} %get-tuple-element.29), channel_id=1, source_target_pairs={{0,1},{1,2},{2,3},{3,0},{4,5},{5,6},{6,7},{7,4},{8,9},{9,10},{10,1... | collective-permute-start | bytes 393224 | tf_op jit(solution)/shard_map/ppermute | solution.py:346
  11.4 7.6 %collective-permute-start.3 = (f32[10,8,128]{2,1,0:T(8,128)S(1)}, f32[10,8,128]{2,1,0:T(8,128)S(1)}, u32[]{:S(2)}, u32[]{:S(2)}) collective-permute-start(f32[10,8,128]{2,1,0:T(8,128)S(1)} %pad_maximum_fusion), channel_id=1, source_target_pairs={{0,1},{1,2},{2,3},{3,0},{4,13},{5,14},{6,15},{7,12},{8,9},{9,10},{... | collective-permute-start | bytes 122888 | tf_op jit(solution)/shard_map/ppermute | solution.py:343
  13.0 6.2 %collective-permute-start.5 = (f32[2,8,128]{2,1,0:T(8,128)S(1)}, f32[2,8,128]{2,1,0:T(8,128)S(1)}, u32[]{:S(2)}, u32[]{:S(2)}) collective-permute-start(f32[2,8,128]{2,1,0:T(8,128)S(1)} %pad_maximum_fusion.1), channel_id=1, source_target_pairs={{0,2},{1,3},{2,0},{3,1},{4,14},{5,15},{6,12},{7,13},{8,10},{9,11},... | collective-permute-start | bytes 24584 | tf_op jit(solution)/shard_map/ppermute | solution.py:343
  14.2 4.9 %collective-permute-start.6 = (f32[2,8,128]{2,1,0:T(8,128)S(1)}, f32[2,8,128]{2,1,0:T(8,128)S(1)}, u32[]{:S(2)}, u32[]{:S(2)}) collective-permute-start(f32[2,8,128]{2,1,0:T(8,128)S(1)} %pad_maximum_fusion.1), channel_id=1, source_target_pairs={{0,3},{1,0},{2,1},{3,2},{4,15},{5,12},{6,13},{7,14},{8,11},{9,8},{... | collective-permute-start | bytes 24584 | tf_op jit(solution)/shard_map/ppermute | solution.py:343
  19.2 1.3 %collective-permute-start.7 = (f32[14,8,128]{2,1,0:T(8,128)S(1)}, f32[14,8,128]{2,1,0:T(8,128)S(1)}, u32[]{:S(2)}, u32[]{:S(2)}) collective-permute-start(f32[14,8,128]{2,1,0:T(8,128)S(1)} %constant_dynamic-update-slice_fusion.refs_2_), channel_id=1, source_target_pairs={{0,4},{4,0},{8,12},{12,8},{1,5},{5,1},{9,13},{13,9},{2,6},{6,2},{1... | collective-permute-start | bytes 172040 | tf_op jit(solution)/shard_map/ppermute | solution.py:364

commit v8 on v7

--- a/solution.py
+++ b/solution.py
@@ -104,7 +104,7 @@
         cross_ref[j * NZ : (j + 1) * NZ] = jnp.where(odd, high, low)
 
 
-def two_steps(v_ref, c_ref, q_ref, p_ref, pv_ref):
+def two_steps(v_ref, c_ref, q_ref, p_ref, pv_ref, waits=()):
     zero = jnp.zeros((ROWS, LANES), f32)
     for ref in (p_ref, pv_ref):
         ref[0:ROWS] = zero
@@ -128,22 +128,31 @@
             dst[pl.ds(at + dst_off, size), :] = total.reshape(size, LANES)
             return carry
 
-        lax.fori_loop(0, NZ // CHUNK, body, 0)
-
-    step(pv_ref, p_ref, ROWS)
-    step(p_ref, q_ref, 0)
+        return lambda first, last: lax.fori_loop(first, last, body, 0)
+
+    chunks = NZ // CHUNK
+    first_step = step(pv_ref, p_ref, ROWS)
+    for half, copies in enumerate(waits or ((), ())):
+        for copy in copies:
+            copy.wait()
+        first_step(half * chunks // 2, (half + 1) * chunks // 2)
+    step(p_ref, q_ref, 0)(0, chunks)
 
 
 def steps_kernel(v_ref, vel_hbm, d_hbm, q_ref, keep_ref, coarse_ref, c_ref, p_ref, pv_ref, sems):
-    parts = ((d_hbm, pl.ds(3 * FLAT, FLAT)), (vel_hbm, pl.ds(0, 3 * FLAT)))
-    copies = [
-        pltpu.make_async_copy(src, c_ref.at[at], sems.at[i]) for i, (src, at) in enumerate(parts)
-    ]
+    copies = []
+    for half in range(2):
+        for d in range(4):
+            src, at = (vel_hbm, d * FLAT) if d < 3 else (d_hbm, 0)
+            at, to = at + half * FLAT // 2, d * FLAT + half * FLAT // 2
+            copies.append(
+                pltpu.make_async_copy(
+                    src.at[pl.ds(at, FLAT // 2)], c_ref.at[pl.ds(to, FLAT // 2)], sems.at[4 * half + d]
+                )
+            )
     for copy in copies:
         copy.start()
-    for copy in copies:
-        copy.wait()
-    two_steps(v_ref, c_ref, q_ref, p_ref, pv_ref)
+    two_steps(v_ref, c_ref, q_ref, p_ref, pv_ref, (copies[:4], copies[4:]))
     for side, at in enumerate((0, ROWS - 1)):
         w = weights(*(row(c_ref, d * FLAT + at) for d in range(4)))
         for j, value in enumerate((w[0], w[1], w[4], w[5], w[6])):
@@ -236,9 +245,9 @@
                 for j in range(2):
                     brick = 2 * source + (c if j == 0 else 1 - c)
                     tiles_ref[k, brick] = ref[at]
-                    if k == 1:
+                    if k == slices - 1:
                         coef_ref[brick] = ref[at + 1 : at + 5]
-                    at += 5 if k == 1 else 1
+                    at += 5 if k == slices - 1 else 1
     w = [
         coarse_weights(coef_ref.at[b], b == 0, b == bricks - 1)
         for b in range(bricks)
@@ -316,7 +325,7 @@
             out(4 * FLAT, LANES),
         ],
         scratch_shapes=[pltpu.VMEM((FLAT + 2 * ROWS, LANES), f32)] * 2
-        + [pltpu.SemaphoreType.DMA((2,))],
+        + [pltpu.SemaphoreType.DMA((8,))],
         name="steps",
     )(*inside(v), velocity.reshape(3 * FLAT, LANES), diffusivity.reshape(FLAT, LANES))
     fine, message, old, added = pl.pallas_call(
@@ -355,7 +364,7 @@
     both = jnp.concatenate([message, partner])
     tiles = jnp.stack([message[0], partner[0]])
     got = [
-        send(both if k == 1 else tiles, group, k)
+        send(both if k == slices - 1 else tiles, group, k)
         for group in range(pl.cdiv(chips, 2))
         for k in range(1, slices)
     ]

time: 21.6 us -> 21.5 us (level)
  transfers between devices with their start and end apart: 9 -> 9, of which waited for: 3 -> 4; matrix products, arithmetic and copies ran while one was open for 0% -> 0% of each run, Pallas kernels for 22% -> 21%
where the time goes in v8:
time: 21.5 us; the launch traced here: 21.4 us
  starting transfers between devices  11.8 us (55%)
  Pallas kernels  6.68 us (31%)
  waiting for transfers between devices  2.24 us (10%)
  between operations  0.69 us (3%)
    ppermute x3, starting transfers between devices, send(): return lax.ppermute(value, ('space', 'tm'), pairs)  5.05 us
    pallas_call x1, Pallas kernels, local(): pl.pallas_call(steps_kernel, in_specs=[vmem, anyspace, anyspace], out_spe...  2.79 us
    ppermute x1, starting transfers between devices, local(): cross = lax.ppermute(mine_cross, ('groups', 'space'), list(partner.items()))  2.59 us
    ppermute x1, starting transfers between devices, local(): added = lax.ppermute(added, 'tm', ring(slices, 1))  1.63 us
    ppermute x1, starting transfers between devices, local(): start_before = lax.ppermute(v, 'tm', ring(slices, 1))  1.58 us
    pallas_call x1, Pallas kernels, local(): pl.pallas_call(two_steps, in_specs=[vmem] * 2, out_specs=vmem, out_shape=...  1.41 us
    ppermute x3, waiting for transfers between devices, send(): return lax.ppermute(value, ('space', 'tm'), pairs)  1.34 us
    pallas_call x1, Pallas kernels, local(): pl.pallas_call(edges_kernel, in_specs=[anyspace] * 3, out_specs=[vmem] *...  1.21 us
  transfers between devices with their start and end apart: 9, of which 4 were waited for; matrix products, arithmetic and copies ran while one was open for 0% of the time, Pallas kernels for 21%

profile of v8, /device:TPU:0, one launch (start us, length us, event | category | flops | bytes accessed | tf_op | source)
XLA Modules:
  0.0 21.4 jit_solution(4696851376715071867)
XLA Ops:
  0.6 1.2 %edges.1 = (f32[512,128]{1,0:T(8,128)S(1)}, f32[200,128]{1,0:T(8,128)S(1)}, f32[200,128]{1,0:T(8,128)S(1)}) custom-call(f32[512,128]{1,0:T(8,128)} %bitcast.7, f32[3,64,8,128]{3,2,1,0:T(8,128)} %vel_hbm.1, f32[64,8,128]{2,1,0:T(8,128)} %d_hbm.1), custom_call_target="tpu_custom_call" | custom-call | tf_op jit(solution)/shard_map/edges/pallas_call | solution.py:288
  1.8 0.5 %collective-permute-start = (f32[200,128]{1,0:T(8,128)S(1)}, f32[200,128]{1,0:T(8,128)S(1)}, u32[]{:S(2)}, u32[]{:S(2)}) collective-permute-start(f32[200,128]{1,0:T(8,128)S(1)} %get-tuple-element.19.refs_1_), channel_id=1, source_target_pairs={{0,4},{4,0},{8,12},{12,8},{1,5},{5,1},{9,13},{13,9},{2,6},{6,2},{1... | collective-permute-start | bytes 307208 | tf_op jit(solution)/shard_map/ppermute | solution.py:313
  2.4 2.6 %collective-permute-start.1 = (f32[200,128]{1,0:T(8,128)S(1)}, f32[200,128]{1,0:T(8,128)S(1)}, u32[]{:S(2)}, u32[]{:S(2)}) collective-permute-start(f32[200,128]{1,0:T(8,128)S(1)} %get-tuple-element.20.refs_2_), channel_id=1, source_target_pairs={{0,16},{4,8},{8,4},{12,28},{16,0},{20,24},{24,20},{28,12},{1,17},{... | collective-permute-start | bytes 307208 | tf_op jit(solution)/shard_map/ppermute | solution.py:311
  5.0 1.6 %collective-permute-start.4 = (f32[512,128]{1,0:T(8,128)S(1)}, f32[512,128]{1,0:T(8,128)S(1)}, u32[]{:S(2)}, u32[]{:S(2)}) collective-permute-start(f32[512,128]{1,0:T(8,128)S(1)} %get-tuple-element.17.v_ref.refs_8_), channel_id=1, source_target_pairs={{0,1},{1,2},{2,3},{3,0},{4,5},{5,6},{6,7},{7,4},{8,9},{9,10},{10,1... | collective-permute-start | bytes 786440 | tf_op jit(solution)/shard_map/ppermute | solution.py:315
  6.5 2.8 %steps.1 = (f32[512,128]{1,0:T(8,128)S(1)}, f32[768,128]{1,0:T(8,128)S(1)}, f32[4,8,128]{2,1,0:T(8,128)S(1)}, f32[2048,128]{1,0:T(8,128)S(1)}) custom-call(f32[512,128]{1,0:T(8,128)S(1)} %get-tuple-element.17.v_ref.refs_8_, f32[1536,128]{1,0:T(8,128)} %bitcast.5, f32[512,128]{1,0:T(8,128)} %bitcast.6), custom_call_target="tpu_custom_call" | custom-call | tf_op jit(solution)/shard_map/steps/pallas_call | solution.py:317
  9.3 0.0 collective-permute-done.refs_3_
  9.3 0.0 collective-permute-done.1.refs_4_
  9.3 0.3 %finish.1 = (f32[512,128]{1,0:T(8,128)S(1)}, f32[5,8,128]{2,1,0:T(8,128)S(1)}, f32[8,128]{1,0:T(8,128)S(1)}, f32[256,128]{1,0:T(8,128)S(1)}) custom-call(f32[512,128]{1,0:T(8,128)S(1)} %get-tuple-element.18.refs_0_, f32[200,128]{1,0:T(8,128)S(1)} %get-tuple-element.19.refs_1_, f32[200,128]{1,0:T(8,128)S(1)} %get-tuple-element.20.refs_2_, ...), custom_call_target="tpu_custom_call" | custom-call | tf_op jit(solution)/shard_map/finish/pallas_call | solution.py:331
  9.7 0.0 collective-permute-start.2
  9.7 1.6 %collective-permute-start.8 = (f32[256,128]{1,0:T(8,128)S(1)}, f32[256,128]{1,0:T(8,128)S(1)}, u32[]{:S(2)}, u32[]{:S(2)}) collective-permute-start(f32[256,128]{1,0:T(8,128)S(1)} %get-tuple-element.29), channel_id=1, source_target_pairs={{0,1},{1,2},{2,3},{3,0},{4,5},{5,6},{6,7},{7,4},{8,9},{9,10},{10,1... | collective-permute-start | bytes 393224 | tf_op jit(solution)/shard_map/ppermute | solution.py:355
  11.3 0.0 collective-permute-done.2.refs_1_
  11.3 1.6 %collective-permute-start.3 = (f32[2,8,128]{2,1,0:T(8,128)S(1)}, f32[2,8,128]{2,1,0:T(8,128)S(1)}, u32[]{:S(2)}, u32[]{:S(2)}) collective-permute-start(f32[2,8,128]{2,1,0:T(8,128)S(1)} %pad_maximum_fusion.1), channel_id=1, source_target_pairs={{0,1},{1,2},{2,3},{3,0},{4,13},{5,14},{6,15},{7,12},{8,9},{9,10},{... | collective-permute-start | bytes 24584 | tf_op jit(solution)/shard_map/ppermute | solution.py:352
  13.0 1.2 %collective-permute-start.5 = (f32[2,8,128]{2,1,0:T(8,128)S(1)}, f32[2,8,128]{2,1,0:T(8,128)S(1)}, u32[]{:S(2)}, u32[]{:S(2)}) collective-permute-start(f32[2,8,128]{2,1,0:T(8,128)S(1)} %pad_maximum_fusion.1), channel_id=1, source_target_pairs={{0,2},{1,3},{2,0},{3,1},{4,14},{5,15},{6,12},{7,13},{8,10},{9,11},... | collective-permute-start | bytes 24584 | tf_op jit(solution)/shard_map/ppermute | solution.py:352
  14.2 2.2 %collective-permute-start.6 = (f32[10,8,128]{2,1,0:T(8,128)S(1)}, f32[10,8,128]{2,1,0:T(8,128)S(1)}, u32[]{:S(2)}, u32[]{:S(2)}) collective-permute-start(f32[10,8,128]{2,1,0:T(8,128)S(1)} %pad_maximum_fusion), channel_id=1, source_target_pairs={{0,3},{1,0},{2,1},{3,2},{4,15},{5,12},{6,13},{7,14},{8,11},{9,8},{... | collective-permute-start | bytes 122888 | tf_op jit(solution)/shard_map/ppermute | solution.py:352
  16.4 0.0 collective-permute-done.4.v_ref
  16.4 1.4 %steps_before.1.refs_6_ = f32[512,128]{1,0:T(8,128)S(1)} custom-call(f32[512,128]{1,0:T(8,128)S(1)} %collective-permute-done.4.v_ref, f32[2048,128]{1,0:T(8,128)S(1)} %get-tuple-element.24.c_ref), custom_call_target="tpu_custom_call" | custom-call | tf_op jit(solution)/shard_map/steps_before/pallas_call | solution.py:356
  17.8 0.5 %collective-permute-done.3 = f32[2,8,128]{2,1,0:T(8,128)S(1)} collective-permute-done((f32[2,8,128]{2,1,0:T(8,128)S(1)}, f32[2,8,128]{2,1,0:T(8,128)S(1)}, u32[]{:S(2)}, u32[]{:S(2)}) %collective-permute-start.3) | collective-permute-done | bytes 8224 | tf_op jit(solution)/shard_map/ppermute | solution.py:352
  18.3 0.2 collective-permute-done.5
  18.5 0.7 %collective-permute-done.6 = f32[10,8,128]{2,1,0:T(8,128)S(1)} collective-permute-done((f32[10,8,128]{2,1,0:T(8,128)S(1)}, f32[10,8,128]{2,1,0:T(8,128)S(1)}, u32[]{:S(2)}, u32[]{:S(2)}) %collective-permute-start.6) | collective-permute-done | bytes 40992 | tf_op jit(solution)/shard_map/ppermute | solution.py:352
  19.2 0.4 %collective-permute-start.7 = (f32[14,8,128]{2,1,0:T(8,128)S(1)}, f32[14,8,128]{2,1,0:T(8,128)S(1)}, u32[]{:S(2)}, u32[]{:S(2)}) collective-permute-start(f32[14,8,128]{2,1,0:T(8,128)S(1)} %constant_dynamic-update-slice_fusion.refs_2_), channel_id=1, source_target_pairs={{0,4},{4,0},{8,12},{12,8},{1,5},{5,1},{9,13},{13,9},{2,6},{6,2},{1... | collective-permute-start | bytes 172040 | tf_op jit(solution)/shard_map/ppermute | solution.py:373
  19.5 0.0 collective-permute-done.8.refs_7_
  19.5 0.9 %collective-permute-done.7.refs_3_ = f32[14,8,128]{2,1,0:T(8,128)S(1)} collective-permute-done((f32[14,8,128]{2,1,0:T(8,128)S(1)}, f32[14,8,128]{2,1,0:T(8,128)S(1)}, u32[]{:S(2)}, u32[]{:S(2)}) %collective-permute-start.7) | collective-permute-done | bytes 57376 | tf_op jit(solution)/shard_map/ppermute | solution.py:373
  20.4 1.0 %sweep.1 = (f32[512,128]{1,0:T(8,128)}, f32[512,128]{1,0:T(8,128)}) custom-call(f32[5,8,128]{2,1,0:T(8,128)S(1)} %get-tuple-element.23.refs_0_, f32[5,8,128]{2,1,0:T(8,128)S(1)} %collective-permute-done.2.refs_1_, f32[14,8,128]{2,1,0:T(8,128)S(1)} %constant_dynamic-update-slice_fusion.refs_2_, f32[14,8,128]{2,1,0:T(8,128)S(1)} %collective-permute-done.7.refs_3_, ...), custom_call_target="tpu_custom_call" | custom-call | tf_op jit(solution)/shard_map/sweep/pallas_call | solution.py:375
  (7 shorter events, 0.0 us)
Async XLA Ops:
  1.8 7.5 %collective-permute-start = (f32[200,128]{1,0:T(8,128)S(1)}, f32[200,128]{1,0:T(8,128)S(1)}, u32[]{:S(2)}, u32[]{:S(2)}) collective-permute-start(f32[200,128]{1,0:T(8,128)S(1)} %get-tuple-element.19.refs_1_), channel_id=1, source_target_pairs={{0,4},{4,0},{8,12},{12,8},{1,5},{5,1},{9,13},{13,9},{2,6},{6,2},{1... | collective-permute-start | bytes 307208 | tf_op jit(solution)/shard_map/ppermute | solution.py:313
  2.4 7.0 %collective-permute-start.1 = (f32[200,128]{1,0:T(8,128)S(1)}, f32[200,128]{1,0:T(8,128)S(1)}, u32[]{:S(2)}, u32[]{:S(2)}) collective-permute-start(f32[200,128]{1,0:T(8,128)S(1)} %get-tuple-element.20.refs_2_), channel_id=1, source_target_pairs={{0,16},{4,8},{8,4},{12,28},{16,0},{20,24},{24,20},{28,12},{1,17},{... | collective-permute-start | bytes 307208 | tf_op jit(solution)/shard_map/ppermute | solution.py:311
  5.0 11.4 %collective-permute-start.4 = (f32[512,128]{1,0:T(8,128)S(1)}, f32[512,128]{1,0:T(8,128)S(1)}, u32[]{:S(2)}, u32[]{:S(2)}) collective-permute-start(f32[512,128]{1,0:T(8,128)S(1)} %get-tuple-element.17.v_ref.refs_8_), channel_id=1, source_target_pairs={{0,1},{1,2},{2,3},{3,0},{4,5},{5,6},{6,7},{7,4},{8,9},{9,10},{10,1... | collective-permute-start | bytes 786440 | tf_op jit(solution)/shard_map/ppermute | solution.py:315
  9.7 1.7 %collective-permute-start.2 = (f32[5,8,128]{2,1,0:T(8,128)S(1)}, f32[5,8,128]{2,1,0:T(8,128)S(1)}, u32[]{:S(2)}, u32[]{:S(2)}) collective-permute-start(f32[5,8,128]{2,1,0:T(8,128)S(1)} %get-tuple-element.23.refs_0_), channel_id=1, source_target_pairs={{0,4},{4,0},{8,12},{12,8},{1,5},{5,1},{9,13},{13,9},{2,6},{6,2},{1... | collective-permute-start | bytes 61448 | tf_op jit(solution)/shard_map/ppermute | solution.py:354
  9.7 9.8 %collective-permute-start.8 = (f32[256,128]{1,0:T(8,128)S(1)}, f32[256,128]{1,0:T(8,128)S(1)}, u32[]{:S(2)}, u32[]{:S(2)}) collective-permute-start(f32[256,128]{1,0:T(8,128)S(1)} %get-tuple-element.29), channel_id=1, source_target_pairs={{0,1},{1,2},{2,3},{3,0},{4,5},{5,6},{6,7},{7,4},{8,9},{9,10},{10,1... | collective-permute-start | bytes 393224 | tf_op jit(solution)/shard_map/ppermute | solution.py:355
  11.3 7.0 %collective-permute-start.3 = (f32[2,8,128]{2,1,0:T(8,128)S(1)}, f32[2,8,128]{2,1,0:T(8,128)S(1)}, u32[]{:S(2)}, u32[]{:S(2)}) collective-permute-start(f32[2,8,128]{2,1,0:T(8,128)S(1)} %pad_maximum_fusion.1), channel_id=1, source_target_pairs={{0,1},{1,2},{2,3},{3,0},{4,13},{5,14},{6,15},{7,12},{8,9},{9,10},{... | collective-permute-start | bytes 24584 | tf_op jit(solution)/shard_map/ppermute | solution.py:352
  13.0 5.5 %collective-permute-start.5 = (f32[2,8,128]{2,1,0:T(8,128)S(1)}, f32[2,8,128]{2,1,0:T(8,128)S(1)}, u32[]{:S(2)}, u32[]{:S(2)}) collective-permute-start(f32[2,8,128]{2,1,0:T(8,128)S(1)} %pad_maximum_fusion.1), channel_id=1, source_target_pairs={{0,2},{1,3},{2,0},{3,1},{4,14},{5,15},{6,12},{7,13},{8,10},{9,11},... | collective-permute-start | bytes 24584 | tf_op jit(solution)/shard_map/ppermute | solution.py:352
  14.2 5.0 %collective-permute-start.6 = (f32[10,8,128]{2,1,0:T(8,128)S(1)}, f32[10,8,128]{2,1,0:T(8,128)S(1)}, u32[]{:S(2)}, u32[]{:S(2)}) collective-permute-start(f32[10,8,128]{2,1,0:T(8,128)S(1)} %pad_maximum_fusion), channel_id=1, source_target_pairs={{0,3},{1,0},{2,1},{3,2},{4,15},{5,12},{6,13},{7,14},{8,11},{9,8},{... | collective-permute-start | bytes 122888 | tf_op jit(solution)/shard_map/ppermute | solution.py:352
  19.2 1.3 %collective-permute-start.7 = (f32[14,8,128]{2,1,0:T(8,128)S(1)}, f32[14,8,128]{2,1,0:T(8,128)S(1)}, u32[]{:S(2)}, u32[]{:S(2)}) collective-permute-start(f32[14,8,128]{2,1,0:T(8,128)S(1)} %constant_dynamic-update-slice_fusion.refs_2_), channel_id=1, source_target_pairs={{0,4},{4,0},{8,12},{12,8},{1,5},{5,1},{9,13},{13,9},{2,6},{6,2},{1... | collective-permute-start | bytes 172040 | tf_op jit(solution)/shard_map/ppermute | solution.py:373

commit v9 on v8

--- a/solution.py
+++ b/solution.py
@@ -7,7 +7,7 @@
 
 NZ, ROWS, LANES = 64, 8, 128
 FLAT = NZ * ROWS
-CHUNK = 8
+CHUNK = 16
 EDGE = 3 * NZ + ROWS
 BITS = ((0, 1), (0, 2), (1, 1), (1, 2))
 

time: 21.5 us -> 21.6 us (level)
  waiting for transfers between devices: 2.24 us -> 3.35 us
  Pallas kernels: 6.68 us -> 5.57 us
    ppermute x3, waiting for transfers between devices: 1.34 us -> 2.38 us  [send(): return lax.ppermute(value, ('space', 'tm'), pairs)]
    pallas_call x1, Pallas kernels: 1.41 us -> 0.85 us  [local(): pl.pallas_call(two_steps, in_specs=[vmem] * 2, out_specs=vmem, out_shape=...]
    pallas_call x1, Pallas kernels: 2.79 us -> 2.23 us  [local(): pl.pallas_call(steps_kernel, in_specs=[vmem, anyspace, anyspace], out_spe...]
  transfers between devices with their start and end apart: 9 -> 9, of which waited for: 4 -> 5; matrix products, arithmetic and copies ran while one was open for 0% -> 0% of each run, Pallas kernels for 21% -> 16%
where the time goes in v9:
time: 21.6 us; the launch traced here: 21.4 us
  starting transfers between devices  11.8 us (55%)
  Pallas kernels  5.57 us (26%)
  waiting for transfers between devices  3.35 us (16%)
  between operations  0.69 us (3%)
    ppermute x3, starting transfers between devices, send(): return lax.ppermute(value, ('space', 'tm'), pairs)  5.05 us
    ppermute x1, starting transfers between devices, local(): cross = lax.ppermute(mine_cross, ('groups', 'space'), list(partner.items()))  2.59 us
    ppermute x3, waiting for transfers between devices, send(): return lax.ppermute(value, ('space', 'tm'), pairs)  2.38 us
    pallas_call x1, Pallas kernels, local(): pl.pallas_call(steps_kernel, in_specs=[vmem, anyspace, anyspace], out_spe...  2.23 us
    ppermute x1, starting transfers between devices, local(): added = lax.ppermute(added, 'tm', ring(slices, 1))  1.63 us
    ppermute x1, starting transfers between devices, local(): start_before = lax.ppermute(v, 'tm', ring(slices, 1))  1.58 us
    pallas_call x1, Pallas kernels, local(): pl.pallas_call(edges_kernel, in_specs=[anyspace] * 3, out_specs=[vmem] *...  1.21 us
    pallas_call x1, Pallas kernels, local(): pl.pallas_call(lambda *refs: sweep_kernel(bricks, slices, *refs), in_spec...  0.96 us
  transfers between devices with their start and end apart: 9, of which 5 were waited for; matrix products, arithmetic and copies ran while one was open for 0% of the time, Pallas kernels for 16%

profile of v9, /device:TPU:0, one launch (start us, length us, event | category | flops | bytes accessed | tf_op | source)
XLA Modules:
  0.0 21.4 jit_solution(11904232754801178691)
XLA Ops:
  0.6 1.2 %edges.1 = (f32[512,128]{1,0:T(8,128)S(1)}, f32[200,128]{1,0:T(8,128)S(1)}, f32[200,128]{1,0:T(8,128)S(1)}) custom-call(f32[512,128]{1,0:T(8,128)} %bitcast.7, f32[3,64,8,128]{3,2,1,0:T(8,128)} %vel_hbm.1, f32[64,8,128]{2,1,0:T(8,128)} %d_hbm.1), custom_call_target="tpu_custom_call" | custom-call | tf_op jit(solution)/shard_map/edges/pallas_call | solution.py:288
  1.8 0.5 %collective-permute-start = (f32[200,128]{1,0:T(8,128)S(1)}, f32[200,128]{1,0:T(8,128)S(1)}, u32[]{:S(2)}, u32[]{:S(2)}) collective-permute-start(f32[200,128]{1,0:T(8,128)S(1)} %get-tuple-element.19.refs_1_), channel_id=1, source_target_pairs={{0,4},{4,0},{8,12},{12,8},{1,5},{5,1},{9,13},{13,9},{2,6},{6,2},{1... | collective-permute-start | bytes 307208 | tf_op jit(solution)/shard_map/ppermute | solution.py:313
  2.4 2.6 %collective-permute-start.1 = (f32[200,128]{1,0:T(8,128)S(1)}, f32[200,128]{1,0:T(8,128)S(1)}, u32[]{:S(2)}, u32[]{:S(2)}) collective-permute-start(f32[200,128]{1,0:T(8,128)S(1)} %get-tuple-element.20.refs_2_), channel_id=1, source_target_pairs={{0,16},{4,8},{8,4},{12,28},{16,0},{20,24},{24,20},{28,12},{1,17},{... | collective-permute-start | bytes 307208 | tf_op jit(solution)/shard_map/ppermute | solution.py:311
  5.0 1.6 %collective-permute-start.4 = (f32[512,128]{1,0:T(8,128)S(1)}, f32[512,128]{1,0:T(8,128)S(1)}, u32[]{:S(2)}, u32[]{:S(2)}) collective-permute-start(f32[512,128]{1,0:T(8,128)S(1)} %get-tuple-element.17.v_ref.refs_8_), channel_id=1, source_target_pairs={{0,1},{1,2},{2,3},{3,0},{4,5},{5,6},{6,7},{7,4},{8,9},{9,10},{10,1... | collective-permute-start | bytes 786440 | tf_op jit(solution)/shard_map/ppermute | solution.py:315
  6.5 2.2 %steps.1 = (f32[512,128]{1,0:T(8,128)S(1)}, f32[768,128]{1,0:T(8,128)S(1)}, f32[4,8,128]{2,1,0:T(8,128)S(1)}, f32[2048,128]{1,0:T(8,128)S(1)}) custom-call(f32[512,128]{1,0:T(8,128)S(1)} %get-tuple-element.17.v_ref.refs_8_, f32[1536,128]{1,0:T(8,128)} %bitcast.5, f32[512,128]{1,0:T(8,128)} %bitcast.6), custom_call_target="tpu_custom_call" | custom-call | tf_op jit(solution)/shard_map/steps/pallas_call | solution.py:317
  8.8 0.0 collective-permute-done.refs_3_
  8.8 0.0 collective-permute-done.1.refs_4_
  8.8 0.3 %finish.1 = (f32[512,128]{1,0:T(8,128)S(1)}, f32[5,8,128]{2,1,0:T(8,128)S(1)}, f32[8,128]{1,0:T(8,128)S(1)}, f32[256,128]{1,0:T(8,128)S(1)}) custom-call(f32[512,128]{1,0:T(8,128)S(1)} %get-tuple-element.18.refs_0_, f32[200,128]{1,0:T(8,128)S(1)} %get-tuple-element.19.refs_1_, f32[200,128]{1,0:T(8,128)S(1)} %get-tuple-element.20.refs_2_, ...), custom_call_target="tpu_custom_call" | custom-call | tf_op jit(solution)/shard_map/finish/pallas_call | solution.py:331
  9.1 0.0 collective-permute-start.2
  9.1 1.6 %collective-permute-start.8 = (f32[256,128]{1,0:T(8,128)S(1)}, f32[256,128]{1,0:T(8,128)S(1)}, u32[]{:S(2)}, u32[]{:S(2)}) collective-permute-start(f32[256,128]{1,0:T(8,128)S(1)} %get-tuple-element.29), channel_id=1, source_target_pairs={{0,1},{1,2},{2,3},{3,0},{4,5},{5,6},{6,7},{7,4},{8,9},{9,10},{10,1... | collective-permute-start | bytes 393224 | tf_op jit(solution)/shard_map/ppermute | solution.py:355
  10.8 0.0 collective-permute-done.2.refs_1_
  10.8 1.6 %collective-permute-start.3 = (f32[2,8,128]{2,1,0:T(8,128)S(1)}, f32[2,8,128]{2,1,0:T(8,128)S(1)}, u32[]{:S(2)}, u32[]{:S(2)}) collective-permute-start(f32[2,8,128]{2,1,0:T(8,128)S(1)} %pad_maximum_fusion.1), channel_id=1, source_target_pairs={{0,1},{1,2},{2,3},{3,0},{4,13},{5,14},{6,15},{7,12},{8,9},{9,10},{... | collective-permute-start | bytes 24584 | tf_op jit(solution)/shard_map/ppermute | solution.py:352
  12.4 1.4 %collective-permute-start.5 = (f32[2,8,128]{2,1,0:T(8,128)S(1)}, f32[2,8,128]{2,1,0:T(8,128)S(1)}, u32[]{:S(2)}, u32[]{:S(2)}) collective-permute-start(f32[2,8,128]{2,1,0:T(8,128)S(1)} %pad_maximum_fusion.1), channel_id=1, source_target_pairs={{0,2},{1,3},{2,0},{3,1},{4,14},{5,15},{6,12},{7,13},{8,10},{9,11},... | collective-permute-start | bytes 24584 | tf_op jit(solution)/shard_map/ppermute | solution.py:352
  13.8 2.0 %collective-permute-start.6 = (f32[10,8,128]{2,1,0:T(8,128)S(1)}, f32[10,8,128]{2,1,0:T(8,128)S(1)}, u32[]{:S(2)}, u32[]{:S(2)}) collective-permute-start(f32[10,8,128]{2,1,0:T(8,128)S(1)} %pad_maximum_fusion), channel_id=1, source_target_pairs={{0,3},{1,0},{2,1},{3,2},{4,15},{5,12},{6,13},{7,14},{8,11},{9,8},{... | collective-permute-start | bytes 122888 | tf_op jit(solution)/shard_map/ppermute | solution.py:352
  15.8 0.1 collective-permute-done.4.v_ref
  15.9 0.9 %steps_before.1.refs_6_ = f32[512,128]{1,0:T(8,128)S(1)} custom-call(f32[512,128]{1,0:T(8,128)S(1)} %collective-permute-done.4.v_ref, f32[2048,128]{1,0:T(8,128)S(1)} %get-tuple-element.24.c_ref), custom_call_target="tpu_custom_call" | custom-call | tf_op jit(solution)/shard_map/steps_before/pallas_call | solution.py:356
  16.8 1.5 %collective-permute-done.3 = f32[2,8,128]{2,1,0:T(8,128)S(1)} collective-permute-done((f32[2,8,128]{2,1,0:T(8,128)S(1)}, f32[2,8,128]{2,1,0:T(8,128)S(1)}, u32[]{:S(2)}, u32[]{:S(2)}) %collective-permute-start.3) | collective-permute-done | bytes 8224 | tf_op jit(solution)/shard_map/ppermute | solution.py:352
  18.3 0.2 collective-permute-done.5
  18.5 0.7 %collective-permute-done.6 = f32[10,8,128]{2,1,0:T(8,128)S(1)} collective-permute-done((f32[10,8,128]{2,1,0:T(8,128)S(1)}, f32[10,8,128]{2,1,0:T(8,128)S(1)}, u32[]{:S(2)}, u32[]{:S(2)}) %collective-permute-start.6) | collective-permute-done | bytes 40992 | tf_op jit(solution)/shard_map/ppermute | solution.py:352
  19.2 0.4 %collective-permute-start.7 = (f32[14,8,128]{2,1,0:T(8,128)S(1)}, f32[14,8,128]{2,1,0:T(8,128)S(1)}, u32[]{:S(2)}, u32[]{:S(2)}) collective-permute-start(f32[14,8,128]{2,1,0:T(8,128)S(1)} %constant_dynamic-update-slice_fusion.refs_2_), channel_id=1, source_target_pairs={{0,4},{4,0},{8,12},{12,8},{1,5},{5,1},{9,13},{13,9},{2,6},{6,2},{1... | collective-permute-start | bytes 172040 | tf_op jit(solution)/shard_map/ppermute | solution.py:373
  19.5 0.0 collective-permute-done.8.refs_7_
  19.6 0.9 %collective-permute-done.7.refs_3_ = f32[14,8,128]{2,1,0:T(8,128)S(1)} collective-permute-done((f32[14,8,128]{2,1,0:T(8,128)S(1)}, f32[14,8,128]{2,1,0:T(8,128)S(1)}, u32[]{:S(2)}, u32[]{:S(2)}) %collective-permute-start.7) | collective-permute-done | bytes 57376 | tf_op jit(solution)/shard_map/ppermute | solution.py:373
  20.4 1.0 %sweep.1 = (f32[512,128]{1,0:T(8,128)}, f32[512,128]{1,0:T(8,128)}) custom-call(f32[5,8,128]{2,1,0:T(8,128)S(1)} %get-tuple-element.23.refs_0_, f32[5,8,128]{2,1,0:T(8,128)S(1)} %collective-permute-done.2.refs_1_, f32[14,8,128]{2,1,0:T(8,128)S(1)} %constant_dynamic-update-slice_fusion.refs_2_, f32[14,8,128]{2,1,0:T(8,128)S(1)} %collective-permute-done.7.refs_3_, ...), custom_call_target="tpu_custom_call" | custom-call | tf_op jit(solution)/shard_map/sweep/pallas_call | solution.py:375
  (7 shorter events, 0.0 us)
Async XLA Ops:
  1.8 6.9 %collective-permute-start = (f32[200,128]{1,0:T(8,128)S(1)}, f32[200,128]{1,0:T(8,128)S(1)}, u32[]{:S(2)}, u32[]{:S(2)}) collective-permute-start(f32[200,128]{1,0:T(8,128)S(1)} %get-tuple-element.19.refs_1_), channel_id=1, source_target_pairs={{0,4},{4,0},{8,12},{12,8},{1,5},{5,1},{9,13},{13,9},{2,6},{6,2},{1... | collective-permute-start | bytes 307208 | tf_op jit(solution)/shard_map/ppermute | solution.py:313
  2.4 6.4 %collective-permute-start.1 = (f32[200,128]{1,0:T(8,128)S(1)}, f32[200,128]{1,0:T(8,128)S(1)}, u32[]{:S(2)}, u32[]{:S(2)}) collective-permute-start(f32[200,128]{1,0:T(8,128)S(1)} %get-tuple-element.20.refs_2_), channel_id=1, source_target_pairs={{0,16},{4,8},{8,4},{12,28},{16,0},{20,24},{24,20},{28,12},{1,17},{... | collective-permute-start | bytes 307208 | tf_op jit(solution)/shard_map/ppermute | solution.py:311
  5.0 10.9 %collective-permute-start.4 = (f32[512,128]{1,0:T(8,128)S(1)}, f32[512,128]{1,0:T(8,128)S(1)}, u32[]{:S(2)}, u32[]{:S(2)}) collective-permute-start(f32[512,128]{1,0:T(8,128)S(1)} %get-tuple-element.17.v_ref.refs_8_), channel_id=1, source_target_pairs={{0,1},{1,2},{2,3},{3,0},{4,5},{5,6},{6,7},{7,4},{8,9},{9,10},{10,1... | collective-permute-start | bytes 786440 | tf_op jit(solution)/shard_map/ppermute | solution.py:315
  9.1 1.7 %collective-permute-start.2 = (f32[5,8,128]{2,1,0:T(8,128)S(1)}, f32[5,8,128]{2,1,0:T(8,128)S(1)}, u32[]{:S(2)}, u32[]{:S(2)}) collective-permute-start(f32[5,8,128]{2,1,0:T(8,128)S(1)} %get-tuple-element.23.refs_0_), channel_id=1, source_target_pairs={{0,4},{4,0},{8,12},{12,8},{1,5},{5,1},{9,13},{13,9},{2,6},{6,2},{1... | collective-permute-start | bytes 61448 | tf_op jit(solution)/shard_map/ppermute | solution.py:354
  9.1 10.4 %collective-permute-start.8 = (f32[256,128]{1,0:T(8,128)S(1)}, f32[256,128]{1,0:T(8,128)S(1)}, u32[]{:S(2)}, u32[]{:S(2)}) collective-permute-start(f32[256,128]{1,0:T(8,128)S(1)} %get-tuple-element.29), channel_id=1, source_target_pairs={{0,1},{1,2},{2,3},{3,0},{4,5},{5,6},{6,7},{7,4},{8,9},{9,10},{10,1... | collective-permute-start | bytes 393224 | tf_op jit(solution)/shard_map/ppermute | solution.py:355
  10.8 7.5 %collective-permute-start.3 = (f32[2,8,128]{2,1,0:T(8,128)S(1)}, f32[2,8,128]{2,1,0:T(8,128)S(1)}, u32[]{:S(2)}, u32[]{:S(2)}) collective-permute-start(f32[2,8,128]{2,1,0:T(8,128)S(1)} %pad_maximum_fusion.1), channel_id=1, source_target_pairs={{0,1},{1,2},{2,3},{3,0},{4,13},{5,14},{6,15},{7,12},{8,9},{9,10},{... | collective-permute-start | bytes 24584 | tf_op jit(solution)/shard_map/ppermute | solution.py:352
  12.4 6.1 %collective-permute-start.5 = (f32[2,8,128]{2,1,0:T(8,128)S(1)}, f32[2,8,128]{2,1,0:T(8,128)S(1)}, u32[]{:S(2)}, u32[]{:S(2)}) collective-permute-start(f32[2,8,128]{2,1,0:T(8,128)S(1)} %pad_maximum_fusion.1), channel_id=1, source_target_pairs={{0,2},{1,3},{2,0},{3,1},{4,14},{5,15},{6,12},{7,13},{8,10},{9,11},... | collective-permute-start | bytes 24584 | tf_op jit(solution)/shard_map/ppermute | solution.py:352
  13.8 5.4 %collective-permute-start.6 = (f32[10,8,128]{2,1,0:T(8,128)S(1)}, f32[10,8,128]{2,1,0:T(8,128)S(1)}, u32[]{:S(2)}, u32[]{:S(2)}) collective-permute-start(f32[10,8,128]{2,1,0:T(8,128)S(1)} %pad_maximum_fusion), channel_id=1, source_target_pairs={{0,3},{1,0},{2,1},{3,2},{4,15},{5,12},{6,13},{7,14},{8,11},{9,8},{... | collective-permute-start | bytes 122888 | tf_op jit(solution)/shard_map/ppermute | solution.py:352
  19.2 1.3 %collective-permute-start.7 = (f32[14,8,128]{2,1,0:T(8,128)S(1)}, f32[14,8,128]{2,1,0:T(8,128)S(1)}, u32[]{:S(2)}, u32[]{:S(2)}) collective-permute-start(f32[14,8,128]{2,1,0:T(8,128)S(1)} %constant_dynamic-update-slice_fusion.refs_2_), channel_id=1, source_target_pairs={{0,4},{4,0},{8,12},{12,8},{1,5},{5,1},{9,13},{13,9},{2,6},{6,2},{1... | collective-permute-start | bytes 172040 | tf_op jit(solution)/shard_map/ppermute | solution.py:373

commit v10 on v9

--- a/solution.py
+++ b/solution.py
@@ -7,7 +7,7 @@
 
 NZ, ROWS, LANES = 64, 8, 128
 FLAT = NZ * ROWS
-CHUNK = 16
+CHUNK = 32
 EDGE = 3 * NZ + ROWS
 BITS = ((0, 1), (0, 2), (1, 1), (1, 2))
 

time: 21.6 us -> 21.6 us (level)
  Pallas kernels: 5.57 us -> 5.19 us
  waiting for transfers between devices: 3.35 us -> 3.67 us
  transfers between devices with their start and end apart: 9 -> 9, of which waited for: 5 -> 5; matrix products, arithmetic and copies ran while one was open for 0% -> 0% of each run, Pallas kernels for 16% -> 14%
where the time goes in v10:
time: 21.6 us; the launch traced here: 21.4 us
  starting transfers between devices  11.8 us (55%)
  Pallas kernels  5.19 us (24%)
  waiting for transfers between devices  3.67 us (17%)
  between operations  0.7 us (3%)
    ppermute x3, starting transfers between devices, send(): return lax.ppermute(value, ('space', 'tm'), pairs)  5.1 us
    ppermute x1, starting transfers between devices, local(): cross = lax.ppermute(mine_cross, ('groups', 'space'), list(partner.items()))  2.59 us
    ppermute x3, waiting for transfers between devices, send(): return lax.ppermute(value, ('space', 'tm'), pairs)  2.59 us
    pallas_call x1, Pallas kernels, local(): pl.pallas_call(steps_kernel, in_specs=[vmem, anyspace, anyspace], out_spe...  2.06 us
    ppermute x1, starting transfers between devices, local(): added = lax.ppermute(added, 'tm', ring(slices, 1))  1.63 us
    ppermute x1, starting transfers between devices, local(): start_before = lax.ppermute(v, 'tm', ring(slices, 1))  1.58 us
    pallas_call x1, Pallas kernels, local(): pl.pallas_call(edges_kernel, in_specs=[anyspace] * 3, out_specs=[vmem] *...  1.21 us
    pallas_call x1, Pallas kernels, local(): pl.pallas_call(lambda *refs: sweep_kernel(bricks, slices, *refs), in_spec...  0.96 us
  transfers between devices with their start and end apart: 9, of which 5 were waited for; matrix products, arithmetic and copies ran while one was open for 0% of the time, Pallas kernels for 14%

profile of v10, /device:TPU:0, one launch (start us, length us, event | category | flops | bytes accessed | tf_op | source)
XLA Modules:
  0.0 21.4 jit_solution(2258476214722731450)
XLA Ops:
  0.6 1.2 %edges.1 = (f32[512,128]{1,0:T(8,128)S(1)}, f32[200,128]{1,0:T(8,128)S(1)}, f32[200,128]{1,0:T(8,128)S(1)}) custom-call(f32[512,128]{1,0:T(8,128)} %bitcast.7, f32[3,64,8,128]{3,2,1,0:T(8,128)} %vel_hbm.1, f32[64,8,128]{2,1,0:T(8,128)} %d_hbm.1), custom_call_target="tpu_custom_call" | custom-call | tf_op jit(solution)/shard_map/edges/pallas_call | solution.py:288
  1.8 0.5 %collective-permute-start = (f32[200,128]{1,0:T(8,128)S(1)}, f32[200,128]{1,0:T(8,128)S(1)}, u32[]{:S(2)}, u32[]{:S(2)}) collective-permute-start(f32[200,128]{1,0:T(8,128)S(1)} %get-tuple-element.19.refs_1_), channel_id=1, source_target_pairs={{0,4},{4,0},{8,12},{12,8},{1,5},{5,1},{9,13},{13,9},{2,6},{6,2},{1... | collective-permute-start | bytes 307208 | tf_op jit(solution)/shard_map/ppermute | solution.py:313
  2.4 2.6 %collective-permute-start.1 = (f32[200,128]{1,0:T(8,128)S(1)}, f32[200,128]{1,0:T(8,128)S(1)}, u32[]{:S(2)}, u32[]{:S(2)}) collective-permute-start(f32[200,128]{1,0:T(8,128)S(1)} %get-tuple-element.20.refs_2_), channel_id=1, source_target_pairs={{0,16},{4,8},{8,4},{12,28},{16,0},{20,24},{24,20},{28,12},{1,17},{... | collective-permute-start | bytes 307208 | tf_op jit(solution)/shard_map/ppermute | solution.py:311
  5.0 1.6 %collective-permute-start.4 = (f32[512,128]{1,0:T(8,128)S(1)}, f32[512,128]{1,0:T(8,128)S(1)}, u32[]{:S(2)}, u32[]{:S(2)}) collective-permute-start(f32[512,128]{1,0:T(8,128)S(1)} %get-tuple-element.17.v_ref.refs_8_), channel_id=1, source_target_pairs={{0,1},{1,2},{2,3},{3,0},{4,5},{5,6},{6,7},{7,4},{8,9},{9,10},{10,1... | collective-permute-start | bytes 786440 | tf_op jit(solution)/shard_map/ppermute | solution.py:315
  6.5 2.1 %steps.1 = (f32[512,128]{1,0:T(8,128)S(1)}, f32[768,128]{1,0:T(8,128)S(1)}, f32[4,8,128]{2,1,0:T(8,128)S(1)}, f32[2048,128]{1,0:T(8,128)S(1)}) custom-call(f32[512,128]{1,0:T(8,128)S(1)} %get-tuple-element.17.v_ref.refs_8_, f32[1536,128]{1,0:T(8,128)} %bitcast.5, f32[512,128]{1,0:T(8,128)} %bitcast.6), custom_call_target="tpu_custom_call" | custom-call | tf_op jit(solution)/shard_map/steps/pallas_call | solution.py:317
  8.6 0.0 collective-permute-done.refs_3_
  8.6 0.0 collective-permute-done.1.refs_4_
  8.6 0.3 %finish.1 = (f32[512,128]{1,0:T(8,128)S(1)}, f32[5,8,128]{2,1,0:T(8,128)S(1)}, f32[8,128]{1,0:T(8,128)S(1)}, f32[256,128]{1,0:T(8,128)S(1)}) custom-call(f32[512,128]{1,0:T(8,128)S(1)} %get-tuple-element.18.refs_0_, f32[200,128]{1,0:T(8,128)S(1)} %get-tuple-element.19.refs_1_, f32[200,128]{1,0:T(8,128)S(1)} %get-tuple-element.20.refs_2_, ...), custom_call_target="tpu_custom_call" | custom-call | tf_op jit(solution)/shard_map/finish/pallas_call | solution.py:331
  8.9 0.0 collective-permute-start.2
  9.0 1.6 %collective-permute-start.8 = (f32[256,128]{1,0:T(8,128)S(1)}, f32[256,128]{1,0:T(8,128)S(1)}, u32[]{:S(2)}, u32[]{:S(2)}) collective-permute-start(f32[256,128]{1,0:T(8,128)S(1)} %get-tuple-element.29), channel_id=1, source_target_pairs={{0,1},{1,2},{2,3},{3,0},{4,5},{5,6},{6,7},{7,4},{8,9},{9,10},{10,1... | collective-permute-start | bytes 393224 | tf_op jit(solution)/shard_map/ppermute | solution.py:355
  10.6 0.0 collective-permute-done.2.refs_1_
  10.6 1.6 %collective-permute-start.3 = (f32[2,8,128]{2,1,0:T(8,128)S(1)}, f32[2,8,128]{2,1,0:T(8,128)S(1)}, u32[]{:S(2)}, u32[]{:S(2)}) collective-permute-start(f32[2,8,128]{2,1,0:T(8,128)S(1)} %pad_maximum_fusion.1), channel_id=1, source_target_pairs={{0,1},{1,2},{2,3},{3,0},{4,13},{5,14},{6,15},{7,12},{8,9},{9,10},{... | collective-permute-start | bytes 24584 | tf_op jit(solution)/shard_map/ppermute | solution.py:352
  12.2 1.5 %collective-permute-start.5 = (f32[2,8,128]{2,1,0:T(8,128)S(1)}, f32[2,8,128]{2,1,0:T(8,128)S(1)}, u32[]{:S(2)}, u32[]{:S(2)}) collective-permute-start(f32[2,8,128]{2,1,0:T(8,128)S(1)} %pad_maximum_fusion.1), channel_id=1, source_target_pairs={{0,2},{1,3},{2,0},{3,1},{4,14},{5,15},{6,12},{7,13},{8,10},{9,11},... | collective-permute-start | bytes 24584 | tf_op jit(solution)/shard_map/ppermute | solution.py:352
  13.8 1.9 %collective-permute-start.6 = (f32[10,8,128]{2,1,0:T(8,128)S(1)}, f32[10,8,128]{2,1,0:T(8,128)S(1)}, u32[]{:S(2)}, u32[]{:S(2)}) collective-permute-start(f32[10,8,128]{2,1,0:T(8,128)S(1)} %pad_maximum_fusion), channel_id=1, source_target_pairs={{0,3},{1,0},{2,1},{3,2},{4,15},{5,12},{6,13},{7,14},{8,11},{9,8},{... | collective-permute-start | bytes 122888 | tf_op jit(solution)/shard_map/ppermute | solution.py:352
  15.7 0.2 collective-permute-done.4.v_ref
  15.9 0.6 %steps_before.1.refs_6_ = f32[512,128]{1,0:T(8,128)S(1)} custom-call(f32[512,128]{1,0:T(8,128)S(1)} %collective-permute-done.4.v_ref, f32[2048,128]{1,0:T(8,128)S(1)} %get-tuple-element.24.c_ref), custom_call_target="tpu_custom_call" | custom-call | tf_op jit(solution)/shard_map/steps_before/pallas_call | solution.py:356
  16.6 1.7 %collective-permute-done.3 = f32[2,8,128]{2,1,0:T(8,128)S(1)} collective-permute-done((f32[2,8,128]{2,1,0:T(8,128)S(1)}, f32[2,8,128]{2,1,0:T(8,128)S(1)}, u32[]{:S(2)}, u32[]{:S(2)}) %collective-permute-start.3) | collective-permute-done | bytes 8224 | tf_op jit(solution)/shard_map/ppermute | solution.py:352
  18.3 0.2 collective-permute-done.5
  18.5 0.7 %collective-permute-done.6 = f32[10,8,128]{2,1,0:T(8,128)S(1)} collective-permute-done((f32[10,8,128]{2,1,0:T(8,128)S(1)}, f32[10,8,128]{2,1,0:T(8,128)S(1)}, u32[]{:S(2)}, u32[]{:S(2)}) %collective-permute-start.6) | collective-permute-done | bytes 40992 | tf_op jit(solution)/shard_map/ppermute | solution.py:352
  19.2 0.4 %collective-permute-start.7 = (f32[14,8,128]{2,1,0:T(8,128)S(1)}, f32[14,8,128]{2,1,0:T(8,128)S(1)}, u32[]{:S(2)}, u32[]{:S(2)}) collective-permute-start(f32[14,8,128]{2,1,0:T(8,128)S(1)} %constant_dynamic-update-slice_fusion.refs_2_), channel_id=1, source_target_pairs={{0,4},{4,0},{8,12},{12,8},{1,5},{5,1},{9,13},{13,9},{2,6},{6,2},{1... | collective-permute-start | bytes 172040 | tf_op jit(solution)/shard_map/ppermute | solution.py:373
  19.6 0.0 collective-permute-done.8.refs_7_
  19.6 0.9 %collective-permute-done.7.refs_3_ = f32[14,8,128]{2,1,0:T(8,128)S(1)} collective-permute-done((f32[14,8,128]{2,1,0:T(8,128)S(1)}, f32[14,8,128]{2,1,0:T(8,128)S(1)}, u32[]{:S(2)}, u32[]{:S(2)}) %collective-permute-start.7) | collective-permute-done | bytes 57376 | tf_op jit(solution)/shard_map/ppermute | solution.py:373
  20.5 1.0 %sweep.1 = (f32[512,128]{1,0:T(8,128)}, f32[512,128]{1,0:T(8,128)}) custom-call(f32[5,8,128]{2,1,0:T(8,128)S(1)} %get-tuple-element.23.refs_0_, f32[5,8,128]{2,1,0:T(8,128)S(1)} %collective-permute-done.2.refs_1_, f32[14,8,128]{2,1,0:T(8,128)S(1)} %constant_dynamic-update-slice_fusion.refs_2_, f32[14,8,128]{2,1,0:T(8,128)S(1)} %collective-permute-done.7.refs_3_, ...), custom_call_target="tpu_custom_call" | custom-call | tf_op jit(solution)/shard_map/sweep/pallas_call | solution.py:375
  (7 shorter events, 0.0 us)
Async XLA Ops:
  1.8 6.8 %collective-permute-start = (f32[200,128]{1,0:T(8,128)S(1)}, f32[200,128]{1,0:T(8,128)S(1)}, u32[]{:S(2)}, u32[]{:S(2)}) collective-permute-start(f32[200,128]{1,0:T(8,128)S(1)} %get-tuple-element.19.refs_1_), channel_id=1, source_target_pairs={{0,4},{4,0},{8,12},{12,8},{1,5},{5,1},{9,13},{13,9},{2,6},{6,2},{1... | collective-permute-start | bytes 307208 | tf_op jit(solution)/shard_map/ppermute | solution.py:313
  2.4 6.3 %collective-permute-start.1 = (f32[200,128]{1,0:T(8,128)S(1)}, f32[200,128]{1,0:T(8,128)S(1)}, u32[]{:S(2)}, u32[]{:S(2)}) collective-permute-start(f32[200,128]{1,0:T(8,128)S(1)} %get-tuple-element.20.refs_2_), channel_id=1, source_target_pairs={{0,16},{4,8},{8,4},{12,28},{16,0},{20,24},{24,20},{28,12},{1,17},{... | collective-permute-start | bytes 307208 | tf_op jit(solution)/shard_map/ppermute | solution.py:311
  5.0 10.9 %collective-permute-start.4 = (f32[512,128]{1,0:T(8,128)S(1)}, f32[512,128]{1,0:T(8,128)S(1)}, u32[]{:S(2)}, u32[]{:S(2)}) collective-permute-start(f32[512,128]{1,0:T(8,128)S(1)} %get-tuple-element.17.v_ref.refs_8_), channel_id=1, source_target_pairs={{0,1},{1,2},{2,3},{3,0},{4,5},{5,6},{6,7},{7,4},{8,9},{9,10},{10,1... | collective-permute-start | bytes 786440 | tf_op jit(solution)/shard_map/ppermute | solution.py:315
  8.9 1.7 %collective-permute-start.2 = (f32[5,8,128]{2,1,0:T(8,128)S(1)}, f32[5,8,128]{2,1,0:T(8,128)S(1)}, u32[]{:S(2)}, u32[]{:S(2)}) collective-permute-start(f32[5,8,128]{2,1,0:T(8,128)S(1)} %get-tuple-element.23.refs_0_), channel_id=1, source_target_pairs={{0,4},{4,0},{8,12},{12,8},{1,5},{5,1},{9,13},{13,9},{2,6},{6,2},{1... | collective-permute-start | bytes 61448 | tf_op jit(solution)/shard_map/ppermute | solution.py:354
  9.0 10.6 %collective-permute-start.8 = (f32[256,128]{1,0:T(8,128)S(1)}, f32[256,128]{1,0:T(8,128)S(1)}, u32[]{:S(2)}, u32[]{:S(2)}) collective-permute-start(f32[256,128]{1,0:T(8,128)S(1)} %get-tuple-element.29), channel_id=1, source_target_pairs={{0,1},{1,2},{2,3},{3,0},{4,5},{5,6},{6,7},{7,4},{8,9},{9,10},{10,1... | collective-permute-start | bytes 393224 | tf_op jit(solution)/shard_map/ppermute | solution.py:355
  10.6 7.7 %collective-permute-start.3 = (f32[2,8,128]{2,1,0:T(8,128)S(1)}, f32[2,8,128]{2,1,0:T(8,128)S(1)}, u32[]{:S(2)}, u32[]{:S(2)}) collective-permute-start(f32[2,8,128]{2,1,0:T(8,128)S(1)} %pad_maximum_fusion.1), channel_id=1, source_target_pairs={{0,1},{1,2},{2,3},{3,0},{4,13},{5,14},{6,15},{7,12},{8,9},{9,10},{... | collective-permute-start | bytes 24584 | tf_op jit(solution)/shard_map/ppermute | solution.py:352
  12.2 6.2 %collective-permute-start.5 = (f32[2,8,128]{2,1,0:T(8,128)S(1)}, f32[2,8,128]{2,1,0:T(8,128)S(1)}, u32[]{:S(2)}, u32[]{:S(2)}) collective-permute-start(f32[2,8,128]{2,1,0:T(8,128)S(1)} %pad_maximum_fusion.1), channel_id=1, source_target_pairs={{0,2},{1,3},{2,0},{3,1},{4,14},{5,15},{6,12},{7,13},{8,10},{9,11},... | collective-permute-start | bytes 24584 | tf_op jit(solution)/shard_map/ppermute | solution.py:352
  13.8 5.4 %collective-permute-start.6 = (f32[10,8,128]{2,1,0:T(8,128)S(1)}, f32[10,8,128]{2,1,0:T(8,128)S(1)}, u32[]{:S(2)}, u32[]{:S(2)}) collective-permute-start(f32[10,8,128]{2,1,0:T(8,128)S(1)} %pad_maximum_fusion), channel_id=1, source_target_pairs={{0,3},{1,0},{2,1},{3,2},{4,15},{5,12},{6,13},{7,14},{8,11},{9,8},{... | collective-permute-start | bytes 122888 | tf_op jit(solution)/shard_map/ppermute | solution.py:352
  19.2 1.3 %collective-permute-start.7 = (f32[14,8,128]{2,1,0:T(8,128)S(1)}, f32[14,8,128]{2,1,0:T(8,128)S(1)}, u32[]{:S(2)}, u32[]{:S(2)}) collective-permute-start(f32[14,8,128]{2,1,0:T(8,128)S(1)} %constant_dynamic-update-slice_fusion.refs_2_), channel_id=1, source_target_pairs={{0,4},{4,0},{8,12},{12,8},{1,5},{5,1},{9,13},{13,9},{2,6},{6,2},{1... | collective-permute-start | bytes 172040 | tf_op jit(solution)/shard_map/ppermute | solution.py:373
